TPU v7x, 32 devices: a whole 2x2x4 slice. The times are simulated.
32 devices in a mesh: rep: 2 (over y), samp: 1, var: 16 (over z, x, core).
Axes of the slice: x: 2, y: 2, z: 4, core: 2. Of those that a mesh axis runs over, the one named last changes fastest.
Arguments:
- genotypes: bfloat16 [8192, 16384], P('samp', 'var'), may hold values from 0 to 2, as said below
- means: float32 [16384], P('var'), may hold values from 0.1 to 1
- scales: float32 [16384], P('var'), may hold values from 0.3 to 1
- causal: int32 [64, 1000], P('rep'), parts along dimension 0, may hold values from 0 to 16383
- effects: float32 [64, 1000], P('rep'), parts along dimension 0, may hold values from -0.19 to 0.19
- heritability: float32 [64], P('rep'), parts along dimension 0, may hold values from 0.1 to 0.9
- noise: bfloat16 [64, 8192], P('rep', 'samp'), parts along dimension 0, may hold values from -6 to 6
Outputs:
- phenotypes: bfloat16 [64, 8192], P('rep', ('samp', 'var')), parts along dimension 0
- scores: float32 [64, 16384], P('rep', ('var', 'samp')), parts along dimension 0
There are 2 independent parts, one for each index of `rep`. A program takes and returns all parts, laid end to end along the dimension named above; an argument that names none is the same for every part. Nothing has to cross between parts.
Inputs may be any that keep to these rules, and one draw needn't show every extreme that they name: `genotypes`: dosages are 0, 1 or 2. `causal`: an index may repeat within a phenotype; its effects then add.
All inputs are finite; a program needn't handle non-finite values.
Results may differ from a plain program's by a relative error of at most 0.017.
Values may be sent and summed in bfloat16 or wider, within the bound.
No kernel may reach another device: no remote copies, remote signals or barrier semaphores. Data moves between devices by JAX's collectives and lax.ppermute only.
A program may use at most 64 MiB of HBM per device.

v0:
```python
import jax
import jax.numpy as jnp
from jax import lax
from jax.sharding import PartitionSpec as P


def build_effects(local, effects, variant_dev):
    pheno_count = local.shape[0]
    causal_count = local.shape[1]
    block_size = 128
    block_count = (causal_count + block_size - 1) // block_size
    padded_count = block_count * block_size
    extra = padded_count - causal_count
    local_pad = jnp.concatenate(
        [local, jnp.full((pheno_count, extra), variant_dev, jnp.int32)], axis=1
    )
    effect_pad = jnp.concatenate([effects, jnp.zeros((pheno_count, extra), jnp.float32)], axis=1)
    columns = lax.broadcasted_iota(jnp.int32, (1, 1, variant_dev), 2)

    def add_block(index, total):
        start = (index * block_size).astype(jnp.int32)
        where_block = lax.dynamic_slice_in_dim(local_pad, start, block_size, 1)
        value_block = lax.dynamic_slice_in_dim(effect_pad, start, block_size, 1)
        hits = where_block[:, :, None] == columns
        return total + jnp.sum(jnp.where(hits, value_block[:, :, None], jnp.float32(0.0)), axis=1)

    initial = jnp.zeros((pheno_count, variant_dev), jnp.float32)
    return lax.fori_loop(0, block_count, add_block, initial)


def on_device(genotypes, means, scales, causal, effects, heritability, noise):
    sample_dev = genotypes.shape[0]
    variant_dev = genotypes.shape[1]
    first = lax.axis_index("var") * variant_dev
    local = causal - first
    inside = (local >= 0) & (local < variant_dev)
    local = jnp.where(inside, local, variant_dev)
    beta = build_effects(local, effects, variant_dev)
    weights = (beta / scales[None, :]).astype(jnp.bfloat16)
    offset = jnp.sum(weights.astype(jnp.float32) * means[None, :], axis=1)
    partial_sum = (
        lax.dot_general(
            weights, genotypes, (((1,), (1,)), ((), ())), preferred_element_type=jnp.float32
        )
        - offset[:, None]
    )
    heavy = jnp.sqrt(heritability)[:, None]
    light = jnp.sqrt(1.0 - heritability)[:, None]
    share = sample_dev // lax.axis_size("var")
    share_start = lax.axis_index("var") * share
    genetic_part = lax.psum_scatter(
        partial_sum.astype(jnp.bfloat16), "var", scatter_dimension=1, tiled=True
    ).astype(jnp.float32)
    noise_part = lax.dynamic_slice_in_dim(noise, share_start, share, 1)
    phen_out = (heavy * genetic_part + light * noise_part.astype(jnp.float32)).astype(jnp.bfloat16)
    piece = lax.all_gather(phen_out, "var", axis=1, tiled=True)
    total = jnp.dot(piece, genotypes, preferred_element_type=jnp.float32)
    column = jnp.sum(piece.astype(jnp.float32), axis=1)
    score_width = variant_dev // lax.axis_size("samp")
    score_start = lax.axis_index("samp") * score_width
    means_part = lax.dynamic_slice_in_dim(means, score_start, score_width, 0)
    scales_part = lax.dynamic_slice_in_dim(scales, score_start, score_width, 0)
    total_samples = jnp.float32(sample_dev * lax.axis_size("samp"))
    column_sum = lax.psum(column, "samp")
    correction = column_sum[:, None] * means_part[None, :]
    summed = lax.psum_scatter(total, "samp", scatter_dimension=1, tiled=True)
    centered = summed - correction
    scores = centered / (scales_part[None, :] * jnp.sqrt(total_samples))
    return (phen_out, scores)


def solution(mesh):
    in_specs = (
        P("samp", "var"),
        P("var"),
        P("var"),
        P("rep", None),
        P("rep", None),
        P("rep"),
        P("rep", "samp"),
    )
    out_specs = (P("rep", ("samp", "var")), P("rep", ("var", "samp")))
    return jax.shard_map(
        on_device, mesh=mesh, in_specs=in_specs, out_specs=out_specs, check_vma=False
    )
```

profile of v0, /device:TPU:0, one launch (start us, length us, event | category | flops | bytes accessed | tf_op | source)
XLA Modules:
  0.0 144.4 jit_solution(5938545068469961959)
XLA Ops:
  7.2 0.0 copy-start.2
  7.2 0.0 copy-start.1
  7.2 0.0 copy-start.3
  7.2 0.0 reduce-scatter.2.cloned.1.call-start
  7.3 0.9 and_select_fusion
  8.2 0.9 concatenate.7
  9.1 25.5 %while.14 = (s32[]{:T(128)}, f32[32,1024]{1,0:T(8,128)S(1)}, s32[32,1024]{1,0:T(8,128)S(1)}, f32[32,1024]{1,0:T(8,128)S(1)}, s32[]{:T(128)}, /*index=5*/s32[]{:T(128)}, s32[]{:T(128)}, s32[]{:T(128)}) while((s32[]{:T(128)}, f32[32,1024]{1,0:T(8,128)S(1)}, s32[32,1024]{1,0:T(8,128)S(1)}, f32[32,1024]{1,0:T(8,128)S(1)}, s32[]{:T(128)}, ...), condition=%wide.region_2.3_spmd.clone, body=%wide.region_0.2_spmd.clone.sunk | while | flops 12615687 | bytes 622749 | solution.py:28
  9.2 3.1 %select_reduce_fusion.2 = f32[32,1024]{1,0:T(8,128)S(1)} fusion(f32[32,128]{1,0:T(8,128)S(1)} %constant_dynamic-slice_fusion.4, s32[32,128]{1,0:T(8,128)S(1)} %constant_dynamic-slice_fusion.5), kind=kLoop, calls=%fused_computation.2.clone.1 | loop fusion | flops 12550144 | bytes 163840 | tf_op jit(solution)/shard_map/while/body/eval_jaxpr/reduce_sum | solution.py:25
  12.4 3.1 %select_reduce_fusion.2 = f32[32,1024]{1,0:T(8,128)S(1)} fusion(f32[32,128]{1,0:T(8,128)S(1)} %constant_dynamic-slice_fusion.4, s32[32,128]{1,0:T(8,128)S(1)} %constant_dynamic-slice_fusion.5), kind=kLoop, calls=%fused_computation.2.clone.1 | loop fusion | flops 12550144 | bytes 163840 | tf_op jit(solution)/shard_map/while/body/eval_jaxpr/reduce_sum | solution.py:25
  15.6 3.1 %select_reduce_fusion.2 = f32[32,1024]{1,0:T(8,128)S(1)} fusion(f32[32,128]{1,0:T(8,128)S(1)} %constant_dynamic-slice_fusion.4, s32[32,128]{1,0:T(8,128)S(1)} %constant_dynamic-slice_fusion.5), kind=kLoop, calls=%fused_computation.2.clone.1 | loop fusion | flops 12550144 | bytes 163840 | tf_op jit(solution)/shard_map/while/body/eval_jaxpr/reduce_sum | solution.py:25
  18.8 3.1 %select_reduce_fusion.2 = f32[32,1024]{1,0:T(8,128)S(1)} fusion(f32[32,128]{1,0:T(8,128)S(1)} %constant_dynamic-slice_fusion.4, s32[32,128]{1,0:T(8,128)S(1)} %constant_dynamic-slice_fusion.5), kind=kLoop, calls=%fused_computation.2.clone.1 | loop fusion | flops 12550144 | bytes 163840 | tf_op jit(solution)/shard_map/while/body/eval_jaxpr/reduce_sum | solution.py:25
  21.9 3.1 %select_reduce_fusion.2 = f32[32,1024]{1,0:T(8,128)S(1)} fusion(f32[32,128]{1,0:T(8,128)S(1)} %constant_dynamic-slice_fusion.4, s32[32,128]{1,0:T(8,128)S(1)} %constant_dynamic-slice_fusion.5), kind=kLoop, calls=%fused_computation.2.clone.1 | loop fusion | flops 12550144 | bytes 163840 | tf_op jit(solution)/shard_map/while/body/eval_jaxpr/reduce_sum | solution.py:25
  25.1 3.1 %select_reduce_fusion.2 = f32[32,1024]{1,0:T(8,128)S(1)} fusion(f32[32,128]{1,0:T(8,128)S(1)} %constant_dynamic-slice_fusion.4, s32[32,128]{1,0:T(8,128)S(1)} %constant_dynamic-slice_fusion.5), kind=kLoop, calls=%fused_computation.2.clone.1 | loop fusion | flops 12550144 | bytes 163840 | tf_op jit(solution)/shard_map/while/body/eval_jaxpr/reduce_sum | solution.py:25
  28.3 3.1 %select_reduce_fusion.2 = f32[32,1024]{1,0:T(8,128)S(1)} fusion(f32[32,128]{1,0:T(8,128)S(1)} %constant_dynamic-slice_fusion.4, s32[32,128]{1,0:T(8,128)S(1)} %constant_dynamic-slice_fusion.5), kind=kLoop, calls=%fused_computation.2.clone.1 | loop fusion | flops 12550144 | bytes 163840 | tf_op jit(solution)/shard_map/while/body/eval_jaxpr/reduce_sum | solution.py:25
  31.5 3.1 %select_reduce_fusion.2 = f32[32,1024]{1,0:T(8,128)S(1)} fusion(f32[32,128]{1,0:T(8,128)S(1)} %constant_dynamic-slice_fusion.4, s32[32,128]{1,0:T(8,128)S(1)} %constant_dynamic-slice_fusion.5), kind=kLoop, calls=%fused_computation.2.clone.1 | loop fusion | flops 12550144 | bytes 163840 | tf_op jit(solution)/shard_map/while/body/eval_jaxpr/reduce_sum | solution.py:25
  34.6 0.8 multiply_reduce_fusion
  35.5 11.7 %fusion.2 = bf16[32,8192]{1,0:T(8,128)(2,1)} fusion(bf16[32,1024]{1,0:T(8,128)(2,1)S(1)} %get-tuple-element.123, bf16[8192,1024]{1,0:T(8,128)(2,1)} %param.9, f32[32]{0:T(128)S(1)} %get-tuple-element.122), kind=kOutput, calls=%fused_computation.7 | convolution fusion | flops 537395200 | bytes 17367168 | tf_op jit(solution)/shard_map/dot_general | solution.py:42
  47.2 0.0 reduce-scatter.2.cloned.1.call-update
  47.2 59.0 %reduce-scatter.2.cloned.1.call-done = bf16[32,512]{1,0:T(8,128)(2,1)} async-done(((bf16[32,8192]{1,0:T(8,128)(2,1)}), bf16[32,512]{1,0:T(8,128)(2,1)}) %reduce-scatter.2.cloned.1.call-update) | async-done | bytes 32784 | tf_op jit(solution)/shard_map/reduce_scatter | solution.py:51
  106.2 0.9 add_convert_fusion
  107.1 0.0 copy-start
  107.1 20.8 %all_gather.3 = bf16[32,8192]{1,0:T(8,128)(2,1)S(1)} all-gather(bf16[32,512]{1,0:T(8,128)(2,1)S(1)} %add_convert_fusion), channel_id=1, replica_groups=mesh['rep'=2,'samp'=1,'var'=16] {'var'}, dimensions={1}, use_global_device_ids=true | all-gather | bytes 557056 | tf_op jit(solution)/shard_map/all_gather | solution.py:56
  127.9 0.2 convert_reduce_fusion
  128.1 9.4 %fusion.3 = f32[32,1024]{1,0:T(8,128)} fusion(bf16[32,8192]{1,0:T(8,128)(2,1)S(1)} %all_gather.3, bf16[8192,1024]{1,0:T(8,128)(2,1)} %param.9, f32[1024]{0:T(1024)S(1)} %broadcast_multiply_fusion, f32[32]{0:T(128)S(1)} %convert_reduce_fusion, f32[1024]{0:T(1024)S(1)} %copy-done.1), kind=kOutput, calls=%fused_computation.9 | convolution fusion | flops 536969216 | bytes 17440896 | tf_op jit(solution)/shard_map/dot_general | solution.py:57
  (32 shorter events, 0.5 us)
Async XLA Ops:
  7.2 40.0 %copy-start.2 = (f32[1024]{0:T(1024)S(1)}, f32[1024]{0:T(1024)}, u32[]{:S(2)}) copy-start(f32[1024]{0:T(1024)} %param.11) | copy-start | bytes 12292
  7.2 120.9 %copy-start.1 = (f32[1024]{0:T(1024)S(1)}, f32[1024]{0:T(1024)}, u32[]{:S(2)}) copy-start(f32[1024]{0:T(1024)} %param.10) | copy-start | bytes 12292
  7.2 40.0 %copy-start.3 = (f32[32]{0:T(128)S(1)}, f32[32]{0:T(128)}, u32[]{:S(2)}) copy-start(f32[32]{0:T(128)} %param.14) | copy-start | bytes 388
  7.2 99.0 %reduce-scatter.2.cloned.1.call-start = ((), (), s32[]{:S(2)}) async-start(), calls=%async_computation.1 | async-start | bytes 557056 | tf_op jit(solution)/shard_map/reduce_scatter | solution.py:51
  107.1 30.5 %copy-start = (bf16[32,512]{1,0:T(8,128)(2,1)}, bf16[32,512]{1,0:T(8,128)(2,1)S(1)}, u32[]{:S(2)}) copy-start(bf16[32,512]{1,0:T(8,128)(2,1)S(1)} %add_convert_fusion) | copy-start | bytes 98308
Sparse Core Ops, SparseCore 0:
  47.3 58.8 reduce-scatter.1
where the time goes:
time: 145 us; the launch traced here: 144 us
  waiting for transfers between devices  59 us (41%)
  other arithmetic  27.7 us (19%)
  matrix products  21.1 us (15%)
  blocking collectives  20.8 us (14%)
  between operations  14.1 us (10%)
    reduce_scatter x1, waiting for transfers between devices, on_device(): lax.psum_scatter(partial_sum.astype(jnp.bfloat16), 'var', scatter_dimensi...  59 us
    reduce_sum x8, other arithmetic, add_block(): jnp.sum(jnp.where(hits, value_block[:, :, None], jnp.float32(0.0)), axis=1)  24.6 us
    all_gather x1, blocking collectives, on_device(): piece = lax.all_gather(phen_out, 'var', axis=1, tiled=True)  20.8 us
    dot_general x1, matrix products, on_device(): lax.dot_general(weights, genotypes, (((1,), (1,)), ((), ())), preferred_e...  11.7 us
    dot_general x1, matrix products, on_device(): total = jnp.dot(piece, genotypes, preferred_element_type=jnp.float32)  9.44 us
  transfers between devices with their start and end apart: 1, of which 1 were waited for; matrix products, arithmetic and copies ran while one was open for 0% of the time, Pallas kernels for 0%

commit v1 on v0

v1 whole, which is shorter than its diff:
```python
import jax
import jax.numpy as jnp
from jax import lax
from jax.experimental import pallas as pl
from jax.experimental.pallas import tpu as pltpu
from jax.sharding import PartitionSpec as P

LANES = 128
MIB = 1 << 20


def evolve_kernel(
    blocks,
    share,
    order,
    genotypes_hbm,
    noise_hbm,
    means_hbm,
    scales_hbm,
    causal_hbm,
    effects_hbm,
    heritability_hbm,
    held_ref,
    send_ref,
    keep_ref,
    tail_ref,
    causal_ref,
    effects_ref,
    means_ref,
    scales_ref,
    heritability_ref,
    high_ref,
    low_ref,
    value_ref,
    beta_ref,
    weight_ref,
    noise_ref,
    block_sem,
    noise_sem,
    small_sem,
):
    pheno, variants = weight_ref.shape
    me = lax.axis_index("var")
    tails = tail_ref.shape[0]

    def fetch(r):
        start = pl.multiple_of((me ^ r) * share, share)
        return pltpu.make_async_copy(
            genotypes_hbm.at[pl.ds(start, share), :], held_ref.at[r], block_sem.at[r]
        )

    def fetch_noise(t):
        start = pl.multiple_of((me ^ (t * (blocks // tails))) * share, share)
        return pltpu.make_async_copy(
            noise_hbm.at[:, pl.ds(start, share)], noise_ref.at[t], noise_sem.at[t]
        )

    small = [
        pltpu.make_async_copy(source, target, small_sem.at[i])
        for i, (source, target) in enumerate(
            (
                (causal_hbm, causal_ref),
                (effects_hbm, effects_ref),
                (scales_hbm, scales_ref),
                (means_hbm, means_ref),
                (heritability_hbm, heritability_ref),
            )
        )
    ]
    for copy in small:
        copy.start()
    for t in range(tails):
        fetch_noise(t).start()
    for r in order:
        fetch(r).start()

    causal_count = causal_ref.shape[1]
    high_count = variants // LANES
    high_ref[...] = jnp.full(high_ref.shape, -1, jnp.int32)
    low_ref[...] = jnp.zeros(low_ref.shape, jnp.int32)
    value_ref[...] = jnp.zeros(value_ref.shape, jnp.float32)
    for copy in small:
        copy.wait()
    local = causal_ref[...] - me * variants
    inside = (local >= 0) & (local < variants)
    high_ref[:, :causal_count] = jnp.where(inside, local // LANES, -1)
    low_ref[:, :causal_count] = jnp.where(inside, local % LANES, 0)
    value_ref[:, :causal_count] = effects_ref[...]
    width = high_ref.shape[1]
    high_iota = lax.broadcasted_iota(jnp.int32, (high_count, width), 0)
    low_iota = lax.broadcasted_iota(jnp.int32, (LANES, width), 0)

    def build(p, carry):
        row = pl.ds(p, 1)
        value = jnp.where(high_ref[row, :] == high_iota, value_ref[row, :], 0.0)
        first = value.astype(jnp.bfloat16)
        rest = value - first.astype(jnp.float32)
        second = rest.astype(jnp.bfloat16)
        third = (rest - second.astype(jnp.float32)).astype(jnp.bfloat16)
        hits = jnp.where(low_ref[row, :] == low_iota, 1.0, 0.0).astype(jnp.bfloat16)
        parts = jnp.concatenate([first, second, third], axis=0)
        sums = lax.dot_general(
            parts, hits, (((1,), (1,)), ((), ())), preferred_element_type=jnp.float32
        )
        beta_ref[p] = (
            sums[:high_count] + sums[high_count : 2 * high_count] + sums[2 * high_count :]
        )
        return carry

    lax.fori_loop(0, pheno, build, 0, unroll=2)

    offset = jnp.zeros((pheno, LANES), jnp.float32)
    for h in range(high_count):
        lanes = slice(h * LANES, (h + 1) * LANES)
        weight = (beta_ref[:, h, :] / scales_ref[:, lanes]).astype(jnp.bfloat16)
        weight_ref[:, lanes] = weight
        offset += weight.astype(jnp.float32) * means_ref[:, lanes]
    offset = jnp.sum(offset, axis=1, keepdims=True)

    square = (pheno, pheno)
    diagonal = lax.broadcasted_iota(jnp.int32, square, 0) == lax.broadcasted_iota(
        jnp.int32, square, 1
    )
    share_genetic = jnp.sum(
        jnp.where(diagonal, jnp.broadcast_to(heritability_ref[...], square), 0.0),
        axis=1,
        keepdims=True,
    )
    heavy = jnp.sqrt(share_genetic)
    light = jnp.sqrt(1.0 - share_genetic)
    for t in range(tails):
        fetch_noise(t).wait()
        tail_ref[t] = light * noise_ref[t].astype(jnp.float32)

    weights = weight_ref[...]
    half = blocks // 2
    for i, r in enumerate(order):
        fetch(r).wait()
        part = heavy * (
            lax.dot_general(
                weights,
                held_ref[r],
                (((1,), (1,)), ((), ())),
                preferred_element_type=jnp.float32,
            )
            - offset
        )
        if i < half:
            send_ref[i] = part.astype(send_ref.dtype)
        else:
            keep_ref[i - half] = part.astype(keep_ref.dtype)


def scan_kernel(order, scale_back, *refs):
    held_ref, means_ref, scales_ref = refs[:3]
    pieces = refs[3:-1]
    out_ref = refs[-1]
    total = None
    column = None
    position = 0
    for piece in pieces:
        for j in range(piece.shape[0]):
            values = piece[j]
            part = jnp.dot(values, held_ref[order[position]], preferred_element_type=jnp.float32)
            sums = jnp.sum(values.astype(jnp.float32), axis=1, keepdims=True)
            total = part if total is None else total + part
            column = sums if column is None else column + sums
            position += 1
    if scale_back is None:
        out_ref[...] = total
    else:
        out_ref[...] = (total - column * means_ref[...]) / (scales_ref[...] * scale_back)


def on_device(genotypes, means, scales, causal, effects, heritability, noise):
    samples, variants = genotypes.shape
    pheno, causal_count = causal.shape
    blocks = lax.axis_size("var")
    samp = lax.axis_size("samp")
    share = samples // blocks
    bits = blocks.bit_length() - 1
    if blocks != 1 << bits or bits < 3:
        raise ValueError("var size")
    tails = blocks // 8

    def relative(core, group, tail):
        return core + 2 * group + 8 * tail

    order = [relative(c, g, t) for c in (1, 0) for g in (1, 2, 3, 0) for t in range(tails)]

    def pairs(k):
        return [(i, i ^ k) for i in range(blocks)]

    vmem = pl.BlockSpec(memory_space=pltpu.VMEM)
    hbm = pl.BlockSpec(memory_space=pltpu.HBM)
    means_row = means[None, :]
    scales_row = scales[None, :]
    width = -(-causal_count // LANES) * LANES
    half = blocks // 2

    held, send, keep, tail = pl.pallas_call(
        lambda *refs: evolve_kernel(blocks, share, order, *refs),
        out_shape=(
            jax.ShapeDtypeStruct((blocks, share, variants), genotypes.dtype),
            jax.ShapeDtypeStruct((half, pheno, share), jnp.bfloat16),
            jax.ShapeDtypeStruct((half, pheno, share), jnp.float32),
            jax.ShapeDtypeStruct((tails, pheno, share), jnp.float32),
        ),
        in_specs=[hbm] * 7,
        out_specs=[vmem] * 4,
        scratch_shapes=[
            pltpu.VMEM((pheno, causal_count), jnp.int32),
            pltpu.VMEM((pheno, causal_count), jnp.float32),
            pltpu.VMEM((1, variants), jnp.float32),
            pltpu.VMEM((1, variants), jnp.float32),
            pltpu.VMEM((1, pheno), jnp.float32),
            pltpu.VMEM((pheno, width), jnp.int32),
            pltpu.VMEM((pheno, width), jnp.int32),
            pltpu.VMEM((pheno, width), jnp.float32),
            pltpu.VMEM((pheno, variants // LANES, LANES), jnp.float32),
            pltpu.VMEM((pheno, variants), jnp.bfloat16),
            pltpu.VMEM((tails, pheno, share), jnp.bfloat16),
            pltpu.SemaphoreType.DMA((blocks,)),
            pltpu.SemaphoreType.DMA((tails,)),
            pltpu.SemaphoreType.DMA((5,)),
        ],
        compiler_params=pltpu.CompilerParams(vmem_limit_bytes=8 * MIB),
        name="evolve",
    )(
        *(
            pltpu.with_memory_space_constraint(x, pltpu.HBM)
            for x in (
                genotypes,
                noise,
                means_row,
                scales_row,
                causal,
                effects,
                heritability[None, :],
            )
        )
    )

    got = lax.ppermute(send, "var", pairs(1))
    chip = [
        keep[i * tails : (i + 1) * tails] + got[i * tails : (i + 1) * tails].astype(jnp.float32)
        for i in range(4)
    ]
    arrived = [
        lax.ppermute(chip[g - 1].astype(jnp.bfloat16), "var", pairs(2 * g)) for g in (1, 2, 3)
    ]
    total = chip[3]
    for other in arrived:
        total = total + other.astype(jnp.float32)

    step = 1
    while step < tails:
        mine = total.astype(jnp.bfloat16)
        other = lax.ppermute(mine, "var", pairs(8 * step))
        other = jnp.concatenate([other[t ^ step][None] for t in range(tails)], axis=0)
        total = mine.astype(jnp.float32) + other.astype(jnp.float32)
        step *= 2

    own = (total + tail).astype(jnp.bfloat16)
    phen_out = own[0]

    groups = {0: own}
    for g in (1, 2, 3):
        groups[g] = lax.ppermute(own, "var", pairs(2 * g))
    others = {g: lax.ppermute(groups[g], "var", pairs(1)) for g in range(4)}
    pieces = [groups[g] for g in range(4)] + [others[g] for g in range(4)]
    used = [relative(c, g, t) for c in (0, 1) for g in range(4) for t in range(tails)]

    alone = samp == 1
    total_samples = jnp.float32(samples * samp)
    scale_back = float(samples * samp) ** 0.5 if alone else None
    scores = pl.pallas_call(
        lambda *refs: scan_kernel(used, scale_back, *refs),
        out_shape=jax.ShapeDtypeStruct((pheno, variants), jnp.float32),
        in_specs=[vmem] * (3 + len(pieces)),
        out_specs=vmem,
        compiler_params=pltpu.CompilerParams(vmem_limit_bytes=8 * MIB),
        name="scan",
    )(held, means_row, scales_row, *pieces)
    if alone:
        return phen_out, scores

    column = sum(jnp.sum(piece.astype(jnp.float32), axis=(0, 2)) for piece in pieces)
    score_width = variants // samp
    score_start = lax.axis_index("samp") * score_width
    means_part = lax.dynamic_slice_in_dim(means, score_start, score_width, 0)
    scales_part = lax.dynamic_slice_in_dim(scales, score_start, score_width, 0)
    column_sum = lax.psum(column, "samp")
    correction = column_sum[:, None] * means_part[None, :]
    summed = lax.psum_scatter(scores, "samp", scatter_dimension=1, tiled=True)
    scores = (summed - correction) / (scales_part[None, :] * jnp.sqrt(total_samples))
    return phen_out, scores


def solution(mesh):
    in_specs = (
        P("samp", "var"),
        P("var"),
        P("var"),
        P("rep", None),
        P("rep", None),
        P("rep"),
        P("rep", "samp"),
    )
    out_specs = (P("rep", ("samp", "var")), P("rep", ("var", "samp")))
    return jax.shard_map(
        on_device, mesh=mesh, in_specs=in_specs, out_specs=out_specs, check_vma=False
    )
```

time: 145 us -> 47.1 us (0.32)
  waiting for transfers between devices: 59 us -> 12.9 us
  other arithmetic: 27.7 us -> 0.13 us
  Pallas kernels: 0 us -> 21.2 us
  matrix products: 21.1 us -> 0 us
  blocking collectives: 20.8 us -> 0 us
  between operations: 14.1 us -> 0.68 us
  starting transfers between devices: 0.04 us -> 11.3 us
    reduce_scatter x1 -> x0, waiting for transfers between devices: 59 us -> none  [on_device(): lax.psum_scatter(partial_sum.astype(jnp.bfloat16), 'var', scatter_dimensi...]
    reduce_sum x10 -> x0, other arithmetic: 25.6 us -> none  [the longest x8 24.6 us: add_block(): jnp.sum(jnp.where(hits, value_block[:, :, None], jnp.float32(0.0)), axis=1)]
    pallas_call x0 -> x2, Pallas kernels: none -> 21.2 us  [the longest x1 17.6 us: on_device(): pl.pallas_call(lambda *refs: evolve_kernel(blocks, share, order, *refs),...]
    dot_general x2 -> x0, matrix products: 21.1 us -> none  [the longest x1 11.7 us: on_device(): lax.dot_general(weights, genotypes, (((1,), (1,)), ((), ())), preferred_e...]
    all_gather x1 -> x0, blocking collectives: 20.8 us -> none  [on_device(): piece = lax.all_gather(phen_out, 'var', axis=1, tiled=True)]
    ppermute x0 -> x12, waiting for transfers between devices: none -> 12.9 us  [the longest x3 4.26 us: on_device(): lax.ppermute(chip[g - 1].astype(jnp.bfloat16), 'var', pairs(2 * g))]
    ppermute x0 -> x12, starting transfers between devices: none -> 11.3 us  [the longest x3 4.44 us: on_device(): lax.ppermute(chip[g - 1].astype(jnp.bfloat16), 'var', pairs(2 * g))]
  transfers between devices with their start and end apart: 1 -> 12, of which waited for: 1 -> 9; matrix products, arithmetic and copies ran while one was open for 0% -> 1% of each run, Pallas kernels for 0% -> 0%
where the time goes in v1:
time: 47.1 us; the launch traced here: 46.9 us
  Pallas kernels  21.2 us (45%)
  waiting for transfers between devices  12.9 us (27%)
  starting transfers between devices  11.3 us (24%)
  between operations  0.68 us (1%)
  local copies, waits for them, and re-layouts  0.63 us (1%)
    pallas_call x1, Pallas kernels, on_device(): pl.pallas_call(lambda *refs: evolve_kernel(blocks, share, order, *refs),...  17.6 us
    ppermute x3, starting transfers between devices, on_device(): lax.ppermute(chip[g - 1].astype(jnp.bfloat16), 'var', pairs(2 * g))  4.44 us
    ppermute x3, waiting for transfers between devices, on_device(): lax.ppermute(chip[g - 1].astype(jnp.bfloat16), 'var', pairs(2 * g))  4.26 us
    ppermute x3, waiting for transfers between devices, on_device(): groups[g] = lax.ppermute(own, 'var', pairs(2 * g))  4.25 us
    pallas_call x1, Pallas kernels, on_device(): pl.pallas_call(lambda *refs: scan_kernel(used, scale_back, *refs), out_sh...  3.67 us
    ppermute x3, starting transfers between devices, on_device(): groups[g] = lax.ppermute(own, 'var', pairs(2 * g))  3.66 us
    ppermute x1, starting transfers between devices, on_device(): other = lax.ppermute(mine, 'var', pairs(8 * step))  2.66 us
    ppermute x1, waiting for transfers between devices, on_device(): other = lax.ppermute(mine, 'var', pairs(8 * step))  2.58 us
  transfers between devices with their start and end apart: 12, of which 9 were waited for; matrix products, arithmetic and copies ran while one was open for 1% of the time, Pallas kernels for 0%

profile of v1, /device:TPU:0, one launch (start us, length us, event | category | flops | bytes accessed | tf_op | source)
XLA Modules:
  0.0 46.9 jit_solution(16355813401718660621)
XLA Ops:
  0.7 17.6 %evolve.1 = (bf16[16,512,1024]{2,1,0:T(8,128)(2,1)S(1)}, bf16[8,32,512]{2,1,0:T(8,128)(2,1)S(1)}, f32[8,32,512]{2,1,0:T(8,128)S(1)}, f32[2,32,512]{2,1,0:T(8,128)S(1)}) custom-call(bf16[8192,1024]{1,0:T(8,128)(2,1)} %refs_0_.1, bf16[32,8192]{1,0:T(8,128)(2,1)} %refs_1_.1, f32[1,1024]{1,0:T(1,128)} %bitcast.5, f32[1,1024]{1,0:T(1,128)} %bitcast.7, ...), custom_call_target="tpu_custom_call" | custom-call | tf_op jit(solution)/shard_map/evolve/pallas_call | solution.py:201
  18.2 0.6 %collective-permute-start = (bf16[8,32,512]{2,1,0:T(8,128)(2,1)S(1)}, bf16[8,32,512]{2,1,0:T(8,128)(2,1)S(1)}, u32[]{:S(2)}, u32[]{:S(2)}) collective-permute-start(bf16[8,32,512]{2,1,0:T(8,128)(2,1)S(1)} %get-tuple-element.7), channel_id=1, source_target_pairs={{0,1},{1,0},{2,3},{3,2},{4,5},{5,4},{6,7},{7,6},{8,9},{9,8},{10,11... | collective-permute-start | bytes 786440 | tf_op jit(solution)/shard_map/ppermute | solution.py:244
  18.8 1.2 %collective-permute-done = bf16[8,32,512]{2,1,0:T(8,128)(2,1)S(1)} collective-permute-done((bf16[8,32,512]{2,1,0:T(8,128)(2,1)S(1)}, bf16[8,32,512]{2,1,0:T(8,128)(2,1)S(1)}, u32[]{:S(2)}, u32[]{:S(2)}) %collective-permute-start) | collective-permute-done | bytes 262176 | tf_op jit(solution)/shard_map/ppermute | solution.py:244
  20.0 0.1 add_convert_fusion.4
  20.0 2.9 %collective-permute-start.1 = (bf16[2,32,512]{2,1,0:T(8,128)(2,1)S(1)}, bf16[2,32,512]{2,1,0:T(8,128)(2,1)S(1)}, u32[]{:S(2)}, u32[]{:S(2)}) collective-permute-start(bf16[2,32,512]{2,1,0:T(8,128)(2,1)S(1)} %get-tuple-element.10), channel_id=1, source_target_pairs={{0,2},{1,3},{2,0},{3,1},{4,6},{5,7},{6,4},{7,5},{8,10},{9,11},{10,... | collective-permute-start | bytes 196616 | tf_op jit(solution)/shard_map/ppermute | solution.py:250
  22.9 1.6 %collective-permute-start.3 = (bf16[2,32,512]{2,1,0:T(8,128)(2,1)S(1)}, bf16[2,32,512]{2,1,0:T(8,128)(2,1)S(1)}, u32[]{:S(2)}, u32[]{:S(2)}) collective-permute-start(bf16[2,32,512]{2,1,0:T(8,128)(2,1)S(1)} %get-tuple-element.11), channel_id=1, source_target_pairs={{0,6},{1,7},{2,4},{3,5},{4,2},{5,3},{6,0},{7,1},{8,14},{9,15},{10,... | collective-permute-start | bytes 196616 | tf_op jit(solution)/shard_map/ppermute | solution.py:250
  24.5 0.0 collective-permute-start.2
  24.5 1.7 %collective-permute-done.1 = bf16[2,32,512]{2,1,0:T(8,128)(2,1)S(1)} collective-permute-done((bf16[2,32,512]{2,1,0:T(8,128)(2,1)S(1)}, bf16[2,32,512]{2,1,0:T(8,128)(2,1)S(1)}, u32[]{:S(2)}, u32[]{:S(2)}) %collective-permute-start.1) | collective-permute-done | bytes 65568 | tf_op jit(solution)/shard_map/ppermute | solution.py:250
  26.1 2.5 %collective-permute-done.3 = bf16[2,32,512]{2,1,0:T(8,128)(2,1)S(1)} collective-permute-done((bf16[2,32,512]{2,1,0:T(8,128)(2,1)S(1)}, bf16[2,32,512]{2,1,0:T(8,128)(2,1)S(1)}, u32[]{:S(2)}, u32[]{:S(2)}) %collective-permute-start.3) | collective-permute-done | bytes 65568 | tf_op jit(solution)/shard_map/ppermute | solution.py:250
  28.6 0.1 collective-permute-done.2
  28.8 2.7 %collective-permute-start.4 = (bf16[2,32,512]{2,1,0:T(8,128)(2,1)S(1)}, bf16[2,32,512]{2,1,0:T(8,128)(2,1)S(1)}, u32[]{:S(2)}, u32[]{:S(2)}) collective-permute-start(bf16[2,32,512]{2,1,0:T(8,128)(2,1)S(1)} %add_convert_fusion.1), channel_id=1, source_target_pairs={{0,8},{1,9},{2,10},{3,11},{4,12},{5,13},{6,14},{7,15},{8,0},{9,1},... | collective-permute-start | bytes 196616 | tf_op jit(solution)/shard_map/ppermute | solution.py:259
  31.4 2.6 %collective-permute-done.4 = bf16[2,32,512]{2,1,0:T(8,128)(2,1)S(1)} collective-permute-done((bf16[2,32,512]{2,1,0:T(8,128)(2,1)S(1)}, bf16[2,32,512]{2,1,0:T(8,128)(2,1)S(1)}, u32[]{:S(2)}, u32[]{:S(2)}) %collective-permute-start.4) | collective-permute-done | bytes 65568 | tf_op jit(solution)/shard_map/ppermute | solution.py:259
  34.0 2.0 %collective-permute-start.7 = (bf16[2,32,512]{2,1,0:T(8,128)(2,1)S(1)}, bf16[2,32,512]{2,1,0:T(8,128)(2,1)S(1)}, u32[]{:S(2)}, u32[]{:S(2)}) collective-permute-start(bf16[2,32,512]{2,1,0:T(8,128)(2,1)S(1)} %add_convert_fusion.refs_3_), channel_id=1, source_target_pairs={{0,6},{1,7},{2,4},{3,5},{4,2},{5,3},{6,0},{7,1},{8,14},{9,15},{10,... | collective-permute-start | bytes 196616 | tf_op jit(solution)/shard_map/ppermute | solution.py:269
  36.1 1.6 %collective-permute-start.6 = (bf16[2,32,512]{2,1,0:T(8,128)(2,1)S(1)}, bf16[2,32,512]{2,1,0:T(8,128)(2,1)S(1)}, u32[]{:S(2)}, u32[]{:S(2)}) collective-permute-start(bf16[2,32,512]{2,1,0:T(8,128)(2,1)S(1)} %add_convert_fusion.refs_3_), channel_id=1, source_target_pairs={{0,4},{1,5},{2,6},{3,7},{4,0},{5,1},{6,2},{7,3},{8,12},{9,13},{10,... | collective-permute-start | bytes 196616 | tf_op jit(solution)/shard_map/ppermute | solution.py:269
  37.7 0.0 collective-permute-start.5
  37.7 1.6 %collective-permute-done.7.refs_6_ = bf16[2,32,512]{2,1,0:T(8,128)(2,1)S(1)} collective-permute-done((bf16[2,32,512]{2,1,0:T(8,128)(2,1)S(1)}, bf16[2,32,512]{2,1,0:T(8,128)(2,1)S(1)}, u32[]{:S(2)}, u32[]{:S(2)}) %collective-permute-start.7) | collective-permute-done | bytes 65568 | tf_op jit(solution)/shard_map/ppermute | solution.py:269
  39.3 0.0 collective-permute-start.11
  39.3 1.4 %collective-permute-done.6.refs_5_ = bf16[2,32,512]{2,1,0:T(8,128)(2,1)S(1)} collective-permute-done((bf16[2,32,512]{2,1,0:T(8,128)(2,1)S(1)}, bf16[2,32,512]{2,1,0:T(8,128)(2,1)S(1)}, u32[]{:S(2)}, u32[]{:S(2)}) %collective-permute-start.6) | collective-permute-done | bytes 65568 | tf_op jit(solution)/shard_map/ppermute | solution.py:269
  40.7 1.3 %collective-permute-done.5.refs_4_ = bf16[2,32,512]{2,1,0:T(8,128)(2,1)S(1)} collective-permute-done((bf16[2,32,512]{2,1,0:T(8,128)(2,1)S(1)}, bf16[2,32,512]{2,1,0:T(8,128)(2,1)S(1)}, u32[]{:S(2)}, u32[]{:S(2)}) %collective-permute-start.5) | collective-permute-done | bytes 65568 | tf_op jit(solution)/shard_map/ppermute | solution.py:269
  42.0 0.6 %slice_bitcast_fusion = bf16[32,512]{1,0:T(8,128)(2,1)} fusion(bf16[2,32,512]{2,1,0:T(8,128)(2,1)S(1)} %add_convert_fusion.refs_3_), kind=kLoop, calls=%fused_computation.5 | loop fusion | bytes 65536 | tf_op jit(solution)/shard_map/squeeze | solution.py:265
  42.6 0.0 collective-permute-done.11.refs_10_
  42.6 0.0 collective-permute-done.10.refs_9_
  42.6 0.6 %collective-permute-done.9.refs_8_ = bf16[2,32,512]{2,1,0:T(8,128)(2,1)S(1)} collective-permute-done((bf16[2,32,512]{2,1,0:T(8,128)(2,1)S(1)}, bf16[2,32,512]{2,1,0:T(8,128)(2,1)S(1)}, u32[]{:S(2)}, u32[]{:S(2)}) %collective-permute-start.9) | collective-permute-done | bytes 65568 | tf_op jit(solution)/shard_map/ppermute | solution.py:270
  43.2 3.7 %scan.1 = f32[32,1024]{1,0:T(8,128)} custom-call(bf16[16,512,1024]{2,1,0:T(8,128)(2,1)S(1)} %get-tuple-element.9.refs_0_, f32[1,1024]{1,0:T(1,128)S(1)} %bitcast.6, f32[1,1024]{1,0:T(1,128)S(1)} %bitcast.8, bf16[2,32,512]{2,1,0:T(8,128)(2,1)S(1)} %add_convert_fusion.refs_3_, bf16[2,32,512]{2,1,0:T(8,128)(2,1)S(1)} %collective-permute-done.5.refs_4_, ...), custom_call_target="tpu_custom_call" | custom-call | tf_op jit(solution)/shard_map/scan/pallas_call | solution.py:277
  (11 shorter events, 0.1 us)
Async XLA Ops:
  0.6 42.6 %copy-start.1 = (f32[1024]{0:T(1024)S(1)}, f32[1024]{0:T(1024)}, u32[]{:S(2)}) copy-start(f32[1024]{0:T(1024)} %param.9) | copy-start | bytes 12292
  0.6 42.6 %copy-start = (f32[1024]{0:T(1024)S(1)}, f32[1024]{0:T(1024)}, u32[]{:S(2)}) copy-start(f32[1024]{0:T(1024)} %param.8) | copy-start | bytes 12292
  18.2 1.7 %collective-permute-start = (bf16[8,32,512]{2,1,0:T(8,128)(2,1)S(1)}, bf16[8,32,512]{2,1,0:T(8,128)(2,1)S(1)}, u32[]{:S(2)}, u32[]{:S(2)}) collective-permute-start(bf16[8,32,512]{2,1,0:T(8,128)(2,1)S(1)} %get-tuple-element.7), channel_id=1, source_target_pairs={{0,1},{1,0},{2,3},{3,2},{4,5},{5,4},{6,7},{7,6},{8,9},{9,8},{10,11... | collective-permute-start | bytes 786440 | tf_op jit(solution)/shard_map/ppermute | solution.py:244
  20.0 6.1 %collective-permute-start.1 = (bf16[2,32,512]{2,1,0:T(8,128)(2,1)S(1)}, bf16[2,32,512]{2,1,0:T(8,128)(2,1)S(1)}, u32[]{:S(2)}, u32[]{:S(2)}) collective-permute-start(bf16[2,32,512]{2,1,0:T(8,128)(2,1)S(1)} %get-tuple-element.10), channel_id=1, source_target_pairs={{0,2},{1,3},{2,0},{3,1},{4,6},{5,7},{6,4},{7,5},{8,10},{9,11},{10,... | collective-permute-start | bytes 196616 | tf_op jit(solution)/shard_map/ppermute | solution.py:250
  22.9 5.7 %collective-permute-start.3 = (bf16[2,32,512]{2,1,0:T(8,128)(2,1)S(1)}, bf16[2,32,512]{2,1,0:T(8,128)(2,1)S(1)}, u32[]{:S(2)}, u32[]{:S(2)}) collective-permute-start(bf16[2,32,512]{2,1,0:T(8,128)(2,1)S(1)} %get-tuple-element.11), channel_id=1, source_target_pairs={{0,6},{1,7},{2,4},{3,5},{4,2},{5,3},{6,0},{7,1},{8,14},{9,15},{10,... | collective-permute-start | bytes 196616 | tf_op jit(solution)/shard_map/ppermute | solution.py:250
  24.5 4.3 %collective-permute-start.2 = (bf16[2,32,512]{2,1,0:T(8,128)(2,1)S(1)}, bf16[2,32,512]{2,1,0:T(8,128)(2,1)S(1)}, u32[]{:S(2)}, u32[]{:S(2)}) collective-permute-start(bf16[2,32,512]{2,1,0:T(8,128)(2,1)S(1)} %get-tuple-element.12), channel_id=1, source_target_pairs={{0,4},{1,5},{2,6},{3,7},{4,0},{5,1},{6,2},{7,3},{8,12},{9,13},{10,... | collective-permute-start | bytes 196616 | tf_op jit(solution)/shard_map/ppermute | solution.py:250
  28.8 5.2 %collective-permute-start.4 = (bf16[2,32,512]{2,1,0:T(8,128)(2,1)S(1)}, bf16[2,32,512]{2,1,0:T(8,128)(2,1)S(1)}, u32[]{:S(2)}, u32[]{:S(2)}) collective-permute-start(bf16[2,32,512]{2,1,0:T(8,128)(2,1)S(1)} %add_convert_fusion.1), channel_id=1, source_target_pairs={{0,8},{1,9},{2,10},{3,11},{4,12},{5,13},{6,14},{7,15},{8,0},{9,1},... | collective-permute-start | bytes 196616 | tf_op jit(solution)/shard_map/ppermute | solution.py:259
  34.0 5.2 %collective-permute-start.7 = (bf16[2,32,512]{2,1,0:T(8,128)(2,1)S(1)}, bf16[2,32,512]{2,1,0:T(8,128)(2,1)S(1)}, u32[]{:S(2)}, u32[]{:S(2)}) collective-permute-start(bf16[2,32,512]{2,1,0:T(8,128)(2,1)S(1)} %add_convert_fusion.refs_3_), channel_id=1, source_target_pairs={{0,6},{1,7},{2,4},{3,5},{4,2},{5,3},{6,0},{7,1},{8,14},{9,15},{10,... | collective-permute-start | bytes 196616 | tf_op jit(solution)/shard_map/ppermute | solution.py:269
  36.1 4.6 %collective-permute-start.6 = (bf16[2,32,512]{2,1,0:T(8,128)(2,1)S(1)}, bf16[2,32,512]{2,1,0:T(8,128)(2,1)S(1)}, u32[]{:S(2)}, u32[]{:S(2)}) collective-permute-start(bf16[2,32,512]{2,1,0:T(8,128)(2,1)S(1)} %add_convert_fusion.refs_3_), channel_id=1, source_target_pairs={{0,4},{1,5},{2,6},{3,7},{4,0},{5,1},{6,2},{7,3},{8,12},{9,13},{10,... | collective-permute-start | bytes 196616 | tf_op jit(solution)/shard_map/ppermute | solution.py:269
  37.7 4.3 %collective-permute-start.5 = (bf16[2,32,512]{2,1,0:T(8,128)(2,1)S(1)}, bf16[2,32,512]{2,1,0:T(8,128)(2,1)S(1)}, u32[]{:S(2)}, u32[]{:S(2)}) collective-permute-start(bf16[2,32,512]{2,1,0:T(8,128)(2,1)S(1)} %add_convert_fusion.refs_3_), channel_id=1, source_target_pairs={{0,2},{1,3},{2,0},{3,1},{4,6},{5,7},{6,4},{7,5},{8,10},{9,11},{10,... | collective-permute-start | bytes 196616 | tf_op jit(solution)/shard_map/ppermute | solution.py:269
  37.7 4.9 %collective-permute-start.8 = (bf16[2,32,512]{2,1,0:T(8,128)(2,1)S(1)}, bf16[2,32,512]{2,1,0:T(8,128)(2,1)S(1)}, u32[]{:S(2)}, u32[]{:S(2)}) collective-permute-start(bf16[2,32,512]{2,1,0:T(8,128)(2,1)S(1)} %add_convert_fusion.refs_3_), channel_id=1, source_target_pairs={{0,1},{1,0},{2,3},{3,2},{4,5},{5,4},{6,7},{7,6},{8,9},{9,8},{10,11... | collective-permute-start | bytes 196616 | tf_op jit(solution)/shard_map/ppermute | solution.py:270
  39.3 3.3 %collective-permute-start.11 = (bf16[2,32,512]{2,1,0:T(8,128)(2,1)S(1)}, bf16[2,32,512]{2,1,0:T(8,128)(2,1)S(1)}, u32[]{:S(2)}, u32[]{:S(2)}) collective-permute-start(bf16[2,32,512]{2,1,0:T(8,128)(2,1)S(1)} %collective-permute-done.7.refs_6_), channel_id=1, source_target_pairs={{0,1},{1,0},{2,3},{3,2},{4,5},{5,4},{6,7},{7,6},{8,9},{9,8},{10,11... | collective-permute-start | bytes 196616 | tf_op jit(solution)/shard_map/ppermute | solution.py:270
  40.6 2.0 %collective-permute-start.10 = (bf16[2,32,512]{2,1,0:T(8,128)(2,1)S(1)}, bf16[2,32,512]{2,1,0:T(8,128)(2,1)S(1)}, u32[]{:S(2)}, u32[]{:S(2)}) collective-permute-start(bf16[2,32,512]{2,1,0:T(8,128)(2,1)S(1)} %collective-permute-done.6.refs_5_), channel_id=1, source_target_pairs={{0,1},{1,0},{2,3},{3,2},{4,5},{5,4},{6,7},{7,6},{8,9},{9,8},{10,11... | collective-permute-start | bytes 196616 | tf_op jit(solution)/shard_map/ppermute | solution.py:270
  42.0 1.3 %collective-permute-start.9 = (bf16[2,32,512]{2,1,0:T(8,128)(2,1)S(1)}, bf16[2,32,512]{2,1,0:T(8,128)(2,1)S(1)}, u32[]{:S(2)}, u32[]{:S(2)}) collective-permute-start(bf16[2,32,512]{2,1,0:T(8,128)(2,1)S(1)} %collective-permute-done.5.refs_4_), channel_id=1, source_target_pairs={{0,1},{1,0},{2,3},{3,2},{4,5},{5,4},{6,7},{7,6},{8,9},{9,8},{10,11... | collective-permute-start | bytes 196616 | tf_op jit(solution)/shard_map/ppermute | solution.py:270

commit v2 on v1

--- a/solution.py
+++ b/solution.py
@@ -7,12 +7,44 @@
 
 LANES = 128
 MIB = 1 << 20
+SMALL = jnp.float8_e4m3fn
+LARGEST = 448.0
+SHIFT = 16.0
+EFFECT_SCALE = 1024.0
+
+
+def row_scale(values):
+    largest = jnp.max(jnp.abs(values), axis=1, keepdims=True)
+    scale = jnp.full_like(largest, 2.0**-30)
+    for step in (32, 16, 8, 4, 2, 1):
+        raised = scale * 2.0**step
+        scale = jnp.where(largest * raised <= LARGEST, raised, scale)
+    return scale
+
+
+def split(values, count):
+    parts = []
+    for i in range(count):
+        part = values.astype(SMALL)
+        parts.append(part)
+        if i + 1 < count:
+            values = (values - part.astype(jnp.float32)) * SHIFT
+    return jnp.concatenate(parts, axis=0)
+
+
+def join(sums, count):
+    rows = sums.shape[0] // count
+    total = sums[(count - 1) * rows :]
+    for i in reversed(range(count - 1)):
+        total = sums[i * rows : (i + 1) * rows] + total * (1.0 / SHIFT)
+    return total
 
 
 def evolve_kernel(
     blocks,
     share,
-    order,
+    flight,
+    relative_of,
     genotypes_hbm,
     noise_hbm,
     means_hbm,
@@ -24,6 +56,7 @@
     send_ref,
     keep_ref,
     tail_ref,
+    staged_ref,
     causal_ref,
     effects_ref,
     means_ref,
@@ -42,11 +75,12 @@
     pheno, variants = weight_ref.shape
     me = lax.axis_index("var")
     tails = tail_ref.shape[0]
-
-    def fetch(r):
-        start = pl.multiple_of((me ^ r) * share, share)
+    half = blocks // 2
+
+    def fetch(i):
+        start = pl.multiple_of((me ^ relative_of(i)) * share, share)
         return pltpu.make_async_copy(
-            genotypes_hbm.at[pl.ds(start, share), :], held_ref.at[r], block_sem.at[r]
+            genotypes_hbm.at[pl.ds(start, share), :], staged_ref.at[i], block_sem.at[i]
         )
 
     def fetch_noise(t):
@@ -69,10 +103,10 @@
     ]
     for copy in small:
         copy.start()
+    for i in range(flight):
+        fetch(i).start()
     for t in range(tails):
         fetch_noise(t).start()
-    for r in order:
-        fetch(r).start()
 
     causal_count = causal_ref.shape[1]
     high_count = variants // LANES
@@ -85,36 +119,44 @@
     inside = (local >= 0) & (local < variants)
     high_ref[:, :causal_count] = jnp.where(inside, local // LANES, -1)
     low_ref[:, :causal_count] = jnp.where(inside, local % LANES, 0)
-    value_ref[:, :causal_count] = effects_ref[...]
+    value_ref[:, :causal_count] = effects_ref[...] * EFFECT_SCALE
     width = high_ref.shape[1]
     high_iota = lax.broadcasted_iota(jnp.int32, (high_count, width), 0)
-    low_iota = lax.broadcasted_iota(jnp.int32, (LANES, width), 0)
-
-    def build(p, carry):
+    low_iota = lax.broadcasted_iota(jnp.int32, (LANES, width), 0).astype(jnp.int16)
+
+    def build(p):
         row = pl.ds(p, 1)
         value = jnp.where(high_ref[row, :] == high_iota, value_ref[row, :], 0.0)
-        first = value.astype(jnp.bfloat16)
-        rest = value - first.astype(jnp.float32)
-        second = rest.astype(jnp.bfloat16)
-        third = (rest - second.astype(jnp.float32)).astype(jnp.bfloat16)
-        hits = jnp.where(low_ref[row, :] == low_iota, 1.0, 0.0).astype(jnp.bfloat16)
-        parts = jnp.concatenate([first, second, third], axis=0)
+        low = jnp.broadcast_to(low_ref[row, :], (LANES, width)).astype(jnp.int16)
+        hits = jnp.where(low == low_iota, jnp.bfloat16(1), jnp.bfloat16(0)).astype(SMALL)
         sums = lax.dot_general(
-            parts, hits, (((1,), (1,)), ((), ())), preferred_element_type=jnp.float32
-        )
-        beta_ref[p] = (
-            sums[:high_count] + sums[high_count : 2 * high_count] + sums[2 * high_count :]
-        )
+            split(value, 4), hits, (((1,), (1,)), ((), ())), preferred_element_type=jnp.float32
+        )
+        beta_ref[p] = join(sums, 4) * (1.0 / EFFECT_SCALE)
+
+    per_step = -(-pheno // half)
+
+    def first(i, carry):
+        fetch(i).wait()
+
+        @pl.when(i + flight < blocks)
+        def _():
+            fetch(i + flight).start()
+
+        held_ref[i] = staged_ref[i].astype(SMALL)
+        for j in range(per_step):
+            build(jnp.minimum(i * per_step + j, pheno - 1))
         return carry
 
-    lax.fori_loop(0, pheno, build, 0, unroll=2)
+    lax.fori_loop(0, half, first, 0)
 
     offset = jnp.zeros((pheno, LANES), jnp.float32)
     for h in range(high_count):
         lanes = slice(h * LANES, (h + 1) * LANES)
         weight = (beta_ref[:, h, :] / scales_ref[:, lanes]).astype(jnp.bfloat16)
+        weight = weight.astype(jnp.float32)
         weight_ref[:, lanes] = weight
-        offset += weight.astype(jnp.float32) * means_ref[:, lanes]
+        offset += weight * means_ref[:, lanes]
     offset = jnp.sum(offset, axis=1, keepdims=True)
 
     square = (pheno, pheno)
@@ -132,40 +174,53 @@
         fetch_noise(t).wait()
         tail_ref[t] = light * noise_ref[t].astype(jnp.float32)
 
-    weights = weight_ref[...]
-    half = blocks // 2
-    for i, r in enumerate(order):
-        fetch(r).wait()
-        part = heavy * (
-            lax.dot_general(
-                weights,
-                held_ref[r],
-                (((1,), (1,)), ((), ())),
-                preferred_element_type=jnp.float32,
-            )
-            - offset
-        )
-        if i < half:
-            send_ref[i] = part.astype(send_ref.dtype)
-        else:
-            keep_ref[i - half] = part.astype(keep_ref.dtype)
+    scale = row_scale(weight_ref[...])
+    weights = split(weight_ref[...] * scale, 2)
+    factor = heavy / scale
+    shift = heavy * offset
+
+    def partial(i):
+        sums = lax.dot_general(
+            weights, held_ref[i], (((1,), (1,)), ((), ())), preferred_element_type=jnp.float32
+        )
+        return join(sums, 2) * factor - shift
+
+    def second(i, carry):
+        send_ref[i] = partial(i).astype(send_ref.dtype)
+        late = half + i
+        fetch(late).wait()
+
+        @pl.when(late + flight < blocks)
+        def _():
+            fetch(late + flight).start()
+
+        held_ref[late] = staged_ref[late].astype(SMALL)
+        keep_ref[i] = partial(late).astype(keep_ref.dtype)
+        return carry
+
+    lax.fori_loop(0, half, second, 0)
 
 
 def scan_kernel(order, scale_back, *refs):
     held_ref, means_ref, scales_ref = refs[:3]
-    pieces = refs[3:-1]
-    out_ref = refs[-1]
+    pieces = refs[3:-2]
+    phen_ref, out_ref = refs[-2:]
+    values = [piece[j].astype(jnp.float32) for piece in pieces for j in range(piece.shape[0])]
+    phen_ref[...] = pieces[0][0]
+    largest = values[0]
+    column = values[0]
+    for value in values[1:]:
+        largest = jnp.maximum(jnp.abs(largest), jnp.abs(value))
+        column = column + value
+    column = jnp.sum(column, axis=1, keepdims=True)
+    scale = row_scale(largest)
     total = None
-    column = None
-    position = 0
-    for piece in pieces:
-        for j in range(piece.shape[0]):
-            values = piece[j]
-            part = jnp.dot(values, held_ref[order[position]], preferred_element_type=jnp.float32)
-            sums = jnp.sum(values.astype(jnp.float32), axis=1, keepdims=True)
-            total = part if total is None else total + part
-            column = sums if column is None else column + sums
-            position += 1
+    for i, value in enumerate(values):
+        part = jnp.dot(
+            split(value * scale, 2), held_ref[order[i]], preferred_element_type=jnp.float32
+        )
+        total = part if total is None else total + part
+    total = join(total, 2) / scale
     if scale_back is None:
         out_ref[...] = total
     else:
@@ -183,10 +238,15 @@
         raise ValueError("var size")
     tails = blocks // 8
 
-    def relative(core, group, tail):
-        return core + 2 * group + 8 * tail
-
-    order = [relative(c, g, t) for c in (1, 0) for g in (1, 2, 3, 0) for t in range(tails)]
+    half = blocks // 2
+
+    def relative_of(i):
+        core = 1 - i // half
+        group = (i % half // tails + 1) % 4
+        return core + 2 * group + 8 * (i % tails)
+
+    def position(core, group, tail):
+        return (1 - core) * half + (group + 3) % 4 * tails + tail
 
     def pairs(k):
         return [(i, i ^ k) for i in range(blocks)]
@@ -196,12 +256,11 @@
     means_row = means[None, :]
     scales_row = scales[None, :]
     width = -(-causal_count // LANES) * LANES
-    half = blocks // 2
 
     held, send, keep, tail = pl.pallas_call(
-        lambda *refs: evolve_kernel(blocks, share, order, *refs),
+        lambda *refs: evolve_kernel(blocks, share, half, relative_of, *refs),
         out_shape=(
-            jax.ShapeDtypeStruct((blocks, share, variants), genotypes.dtype),
+            jax.ShapeDtypeStruct((blocks, share, variants), SMALL),
             jax.ShapeDtypeStruct((half, pheno, share), jnp.bfloat16),
             jax.ShapeDtypeStruct((half, pheno, share), jnp.float32),
             jax.ShapeDtypeStruct((tails, pheno, share), jnp.float32),
@@ -209,6 +268,7 @@
         in_specs=[hbm] * 7,
         out_specs=[vmem] * 4,
         scratch_shapes=[
+            pltpu.VMEM((blocks, share, variants), genotypes.dtype),
             pltpu.VMEM((pheno, causal_count), jnp.int32),
             pltpu.VMEM((pheno, causal_count), jnp.float32),
             pltpu.VMEM((1, variants), jnp.float32),
@@ -218,13 +278,13 @@
             pltpu.VMEM((pheno, width), jnp.int32),
             pltpu.VMEM((pheno, width), jnp.float32),
             pltpu.VMEM((pheno, variants // LANES, LANES), jnp.float32),
-            pltpu.VMEM((pheno, variants), jnp.bfloat16),
+            pltpu.VMEM((pheno, variants), jnp.float32),
             pltpu.VMEM((tails, pheno, share), jnp.bfloat16),
             pltpu.SemaphoreType.DMA((blocks,)),
             pltpu.SemaphoreType.DMA((tails,)),
             pltpu.SemaphoreType.DMA((5,)),
         ],
-        compiler_params=pltpu.CompilerParams(vmem_limit_bytes=8 * MIB),
+        compiler_params=pltpu.CompilerParams(vmem_limit_bytes=24 * MIB),
         name="evolve",
     )(
         *(
@@ -262,23 +322,24 @@
         step *= 2
 
     own = (total + tail).astype(jnp.bfloat16)
-    phen_out = own[0]
-
     groups = {0: own}
     for g in (1, 2, 3):
         groups[g] = lax.ppermute(own, "var", pairs(2 * g))
     others = {g: lax.ppermute(groups[g], "var", pairs(1)) for g in range(4)}
     pieces = [groups[g] for g in range(4)] + [others[g] for g in range(4)]
-    used = [relative(c, g, t) for c in (0, 1) for g in range(4) for t in range(tails)]
+    used = [position(c, g, t) for c in (0, 1) for g in range(4) for t in range(tails)]
 
     alone = samp == 1
     total_samples = jnp.float32(samples * samp)
     scale_back = float(samples * samp) ** 0.5 if alone else None
-    scores = pl.pallas_call(
+    phen_out, scores = pl.pallas_call(
         lambda *refs: scan_kernel(used, scale_back, *refs),
-        out_shape=jax.ShapeDtypeStruct((pheno, variants), jnp.float32),
+        out_shape=(
+            jax.ShapeDtypeStruct((pheno, share), jnp.bfloat16),
+            jax.ShapeDtypeStruct((pheno, variants), jnp.float32),
+        ),
         in_specs=[vmem] * (3 + len(pieces)),
-        out_specs=vmem,
+        out_specs=[vmem] * 2,
         compiler_params=pltpu.CompilerParams(vmem_limit_bytes=8 * MIB),
         name="scan",
     )(held, means_row, scales_row, *pieces)

time: 47.1 us -> 39.4 us (0.84)
  Pallas kernels: 21.2 us -> 13.6 us
  waiting for transfers between devices: 12.9 us -> 13.6 us
  local copies, waits for them, and re-layouts: 0.63 us -> 0.01 us
    pallas_call x1, Pallas kernels: 17.6 us -> 11.5 us  [on_device(): pl.pallas_call(lambda *refs: evolve_kernel(blocks, share, half, relative_...]
    pallas_call x1, Pallas kernels: 3.67 us -> 2.08 us  [on_device(): pl.pallas_call(lambda *refs: scan_kernel(used, scale_back, *refs), out_sh...]
    ppermute x1, waiting for transfers between devices: 2.58 us -> 3.31 us  [on_device(): other = lax.ppermute(mine, 'var', pairs(8 * step))]
    squeeze x1 -> x0, local copies, waits for them, and re-layouts: 0.62 us -> none  [on_device(): phen_out = own[0]]
    ppermute x4, waiting for transfers between devices: 0.63 us -> 1.24 us  [on_device(): others = {g: lax.ppermute(groups[g], 'var', pairs(1)) for g in range(4)}]
    ppermute x3, waiting for transfers between devices: 4.25 us -> 3.66 us  [on_device(): groups[g] = lax.ppermute(own, 'var', pairs(2 * g))]
  transfers between devices with their start and end apart: 12 -> 12, of which waited for: 9 -> 9; matrix products, arithmetic and copies ran while one was open for 1% -> 0% of each run, Pallas kernels for 0% -> 0%
where the time goes in v2:
time: 39.4 us; the launch traced here: 39.2 us
  Pallas kernels  13.6 us (35%)
  waiting for transfers between devices  13.6 us (35%)
  starting transfers between devices  11.2 us (28%)
  between operations  0.69 us (2%)
    pallas_call x1, Pallas kernels, on_device(): pl.pallas_call(lambda *refs: evolve_kernel(blocks, share, half, relative_...  11.5 us
    ppermute x3, starting transfers between devices, on_device(): lax.ppermute(chip[g - 1].astype(jnp.bfloat16), 'var', pairs(2 * g))  4.44 us
    ppermute x3, waiting for transfers between devices, on_device(): lax.ppermute(chip[g - 1].astype(jnp.bfloat16), 'var', pairs(2 * g))  4.26 us
    ppermute x3, waiting for transfers between devices, on_device(): groups[g] = lax.ppermute(own, 'var', pairs(2 * g))  3.66 us
    ppermute x3, starting transfers between devices, on_device(): groups[g] = lax.ppermute(own, 'var', pairs(2 * g))  3.55 us
    ppermute x1, waiting for transfers between devices, on_device(): other = lax.ppermute(mine, 'var', pairs(8 * step))  3.31 us
    ppermute x1, starting transfers between devices, on_device(): other = lax.ppermute(mine, 'var', pairs(8 * step))  2.62 us
    pallas_call x1, Pallas kernels, on_device(): pl.pallas_call(lambda *refs: scan_kernel(used, scale_back, *refs), out_sh...  2.08 us
  transfers between devices with their start and end apart: 12, of which 9 were waited for; matrix products, arithmetic and copies ran while one was open for 0% of the time, Pallas kernels for 0%

profile of v2, /device:TPU:0, one launch (start us, length us, event | category | flops | bytes accessed | tf_op | source)
XLA Modules:
  0.0 39.2 jit_solution(2644375209453270220)
XLA Ops:
  0.7 11.5 %evolve.1 = (f8e4m3fn[16,512,1024]{2,1,0:T(32,128)(4,1)S(1)}, bf16[8,32,512]{2,1,0:T(8,128)(2,1)S(1)}, f32[8,32,512]{2,1,0:T(8,128)S(1)}, f32[2,32,512]{2,1,0:T(8,128)S(1)}) custom-call(bf16[8192,1024]{1,0:T(8,128)(2,1)} %refs_0_.1, bf16[32,8192]{1,0:T(8,128)(2,1)} %refs_1_.1, f32[1,1024]{1,0:T(1,128)} %bitcast.3, f32[1,1024]{1,0:T(1,128)} %bitcast.5, ...), custom_call_target="tpu_custom_call" | custom-call | tf_op jit(solution)/shard_map/evolve/pallas_call | solution.py:260
  12.1 0.6 %collective-permute-start = (bf16[8,32,512]{2,1,0:T(8,128)(2,1)S(1)}, bf16[8,32,512]{2,1,0:T(8,128)(2,1)S(1)}, u32[]{:S(2)}, u32[]{:S(2)}) collective-permute-start(bf16[8,32,512]{2,1,0:T(8,128)(2,1)S(1)} %get-tuple-element.8), channel_id=1, source_target_pairs={{0,1},{1,0},{2,3},{3,2},{4,5},{5,4},{6,7},{7,6},{8,9},{9,8},{10,11... | collective-permute-start | bytes 786440 | tf_op jit(solution)/shard_map/ppermute | solution.py:304
  12.7 1.2 %collective-permute-done = bf16[8,32,512]{2,1,0:T(8,128)(2,1)S(1)} collective-permute-done((bf16[8,32,512]{2,1,0:T(8,128)(2,1)S(1)}, bf16[8,32,512]{2,1,0:T(8,128)(2,1)S(1)}, u32[]{:S(2)}, u32[]{:S(2)}) %collective-permute-start) | collective-permute-done | bytes 262176 | tf_op jit(solution)/shard_map/ppermute | solution.py:304
  13.9 0.1 add_convert_fusion.4
  13.9 2.9 %collective-permute-start.1 = (bf16[2,32,512]{2,1,0:T(8,128)(2,1)S(1)}, bf16[2,32,512]{2,1,0:T(8,128)(2,1)S(1)}, u32[]{:S(2)}, u32[]{:S(2)}) collective-permute-start(bf16[2,32,512]{2,1,0:T(8,128)(2,1)S(1)} %get-tuple-element.10), channel_id=1, source_target_pairs={{0,2},{1,3},{2,0},{3,1},{4,6},{5,7},{6,4},{7,5},{8,10},{9,11},{10,... | collective-permute-start | bytes 196616 | tf_op jit(solution)/shard_map/ppermute | solution.py:310
  16.8 1.6 %collective-permute-start.3 = (bf16[2,32,512]{2,1,0:T(8,128)(2,1)S(1)}, bf16[2,32,512]{2,1,0:T(8,128)(2,1)S(1)}, u32[]{:S(2)}, u32[]{:S(2)}) collective-permute-start(bf16[2,32,512]{2,1,0:T(8,128)(2,1)S(1)} %get-tuple-element.11), channel_id=1, source_target_pairs={{0,6},{1,7},{2,4},{3,5},{4,2},{5,3},{6,0},{7,1},{8,14},{9,15},{10,... | collective-permute-start | bytes 196616 | tf_op jit(solution)/shard_map/ppermute | solution.py:310
  18.4 0.0 collective-permute-start.2
  18.4 1.6 %collective-permute-done.1 = bf16[2,32,512]{2,1,0:T(8,128)(2,1)S(1)} collective-permute-done((bf16[2,32,512]{2,1,0:T(8,128)(2,1)S(1)}, bf16[2,32,512]{2,1,0:T(8,128)(2,1)S(1)}, u32[]{:S(2)}, u32[]{:S(2)}) %collective-permute-start.1) | collective-permute-done | bytes 65568 | tf_op jit(solution)/shard_map/ppermute | solution.py:310
  20.0 2.5 %collective-permute-done.3 = bf16[2,32,512]{2,1,0:T(8,128)(2,1)S(1)} collective-permute-done((bf16[2,32,512]{2,1,0:T(8,128)(2,1)S(1)}, bf16[2,32,512]{2,1,0:T(8,128)(2,1)S(1)}, u32[]{:S(2)}, u32[]{:S(2)}) %collective-permute-start.3) | collective-permute-done | bytes 65568 | tf_op jit(solution)/shard_map/ppermute | solution.py:310
  22.5 0.1 collective-permute-done.2
  22.7 2.6 %collective-permute-start.4 = (bf16[2,32,512]{2,1,0:T(8,128)(2,1)S(1)}, bf16[2,32,512]{2,1,0:T(8,128)(2,1)S(1)}, u32[]{:S(2)}, u32[]{:S(2)}) collective-permute-start(bf16[2,32,512]{2,1,0:T(8,128)(2,1)S(1)} %add_convert_fusion.1), channel_id=1, source_target_pairs={{0,8},{1,9},{2,10},{3,11},{4,12},{5,13},{6,14},{7,15},{8,0},{9,1},... | collective-permute-start | bytes 196616 | tf_op jit(solution)/shard_map/ppermute | solution.py:319
  25.3 3.3 %collective-permute-done.4 = bf16[2,32,512]{2,1,0:T(8,128)(2,1)S(1)} collective-permute-done((bf16[2,32,512]{2,1,0:T(8,128)(2,1)S(1)}, bf16[2,32,512]{2,1,0:T(8,128)(2,1)S(1)}, u32[]{:S(2)}, u32[]{:S(2)}) %collective-permute-start.4) | collective-permute-done | bytes 65568 | tf_op jit(solution)/shard_map/ppermute | solution.py:319
  28.6 1.3 %collective-permute-start.7 = (bf16[2,32,512]{2,1,0:T(8,128)(2,1)S(1)}, bf16[2,32,512]{2,1,0:T(8,128)(2,1)S(1)}, u32[]{:S(2)}, u32[]{:S(2)}) collective-permute-start(bf16[2,32,512]{2,1,0:T(8,128)(2,1)S(1)} %add_convert_fusion.refs_3_), channel_id=1, source_target_pairs={{0,6},{1,7},{2,4},{3,5},{4,2},{5,3},{6,0},{7,1},{8,14},{9,15},{10,... | collective-permute-start | bytes 196616 | tf_op jit(solution)/shard_map/ppermute | solution.py:327
  30.0 1.6 %collective-permute-start.6 = (bf16[2,32,512]{2,1,0:T(8,128)(2,1)S(1)}, bf16[2,32,512]{2,1,0:T(8,128)(2,1)S(1)}, u32[]{:S(2)}, u32[]{:S(2)}) collective-permute-start(bf16[2,32,512]{2,1,0:T(8,128)(2,1)S(1)} %add_convert_fusion.refs_3_), channel_id=1, source_target_pairs={{0,4},{1,5},{2,6},{3,7},{4,0},{5,1},{6,2},{7,3},{8,12},{9,13},{10,... | collective-permute-start | bytes 196616 | tf_op jit(solution)/shard_map/ppermute | solution.py:327
  31.6 0.6 %collective-permute-start.5 = (bf16[2,32,512]{2,1,0:T(8,128)(2,1)S(1)}, bf16[2,32,512]{2,1,0:T(8,128)(2,1)S(1)}, u32[]{:S(2)}, u32[]{:S(2)}) collective-permute-start(bf16[2,32,512]{2,1,0:T(8,128)(2,1)S(1)} %add_convert_fusion.refs_3_), channel_id=1, source_target_pairs={{0,2},{1,3},{2,0},{3,1},{4,6},{5,7},{6,4},{7,5},{8,10},{9,11},{10,... | collective-permute-start | bytes 196616 | tf_op jit(solution)/shard_map/ppermute | solution.py:327
  32.2 0.0 collective-permute-start.8
  32.2 1.7 %collective-permute-done.7.refs_6_ = bf16[2,32,512]{2,1,0:T(8,128)(2,1)S(1)} collective-permute-done((bf16[2,32,512]{2,1,0:T(8,128)(2,1)S(1)}, bf16[2,32,512]{2,1,0:T(8,128)(2,1)S(1)}, u32[]{:S(2)}, u32[]{:S(2)}) %collective-permute-start.7) | collective-permute-done | bytes 65568 | tf_op jit(solution)/shard_map/ppermute | solution.py:327
  33.9 0.0 collective-permute-start.11
  33.9 0.7 %collective-permute-done.6.refs_5_ = bf16[2,32,512]{2,1,0:T(8,128)(2,1)S(1)} collective-permute-done((bf16[2,32,512]{2,1,0:T(8,128)(2,1)S(1)}, bf16[2,32,512]{2,1,0:T(8,128)(2,1)S(1)}, u32[]{:S(2)}, u32[]{:S(2)}) %collective-permute-start.6) | collective-permute-done | bytes 65568 | tf_op jit(solution)/shard_map/ppermute | solution.py:327
  34.5 0.0 collective-permute-start.10
  34.6 1.3 %collective-permute-done.5.refs_4_ = bf16[2,32,512]{2,1,0:T(8,128)(2,1)S(1)} collective-permute-done((bf16[2,32,512]{2,1,0:T(8,128)(2,1)S(1)}, bf16[2,32,512]{2,1,0:T(8,128)(2,1)S(1)}, u32[]{:S(2)}, u32[]{:S(2)}) %collective-permute-start.5) | collective-permute-done | bytes 65568 | tf_op jit(solution)/shard_map/ppermute | solution.py:327
  35.9 0.0 collective-permute-done.10.refs_9_
  35.9 1.2 %collective-permute-done.9.refs_8_ = bf16[2,32,512]{2,1,0:T(8,128)(2,1)S(1)} collective-permute-done((bf16[2,32,512]{2,1,0:T(8,128)(2,1)S(1)}, bf16[2,32,512]{2,1,0:T(8,128)(2,1)S(1)}, u32[]{:S(2)}, u32[]{:S(2)}) %collective-permute-start.9) | collective-permute-done | bytes 65568 | tf_op jit(solution)/shard_map/ppermute | solution.py:328
  37.1 2.1 %scan.1 = (bf16[32,512]{1,0:T(8,128)(2,1)}, f32[32,1024]{1,0:T(8,128)}) custom-call(f8e4m3fn[16,512,1024]{2,1,0:T(32,128)(4,1)S(1)} %get-tuple-element.6.refs_0_, f32[1,1024]{1,0:T(1,128)S(1)} %bitcast.4, f32[1,1024]{1,0:T(1,128)S(1)} %bitcast.6, bf16[2,32,512]{2,1,0:T(8,128)(2,1)S(1)} %add_convert_fusion.refs_3_, ...), custom_call_target="tpu_custom_call" | custom-call | tf_op jit(solution)/shard_map/scan/pallas_call | solution.py:335
  (10 shorter events, 0.1 us)
Async XLA Ops:
  0.6 36.5 %copy-start.1 = (f32[1024]{0:T(1024)S(1)}, f32[1024]{0:T(1024)}, u32[]{:S(2)}) copy-start(f32[1024]{0:T(1024)} %param.9) | copy-start | bytes 12292
  0.6 36.5 %copy-start = (f32[1024]{0:T(1024)S(1)}, f32[1024]{0:T(1024)}, u32[]{:S(2)}) copy-start(f32[1024]{0:T(1024)} %param.8) | copy-start | bytes 12292
  12.1 1.7 %collective-permute-start = (bf16[8,32,512]{2,1,0:T(8,128)(2,1)S(1)}, bf16[8,32,512]{2,1,0:T(8,128)(2,1)S(1)}, u32[]{:S(2)}, u32[]{:S(2)}) collective-permute-start(bf16[8,32,512]{2,1,0:T(8,128)(2,1)S(1)} %get-tuple-element.8), channel_id=1, source_target_pairs={{0,1},{1,0},{2,3},{3,2},{4,5},{5,4},{6,7},{7,6},{8,9},{9,8},{10,11... | collective-permute-start | bytes 786440 | tf_op jit(solution)/shard_map/ppermute | solution.py:304
  13.9 6.1 %collective-permute-start.1 = (bf16[2,32,512]{2,1,0:T(8,128)(2,1)S(1)}, bf16[2,32,512]{2,1,0:T(8,128)(2,1)S(1)}, u32[]{:S(2)}, u32[]{:S(2)}) collective-permute-start(bf16[2,32,512]{2,1,0:T(8,128)(2,1)S(1)} %get-tuple-element.10), channel_id=1, source_target_pairs={{0,2},{1,3},{2,0},{3,1},{4,6},{5,7},{6,4},{7,5},{8,10},{9,11},{10,... | collective-permute-start | bytes 196616 | tf_op jit(solution)/shard_map/ppermute | solution.py:310
  16.8 5.7 %collective-permute-start.3 = (bf16[2,32,512]{2,1,0:T(8,128)(2,1)S(1)}, bf16[2,32,512]{2,1,0:T(8,128)(2,1)S(1)}, u32[]{:S(2)}, u32[]{:S(2)}) collective-permute-start(bf16[2,32,512]{2,1,0:T(8,128)(2,1)S(1)} %get-tuple-element.11), channel_id=1, source_target_pairs={{0,6},{1,7},{2,4},{3,5},{4,2},{5,3},{6,0},{7,1},{8,14},{9,15},{10,... | collective-permute-start | bytes 196616 | tf_op jit(solution)/shard_map/ppermute | solution.py:310
  18.4 4.3 %collective-permute-start.2 = (bf16[2,32,512]{2,1,0:T(8,128)(2,1)S(1)}, bf16[2,32,512]{2,1,0:T(8,128)(2,1)S(1)}, u32[]{:S(2)}, u32[]{:S(2)}) collective-permute-start(bf16[2,32,512]{2,1,0:T(8,128)(2,1)S(1)} %get-tuple-element.12), channel_id=1, source_target_pairs={{0,4},{1,5},{2,6},{3,7},{4,0},{5,1},{6,2},{7,3},{8,12},{9,13},{10,... | collective-permute-start | bytes 196616 | tf_op jit(solution)/shard_map/ppermute | solution.py:310
  22.7 5.9 %collective-permute-start.4 = (bf16[2,32,512]{2,1,0:T(8,128)(2,1)S(1)}, bf16[2,32,512]{2,1,0:T(8,128)(2,1)S(1)}, u32[]{:S(2)}, u32[]{:S(2)}) collective-permute-start(bf16[2,32,512]{2,1,0:T(8,128)(2,1)S(1)} %add_convert_fusion.1), channel_id=1, source_target_pairs={{0,8},{1,9},{2,10},{3,11},{4,12},{5,13},{6,14},{7,15},{8,0},{9,1},... | collective-permute-start | bytes 196616 | tf_op jit(solution)/shard_map/ppermute | solution.py:319
  28.6 5.2 %collective-permute-start.7 = (bf16[2,32,512]{2,1,0:T(8,128)(2,1)S(1)}, bf16[2,32,512]{2,1,0:T(8,128)(2,1)S(1)}, u32[]{:S(2)}, u32[]{:S(2)}) collective-permute-start(bf16[2,32,512]{2,1,0:T(8,128)(2,1)S(1)} %add_convert_fusion.refs_3_), channel_id=1, source_target_pairs={{0,6},{1,7},{2,4},{3,5},{4,2},{5,3},{6,0},{7,1},{8,14},{9,15},{10,... | collective-permute-start | bytes 196616 | tf_op jit(solution)/shard_map/ppermute | solution.py:327
  30.0 4.6 %collective-permute-start.6 = (bf16[2,32,512]{2,1,0:T(8,128)(2,1)S(1)}, bf16[2,32,512]{2,1,0:T(8,128)(2,1)S(1)}, u32[]{:S(2)}, u32[]{:S(2)}) collective-permute-start(bf16[2,32,512]{2,1,0:T(8,128)(2,1)S(1)} %add_convert_fusion.refs_3_), channel_id=1, source_target_pairs={{0,4},{1,5},{2,6},{3,7},{4,0},{5,1},{6,2},{7,3},{8,12},{9,13},{10,... | collective-permute-start | bytes 196616 | tf_op jit(solution)/shard_map/ppermute | solution.py:327
  31.6 4.3 %collective-permute-start.5 = (bf16[2,32,512]{2,1,0:T(8,128)(2,1)S(1)}, bf16[2,32,512]{2,1,0:T(8,128)(2,1)S(1)}, u32[]{:S(2)}, u32[]{:S(2)}) collective-permute-start(bf16[2,32,512]{2,1,0:T(8,128)(2,1)S(1)} %add_convert_fusion.refs_3_), channel_id=1, source_target_pairs={{0,2},{1,3},{2,0},{3,1},{4,6},{5,7},{6,4},{7,5},{8,10},{9,11},{10,... | collective-permute-start | bytes 196616 | tf_op jit(solution)/shard_map/ppermute | solution.py:327
  32.2 3.7 %collective-permute-start.8 = (bf16[2,32,512]{2,1,0:T(8,128)(2,1)S(1)}, bf16[2,32,512]{2,1,0:T(8,128)(2,1)S(1)}, u32[]{:S(2)}, u32[]{:S(2)}) collective-permute-start(bf16[2,32,512]{2,1,0:T(8,128)(2,1)S(1)} %add_convert_fusion.refs_3_), channel_id=1, source_target_pairs={{0,1},{1,0},{2,3},{3,2},{4,5},{5,4},{6,7},{7,6},{8,9},{9,8},{10,11... | collective-permute-start | bytes 196616 | tf_op jit(solution)/shard_map/ppermute | solution.py:328
  33.9 2.0 %collective-permute-start.11 = (bf16[2,32,512]{2,1,0:T(8,128)(2,1)S(1)}, bf16[2,32,512]{2,1,0:T(8,128)(2,1)S(1)}, u32[]{:S(2)}, u32[]{:S(2)}) collective-permute-start(bf16[2,32,512]{2,1,0:T(8,128)(2,1)S(1)} %collective-permute-done.7.refs_6_), channel_id=1, source_target_pairs={{0,1},{1,0},{2,3},{3,2},{4,5},{5,4},{6,7},{7,6},{8,9},{9,8},{10,11... | collective-permute-start | bytes 196616 | tf_op jit(solution)/shard_map/ppermute | solution.py:328
  34.5 1.3 %collective-permute-start.10 = (bf16[2,32,512]{2,1,0:T(8,128)(2,1)S(1)}, bf16[2,32,512]{2,1,0:T(8,128)(2,1)S(1)}, u32[]{:S(2)}, u32[]{:S(2)}) collective-permute-start(bf16[2,32,512]{2,1,0:T(8,128)(2,1)S(1)} %collective-permute-done.6.refs_5_), channel_id=1, source_target_pairs={{0,1},{1,0},{2,3},{3,2},{4,5},{5,4},{6,7},{7,6},{8,9},{9,8},{10,11... | collective-permute-start | bytes 196616 | tf_op jit(solution)/shard_map/ppermute | solution.py:328
  35.9 1.3 %collective-permute-start.9 = (bf16[2,32,512]{2,1,0:T(8,128)(2,1)S(1)}, bf16[2,32,512]{2,1,0:T(8,128)(2,1)S(1)}, u32[]{:S(2)}, u32[]{:S(2)}) collective-permute-start(bf16[2,32,512]{2,1,0:T(8,128)(2,1)S(1)} %collective-permute-done.5.refs_4_), channel_id=1, source_target_pairs={{0,1},{1,0},{2,3},{3,2},{4,5},{5,4},{6,7},{7,6},{8,9},{9,8},{10,11... | collective-permute-start | bytes 196616 | tf_op jit(solution)/shard_map/ppermute | solution.py:328

commit v3 on v2

--- a/solution.py
+++ b/solution.py
@@ -9,6 +9,7 @@
 MIB = 1 << 20
 SMALL = jnp.float8_e4m3fn
 LARGEST = 448.0
+FLIGHT = 3
 SHIFT = 16.0
 EFFECT_SCALE = 1024.0
 
@@ -103,8 +104,6 @@
     ]
     for copy in small:
         copy.start()
-    for i in range(flight):
-        fetch(i).start()
     for t in range(tails):
         fetch_noise(t).start()
 
@@ -115,6 +114,8 @@
     value_ref[...] = jnp.zeros(value_ref.shape, jnp.float32)
     for copy in small:
         copy.wait()
+    for i in range(flight):
+        fetch(i).start()
     local = causal_ref[...] - me * variants
     inside = (local >= 0) & (local < variants)
     high_ref[:, :causal_count] = jnp.where(inside, local // LANES, -1)
@@ -134,21 +135,21 @@
         )
         beta_ref[p] = join(sums, 4) * (1.0 / EFFECT_SCALE)
 
-    per_step = -(-pheno // half)
-
-    def first(i, carry):
-        fetch(i).wait()
-
-        @pl.when(i + flight < blocks)
+    steps = half
+    per_step = -(-pheno // steps)
+
+    def build_step(i, carry):
+        @pl.when(flight + i < blocks)
         def _():
-            fetch(i + flight).start()
-
-        held_ref[i] = staged_ref[i].astype(SMALL)
+            fetch(flight + i).start()
+
         for j in range(per_step):
             build(jnp.minimum(i * per_step + j, pheno - 1))
         return carry
 
-    lax.fori_loop(0, half, first, 0)
+    lax.fori_loop(0, steps, build_step, 0, unroll=True)
+    for i in range(flight + steps, blocks):
+        fetch(i).start()
 
     offset = jnp.zeros((pheno, LANES), jnp.float32)
     for h in range(high_count):
@@ -179,26 +180,31 @@
     factor = heavy / scale
     shift = heavy * offset
 
+    def convert(i):
+        fetch(i).wait()
+        held_ref[i] = staged_ref[i].astype(SMALL)
+
     def partial(i):
         sums = lax.dot_general(
             weights, held_ref[i], (((1,), (1,)), ((), ())), preferred_element_type=jnp.float32
         )
         return join(sums, 2) * factor - shift
 
-    def second(i, carry):
+    convert(0)
+
+    def multiply_send(i, carry):
+        convert(i + 1)
         send_ref[i] = partial(i).astype(send_ref.dtype)
-        late = half + i
-        fetch(late).wait()
-
-        @pl.when(late + flight < blocks)
-        def _():
-            fetch(late + flight).start()
-
-        held_ref[late] = staged_ref[late].astype(SMALL)
-        keep_ref[i] = partial(late).astype(keep_ref.dtype)
         return carry
 
-    lax.fori_loop(0, half, second, 0)
+    def multiply_keep(i, carry):
+        convert(half + i + 1)
+        keep_ref[i] = partial(half + i).astype(keep_ref.dtype)
+        return carry
+
+    lax.fori_loop(0, half, multiply_send, 0, unroll=True)
+    lax.fori_loop(0, half - 1, multiply_keep, 0, unroll=True)
+    keep_ref[half - 1] = partial(blocks - 1).astype(keep_ref.dtype)
 
 
 def scan_kernel(order, scale_back, *refs):
@@ -258,7 +264,7 @@
     width = -(-causal_count // LANES) * LANES
 
     held, send, keep, tail = pl.pallas_call(
-        lambda *refs: evolve_kernel(blocks, share, half, relative_of, *refs),
+        lambda *refs: evolve_kernel(blocks, share, FLIGHT, relative_of, *refs),
         out_shape=(
             jax.ShapeDtypeStruct((blocks, share, variants), SMALL),
             jax.ShapeDtypeStruct((half, pheno, share), jnp.bfloat16),

time: 39.4 us -> 36.5 us (0.926)
  Pallas kernels: 13.6 us -> 10.6 us
    pallas_call x1, Pallas kernels: 11.5 us -> 8.51 us  [on_device(): pl.pallas_call(lambda *refs: evolve_kernel(blocks, share, FLIGHT, relativ...]
    ppermute x1, waiting for transfers between devices: 3.31 us -> 2.59 us  [on_device(): other = lax.ppermute(mine, 'var', pairs(8 * step))]
    ppermute x3, waiting for transfers between devices: 3.66 us -> 4.25 us  [on_device(): groups[g] = lax.ppermute(own, 'var', pairs(2 * g))]
where the time goes in v3:
time: 36.5 us; the launch traced here: 36.3 us
  waiting for transfers between devices  13.5 us (37%)
  starting transfers between devices  11.4 us (31%)
  Pallas kernels  10.6 us (29%)
  between operations  0.69 us (2%)
    pallas_call x1, Pallas kernels, on_device(): pl.pallas_call(lambda *refs: evolve_kernel(blocks, share, FLIGHT, relativ...  8.51 us
    ppermute x3, starting transfers between devices, on_device(): lax.ppermute(chip[g - 1].astype(jnp.bfloat16), 'var', pairs(2 * g))  4.49 us
    ppermute x3, waiting for transfers between devices, on_device(): groups[g] = lax.ppermute(own, 'var', pairs(2 * g))  4.25 us
    ppermute x3, waiting for transfers between devices, on_device(): lax.ppermute(chip[g - 1].astype(jnp.bfloat16), 'var', pairs(2 * g))  4.23 us
    ppermute x3, starting transfers between devices, on_device(): groups[g] = lax.ppermute(own, 'var', pairs(2 * g))  3.71 us
    ppermute x1, starting transfers between devices, on_device(): other = lax.ppermute(mine, 'var', pairs(8 * step))  2.65 us
    ppermute x1, waiting for transfers between devices, on_device(): other = lax.ppermute(mine, 'var', pairs(8 * step))  2.59 us
    pallas_call x1, Pallas kernels, on_device(): pl.pallas_call(lambda *refs: scan_kernel(used, scale_back, *refs), out_sh...  2.08 us
  transfers between devices with their start and end apart: 12, of which 9 were waited for; matrix products, arithmetic and copies ran while one was open for 0% of the time, Pallas kernels for 0%

profile of v3, /device:TPU:0, one launch (start us, length us, event | category | flops | bytes accessed | tf_op | source)
XLA Modules:
  0.0 36.3 jit_solution(4516356406580681930)
XLA Ops:
  0.7 8.5 %evolve.1 = (f8e4m3fn[16,512,1024]{2,1,0:T(32,128)(4,1)S(1)}, bf16[8,32,512]{2,1,0:T(8,128)(2,1)S(1)}, f32[8,32,512]{2,1,0:T(8,128)S(1)}, f32[2,32,512]{2,1,0:T(8,128)S(1)}) custom-call(bf16[8192,1024]{1,0:T(8,128)(2,1)} %refs_0_.1, bf16[32,8192]{1,0:T(8,128)(2,1)} %refs_1_.1, f32[1,1024]{1,0:T(1,128)} %bitcast.3, f32[1,1024]{1,0:T(1,128)} %bitcast.5, ...), custom_call_target="tpu_custom_call" | custom-call | tf_op jit(solution)/shard_map/evolve/pallas_call | solution.py:266
  9.2 0.6 %collective-permute-start = (bf16[8,32,512]{2,1,0:T(8,128)(2,1)S(1)}, bf16[8,32,512]{2,1,0:T(8,128)(2,1)S(1)}, u32[]{:S(2)}, u32[]{:S(2)}) collective-permute-start(bf16[8,32,512]{2,1,0:T(8,128)(2,1)S(1)} %get-tuple-element.8), channel_id=1, source_target_pairs={{0,1},{1,0},{2,3},{3,2},{4,5},{5,4},{6,7},{7,6},{8,9},{9,8},{10,11... | collective-permute-start | bytes 786440 | tf_op jit(solution)/shard_map/ppermute | solution.py:310
  9.7 1.2 %collective-permute-done = bf16[8,32,512]{2,1,0:T(8,128)(2,1)S(1)} collective-permute-done((bf16[8,32,512]{2,1,0:T(8,128)(2,1)S(1)}, bf16[8,32,512]{2,1,0:T(8,128)(2,1)S(1)}, u32[]{:S(2)}, u32[]{:S(2)}) %collective-permute-start) | collective-permute-done | bytes 262176 | tf_op jit(solution)/shard_map/ppermute | solution.py:310
  10.9 0.1 add_convert_fusion.4
  10.9 2.9 %collective-permute-start.1 = (bf16[2,32,512]{2,1,0:T(8,128)(2,1)S(1)}, bf16[2,32,512]{2,1,0:T(8,128)(2,1)S(1)}, u32[]{:S(2)}, u32[]{:S(2)}) collective-permute-start(bf16[2,32,512]{2,1,0:T(8,128)(2,1)S(1)} %get-tuple-element.10), channel_id=1, source_target_pairs={{0,2},{1,3},{2,0},{3,1},{4,6},{5,7},{6,4},{7,5},{8,10},{9,11},{10,... | collective-permute-start | bytes 196616 | tf_op jit(solution)/shard_map/ppermute | solution.py:316
  13.9 1.5 %collective-permute-start.3 = (bf16[2,32,512]{2,1,0:T(8,128)(2,1)S(1)}, bf16[2,32,512]{2,1,0:T(8,128)(2,1)S(1)}, u32[]{:S(2)}, u32[]{:S(2)}) collective-permute-start(bf16[2,32,512]{2,1,0:T(8,128)(2,1)S(1)} %get-tuple-element.11), channel_id=1, source_target_pairs={{0,6},{1,7},{2,4},{3,5},{4,2},{5,3},{6,0},{7,1},{8,14},{9,15},{10,... | collective-permute-start | bytes 196616 | tf_op jit(solution)/shard_map/ppermute | solution.py:316
  15.4 0.0 collective-permute-start.2
  15.4 1.6 %collective-permute-done.1 = bf16[2,32,512]{2,1,0:T(8,128)(2,1)S(1)} collective-permute-done((bf16[2,32,512]{2,1,0:T(8,128)(2,1)S(1)}, bf16[2,32,512]{2,1,0:T(8,128)(2,1)S(1)}, u32[]{:S(2)}, u32[]{:S(2)}) %collective-permute-start.1) | collective-permute-done | bytes 65568 | tf_op jit(solution)/shard_map/ppermute | solution.py:316
  17.1 2.5 %collective-permute-done.3 = bf16[2,32,512]{2,1,0:T(8,128)(2,1)S(1)} collective-permute-done((bf16[2,32,512]{2,1,0:T(8,128)(2,1)S(1)}, bf16[2,32,512]{2,1,0:T(8,128)(2,1)S(1)}, u32[]{:S(2)}, u32[]{:S(2)}) %collective-permute-start.3) | collective-permute-done | bytes 65568 | tf_op jit(solution)/shard_map/ppermute | solution.py:316
  19.5 0.1 collective-permute-done.2
  19.7 2.7 %collective-permute-start.4 = (bf16[2,32,512]{2,1,0:T(8,128)(2,1)S(1)}, bf16[2,32,512]{2,1,0:T(8,128)(2,1)S(1)}, u32[]{:S(2)}, u32[]{:S(2)}) collective-permute-start(bf16[2,32,512]{2,1,0:T(8,128)(2,1)S(1)} %add_convert_fusion.1), channel_id=1, source_target_pairs={{0,8},{1,9},{2,10},{3,11},{4,12},{5,13},{6,14},{7,15},{8,0},{9,1},... | collective-permute-start | bytes 196616 | tf_op jit(solution)/shard_map/ppermute | solution.py:325
  22.4 2.6 %collective-permute-done.4 = bf16[2,32,512]{2,1,0:T(8,128)(2,1)S(1)} collective-permute-done((bf16[2,32,512]{2,1,0:T(8,128)(2,1)S(1)}, bf16[2,32,512]{2,1,0:T(8,128)(2,1)S(1)}, u32[]{:S(2)}, u32[]{:S(2)}) %collective-permute-start.4) | collective-permute-done | bytes 65568 | tf_op jit(solution)/shard_map/ppermute | solution.py:325
  25.0 2.1 %collective-permute-start.7 = (bf16[2,32,512]{2,1,0:T(8,128)(2,1)S(1)}, bf16[2,32,512]{2,1,0:T(8,128)(2,1)S(1)}, u32[]{:S(2)}, u32[]{:S(2)}) collective-permute-start(bf16[2,32,512]{2,1,0:T(8,128)(2,1)S(1)} %add_convert_fusion.refs_3_), channel_id=1, source_target_pairs={{0,6},{1,7},{2,4},{3,5},{4,2},{5,3},{6,0},{7,1},{8,14},{9,15},{10,... | collective-permute-start | bytes 196616 | tf_op jit(solution)/shard_map/ppermute | solution.py:333
  27.1 1.6 %collective-permute-start.6 = (bf16[2,32,512]{2,1,0:T(8,128)(2,1)S(1)}, bf16[2,32,512]{2,1,0:T(8,128)(2,1)S(1)}, u32[]{:S(2)}, u32[]{:S(2)}) collective-permute-start(bf16[2,32,512]{2,1,0:T(8,128)(2,1)S(1)} %add_convert_fusion.refs_3_), channel_id=1, source_target_pairs={{0,4},{1,5},{2,6},{3,7},{4,0},{5,1},{6,2},{7,3},{8,12},{9,13},{10,... | collective-permute-start | bytes 196616 | tf_op jit(solution)/shard_map/ppermute | solution.py:333
  28.7 0.0 collective-permute-start.5
  28.7 0.0 collective-permute-start.8
  28.7 1.5 %collective-permute-done.7.refs_6_ = bf16[2,32,512]{2,1,0:T(8,128)(2,1)S(1)} collective-permute-done((bf16[2,32,512]{2,1,0:T(8,128)(2,1)S(1)}, bf16[2,32,512]{2,1,0:T(8,128)(2,1)S(1)}, u32[]{:S(2)}, u32[]{:S(2)}) %collective-permute-start.7) | collective-permute-done | bytes 65568 | tf_op jit(solution)/shard_map/ppermute | solution.py:333
  30.2 0.0 collective-permute-start.11
  30.2 1.4 %collective-permute-done.6.refs_5_ = bf16[2,32,512]{2,1,0:T(8,128)(2,1)S(1)} collective-permute-done((bf16[2,32,512]{2,1,0:T(8,128)(2,1)S(1)}, bf16[2,32,512]{2,1,0:T(8,128)(2,1)S(1)}, u32[]{:S(2)}, u32[]{:S(2)}) %collective-permute-start.6) | collective-permute-done | bytes 65568 | tf_op jit(solution)/shard_map/ppermute | solution.py:333
  31.6 0.0 collective-permute-start.10
  31.6 1.3 %collective-permute-done.5.refs_4_ = bf16[2,32,512]{2,1,0:T(8,128)(2,1)S(1)} collective-permute-done((bf16[2,32,512]{2,1,0:T(8,128)(2,1)S(1)}, bf16[2,32,512]{2,1,0:T(8,128)(2,1)S(1)}, u32[]{:S(2)}, u32[]{:S(2)}) %collective-permute-start.5) | collective-permute-done | bytes 65568 | tf_op jit(solution)/shard_map/ppermute | solution.py:333
  33.0 0.0 collective-permute-start.9
  33.0 1.2 %collective-permute-done.9.refs_8_ = bf16[2,32,512]{2,1,0:T(8,128)(2,1)S(1)} collective-permute-done((bf16[2,32,512]{2,1,0:T(8,128)(2,1)S(1)}, bf16[2,32,512]{2,1,0:T(8,128)(2,1)S(1)}, u32[]{:S(2)}, u32[]{:S(2)}) %collective-permute-start.9) | collective-permute-done | bytes 65568 | tf_op jit(solution)/shard_map/ppermute | solution.py:334
  34.2 2.1 %scan.1 = (bf16[32,512]{1,0:T(8,128)(2,1)}, f32[32,1024]{1,0:T(8,128)}) custom-call(f8e4m3fn[16,512,1024]{2,1,0:T(32,128)(4,1)S(1)} %get-tuple-element.6.refs_0_, f32[1,1024]{1,0:T(1,128)S(1)} %bitcast.4, f32[1,1024]{1,0:T(1,128)S(1)} %bitcast.6, bf16[2,32,512]{2,1,0:T(8,128)(2,1)S(1)} %add_convert_fusion.refs_3_, ...), custom_call_target="tpu_custom_call" | custom-call | tf_op jit(solution)/shard_map/scan/pallas_call | solution.py:341
  (10 shorter events, 0.1 us)
Async XLA Ops:
  0.6 33.6 %copy-start.1 = (f32[1024]{0:T(1024)S(1)}, f32[1024]{0:T(1024)}, u32[]{:S(2)}) copy-start(f32[1024]{0:T(1024)} %param.9) | copy-start | bytes 12292
  0.6 33.6 %copy-start = (f32[1024]{0:T(1024)S(1)}, f32[1024]{0:T(1024)}, u32[]{:S(2)}) copy-start(f32[1024]{0:T(1024)} %param.8) | copy-start | bytes 12292
  9.2 1.7 %collective-permute-start = (bf16[8,32,512]{2,1,0:T(8,128)(2,1)S(1)}, bf16[8,32,512]{2,1,0:T(8,128)(2,1)S(1)}, u32[]{:S(2)}, u32[]{:S(2)}) collective-permute-start(bf16[8,32,512]{2,1,0:T(8,128)(2,1)S(1)} %get-tuple-element.8), channel_id=1, source_target_pairs={{0,1},{1,0},{2,3},{3,2},{4,5},{5,4},{6,7},{7,6},{8,9},{9,8},{10,11... | collective-permute-start | bytes 786440 | tf_op jit(solution)/shard_map/ppermute | solution.py:310
  10.9 6.1 %collective-permute-start.1 = (bf16[2,32,512]{2,1,0:T(8,128)(2,1)S(1)}, bf16[2,32,512]{2,1,0:T(8,128)(2,1)S(1)}, u32[]{:S(2)}, u32[]{:S(2)}) collective-permute-start(bf16[2,32,512]{2,1,0:T(8,128)(2,1)S(1)} %get-tuple-element.10), channel_id=1, source_target_pairs={{0,2},{1,3},{2,0},{3,1},{4,6},{5,7},{6,4},{7,5},{8,10},{9,11},{10,... | collective-permute-start | bytes 196616 | tf_op jit(solution)/shard_map/ppermute | solution.py:316
  13.9 5.7 %collective-permute-start.3 = (bf16[2,32,512]{2,1,0:T(8,128)(2,1)S(1)}, bf16[2,32,512]{2,1,0:T(8,128)(2,1)S(1)}, u32[]{:S(2)}, u32[]{:S(2)}) collective-permute-start(bf16[2,32,512]{2,1,0:T(8,128)(2,1)S(1)} %get-tuple-element.11), channel_id=1, source_target_pairs={{0,6},{1,7},{2,4},{3,5},{4,2},{5,3},{6,0},{7,1},{8,14},{9,15},{10,... | collective-permute-start | bytes 196616 | tf_op jit(solution)/shard_map/ppermute | solution.py:316
  15.4 4.3 %collective-permute-start.2 = (bf16[2,32,512]{2,1,0:T(8,128)(2,1)S(1)}, bf16[2,32,512]{2,1,0:T(8,128)(2,1)S(1)}, u32[]{:S(2)}, u32[]{:S(2)}) collective-permute-start(bf16[2,32,512]{2,1,0:T(8,128)(2,1)S(1)} %get-tuple-element.12), channel_id=1, source_target_pairs={{0,4},{1,5},{2,6},{3,7},{4,0},{5,1},{6,2},{7,3},{8,12},{9,13},{10,... | collective-permute-start | bytes 196616 | tf_op jit(solution)/shard_map/ppermute | solution.py:316
  19.7 5.2 %collective-permute-start.4 = (bf16[2,32,512]{2,1,0:T(8,128)(2,1)S(1)}, bf16[2,32,512]{2,1,0:T(8,128)(2,1)S(1)}, u32[]{:S(2)}, u32[]{:S(2)}) collective-permute-start(bf16[2,32,512]{2,1,0:T(8,128)(2,1)S(1)} %add_convert_fusion.1), channel_id=1, source_target_pairs={{0,8},{1,9},{2,10},{3,11},{4,12},{5,13},{6,14},{7,15},{8,0},{9,1},... | collective-permute-start | bytes 196616 | tf_op jit(solution)/shard_map/ppermute | solution.py:325
  25.0 5.2 %collective-permute-start.7 = (bf16[2,32,512]{2,1,0:T(8,128)(2,1)S(1)}, bf16[2,32,512]{2,1,0:T(8,128)(2,1)S(1)}, u32[]{:S(2)}, u32[]{:S(2)}) collective-permute-start(bf16[2,32,512]{2,1,0:T(8,128)(2,1)S(1)} %add_convert_fusion.refs_3_), channel_id=1, source_target_pairs={{0,6},{1,7},{2,4},{3,5},{4,2},{5,3},{6,0},{7,1},{8,14},{9,15},{10,... | collective-permute-start | bytes 196616 | tf_op jit(solution)/shard_map/ppermute | solution.py:333
  27.1 4.6 %collective-permute-start.6 = (bf16[2,32,512]{2,1,0:T(8,128)(2,1)S(1)}, bf16[2,32,512]{2,1,0:T(8,128)(2,1)S(1)}, u32[]{:S(2)}, u32[]{:S(2)}) collective-permute-start(bf16[2,32,512]{2,1,0:T(8,128)(2,1)S(1)} %add_convert_fusion.refs_3_), channel_id=1, source_target_pairs={{0,4},{1,5},{2,6},{3,7},{4,0},{5,1},{6,2},{7,3},{8,12},{9,13},{10,... | collective-permute-start | bytes 196616 | tf_op jit(solution)/shard_map/ppermute | solution.py:333
  28.7 4.3 %collective-permute-start.5 = (bf16[2,32,512]{2,1,0:T(8,128)(2,1)S(1)}, bf16[2,32,512]{2,1,0:T(8,128)(2,1)S(1)}, u32[]{:S(2)}, u32[]{:S(2)}) collective-permute-start(bf16[2,32,512]{2,1,0:T(8,128)(2,1)S(1)} %add_convert_fusion.refs_3_), channel_id=1, source_target_pairs={{0,2},{1,3},{2,0},{3,1},{4,6},{5,7},{6,4},{7,5},{8,10},{9,11},{10,... | collective-permute-start | bytes 196616 | tf_op jit(solution)/shard_map/ppermute | solution.py:333
  28.7 4.3 %collective-permute-start.8 = (bf16[2,32,512]{2,1,0:T(8,128)(2,1)S(1)}, bf16[2,32,512]{2,1,0:T(8,128)(2,1)S(1)}, u32[]{:S(2)}, u32[]{:S(2)}) collective-permute-start(bf16[2,32,512]{2,1,0:T(8,128)(2,1)S(1)} %add_convert_fusion.refs_3_), channel_id=1, source_target_pairs={{0,1},{1,0},{2,3},{3,2},{4,5},{5,4},{6,7},{7,6},{8,9},{9,8},{10,11... | collective-permute-start | bytes 196616 | tf_op jit(solution)/shard_map/ppermute | solution.py:334
  30.2 2.8 %collective-permute-start.11 = (bf16[2,32,512]{2,1,0:T(8,128)(2,1)S(1)}, bf16[2,32,512]{2,1,0:T(8,128)(2,1)S(1)}, u32[]{:S(2)}, u32[]{:S(2)}) collective-permute-start(bf16[2,32,512]{2,1,0:T(8,128)(2,1)S(1)} %collective-permute-done.7.refs_6_), channel_id=1, source_target_pairs={{0,1},{1,0},{2,3},{3,2},{4,5},{5,4},{6,7},{7,6},{8,9},{9,8},{10,11... | collective-permute-start | bytes 196616 | tf_op jit(solution)/shard_map/ppermute | solution.py:334
  31.6 1.3 %collective-permute-start.10 = (bf16[2,32,512]{2,1,0:T(8,128)(2,1)S(1)}, bf16[2,32,512]{2,1,0:T(8,128)(2,1)S(1)}, u32[]{:S(2)}, u32[]{:S(2)}) collective-permute-start(bf16[2,32,512]{2,1,0:T(8,128)(2,1)S(1)} %collective-permute-done.6.refs_5_), channel_id=1, source_target_pairs={{0,1},{1,0},{2,3},{3,2},{4,5},{5,4},{6,7},{7,6},{8,9},{9,8},{10,11... | collective-permute-start | bytes 196616 | tf_op jit(solution)/shard_map/ppermute | solution.py:334
  33.0 1.3 %collective-permute-start.9 = (bf16[2,32,512]{2,1,0:T(8,128)(2,1)S(1)}, bf16[2,32,512]{2,1,0:T(8,128)(2,1)S(1)}, u32[]{:S(2)}, u32[]{:S(2)}) collective-permute-start(bf16[2,32,512]{2,1,0:T(8,128)(2,1)S(1)} %collective-permute-done.5.refs_4_), channel_id=1, source_target_pairs={{0,1},{1,0},{2,3},{3,2},{4,5},{5,4},{6,7},{7,6},{8,9},{9,8},{10,11... | collective-permute-start | bytes 196616 | tf_op jit(solution)/shard_map/ppermute | solution.py:334

commit v4 on v3

--- a/solution.py
+++ b/solution.py
@@ -112,7 +112,7 @@
     high_ref[...] = jnp.full(high_ref.shape, -1, jnp.int32)
     low_ref[...] = jnp.zeros(low_ref.shape, jnp.int32)
     value_ref[...] = jnp.zeros(value_ref.shape, jnp.float32)
-    for copy in small:
+    for copy in small[:2]:
         copy.wait()
     for i in range(flight):
         fetch(i).start()
@@ -151,6 +151,8 @@
     for i in range(flight + steps, blocks):
         fetch(i).start()
 
+    for copy in small[2:]:
+        copy.wait()
     offset = jnp.zeros((pheno, LANES), jnp.float32)
     for h in range(high_count):
         lanes = slice(h * LANES, (h + 1) * LANES)
@@ -171,10 +173,6 @@
     )
     heavy = jnp.sqrt(share_genetic)
     light = jnp.sqrt(1.0 - share_genetic)
-    for t in range(tails):
-        fetch_noise(t).wait()
-        tail_ref[t] = light * noise_ref[t].astype(jnp.float32)
-
     scale = row_scale(weight_ref[...])
     weights = split(weight_ref[...] * scale, 2)
     factor = heavy / scale
@@ -205,20 +203,18 @@
     lax.fori_loop(0, half, multiply_send, 0, unroll=True)
     lax.fori_loop(0, half - 1, multiply_keep, 0, unroll=True)
     keep_ref[half - 1] = partial(blocks - 1).astype(keep_ref.dtype)
-
-
-def scan_kernel(order, scale_back, *refs):
-    held_ref, means_ref, scales_ref = refs[:3]
-    pieces = refs[3:-2]
-    phen_ref, out_ref = refs[-2:]
+    for t in range(tails):
+        fetch_noise(t).wait()
+        tail_ref[t] = light * noise_ref[t].astype(jnp.float32)
+
+
+def scan_pieces(order, held_ref, pieces):
     values = [piece[j].astype(jnp.float32) for piece in pieces for j in range(piece.shape[0])]
-    phen_ref[...] = pieces[0][0]
-    largest = values[0]
+    largest = jnp.abs(values[0])
     column = values[0]
     for value in values[1:]:
-        largest = jnp.maximum(jnp.abs(largest), jnp.abs(value))
+        largest = jnp.maximum(largest, jnp.abs(value))
         column = column + value
-    column = jnp.sum(column, axis=1, keepdims=True)
     scale = row_scale(largest)
     total = None
     for i, value in enumerate(values):
@@ -226,7 +222,25 @@
             split(value * scale, 2), held_ref[order[i]], preferred_element_type=jnp.float32
         )
         total = part if total is None else total + part
-    total = join(total, 2) / scale
+    return join(total, 2) / scale, jnp.sum(column, axis=1, keepdims=True)
+
+
+def early_kernel(order, held_ref, *refs):
+    pieces = refs[:-2]
+    total_ref, column_ref = refs[-2:]
+    total, column = scan_pieces(order, held_ref, pieces)
+    total_ref[...] = total
+    column_ref[...] = jnp.broadcast_to(column, column_ref.shape)
+
+
+def late_kernel(order, scale_back, held_ref, means_ref, scales_ref, own_ref, *refs):
+    early_ref, early_column_ref = refs[:2]
+    pieces = refs[2:-2]
+    phen_ref, out_ref = refs[-2:]
+    phen_ref[...] = own_ref[0]
+    total, column = scan_pieces(order, held_ref, pieces)
+    total = total + early_ref[...]
+    column = column + early_column_ref[:, :1]
     if scale_back is None:
         out_ref[...] = total
     else:
@@ -332,26 +346,45 @@
     for g in (1, 2, 3):
         groups[g] = lax.ppermute(own, "var", pairs(2 * g))
     others = {g: lax.ppermute(groups[g], "var", pairs(1)) for g in range(4)}
-    pieces = [groups[g] for g in range(4)] + [others[g] for g in range(4)]
-    used = [position(c, g, t) for c in (0, 1) for g in range(4) for t in range(tails)]
+    first = [(0, g, groups[g]) for g in range(4)] + [(1, g, others[g]) for g in (0, 3, 2)]
+    last = [(1, 1, others[1])]
+
+    def places(chosen):
+        return [position(core, g, t) for core, g, _ in chosen for t in range(tails)]
+
+    def arrays(chosen):
+        return [array for _, _, array in chosen]
 
     alone = samp == 1
     total_samples = jnp.float32(samples * samp)
     scale_back = float(samples * samp) ** 0.5 if alone else None
+    params = pltpu.CompilerParams(vmem_limit_bytes=8 * MIB)
+    early, early_column = pl.pallas_call(
+        lambda *refs: early_kernel(places(first), *refs),
+        out_shape=(
+            jax.ShapeDtypeStruct((pheno, variants), jnp.float32),
+            jax.ShapeDtypeStruct((pheno, LANES), jnp.float32),
+        ),
+        in_specs=[vmem] * (1 + len(first)),
+        out_specs=[vmem] * 2,
+        compiler_params=params,
+        name="scan_early",
+    )(held, *arrays(first))
     phen_out, scores = pl.pallas_call(
-        lambda *refs: scan_kernel(used, scale_back, *refs),
+        lambda *refs: late_kernel(places(last), scale_back, *refs),
         out_shape=(
             jax.ShapeDtypeStruct((pheno, share), jnp.bfloat16),
             jax.ShapeDtypeStruct((pheno, variants), jnp.float32),
         ),
-        in_specs=[vmem] * (3 + len(pieces)),
+        in_specs=[vmem] * (6 + len(last)),
         out_specs=[vmem] * 2,
-        compiler_params=pltpu.CompilerParams(vmem_limit_bytes=8 * MIB),
-        name="scan",
-    )(held, means_row, scales_row, *pieces)
+        compiler_params=params,
+        name="scan_late",
+    )(held, means_row, scales_row, own, early, early_column, *arrays(last))
     if alone:
         return phen_out, scores
 
+    pieces = arrays(first + last)
     column = sum(jnp.sum(piece.astype(jnp.float32), axis=(0, 2)) for piece in pieces)
     score_width = variants // samp
     score_start = lax.axis_index("samp") * score_width

time: 36.5 us -> 35.4 us (0.970)
  waiting for transfers between devices: 13.5 us -> 12.2 us
    ppermute x4, waiting for transfers between devices: 1.24 us -> 0.01 us  [on_device(): others = {g: lax.ppermute(groups[g], 'var', pairs(1)) for g in range(4)}]
    pallas_call x1 -> x2, Pallas kernels: 2.08 us -> 2.31 us  [the longest x1 1.29 us: on_device(): pl.pallas_call(lambda *refs: early_kernel(places(first), *refs), out_shap...]
  transfers between devices with their start and end apart: 12 -> 12, of which waited for: 9 -> 8; matrix products, arithmetic and copies ran while one was open for 0% -> 0% of each run, Pallas kernels for 0% -> 4%
where the time goes in v4:
time: 35.4 us; the launch traced here: 35.3 us
  waiting for transfers between devices  12.2 us (34%)
  starting transfers between devices  11.4 us (32%)
  Pallas kernels  10.8 us (31%)
  between operations  0.72 us (2%)
    pallas_call x1, Pallas kernels, on_device(): pl.pallas_call(lambda *refs: evolve_kernel(blocks, share, FLIGHT, relativ...  8.44 us
    ppermute x3, starting transfers between devices, on_device(): lax.ppermute(chip[g - 1].astype(jnp.bfloat16), 'var', pairs(2 * g))  4.49 us
    ppermute x3, waiting for transfers between devices, on_device(): groups[g] = lax.ppermute(own, 'var', pairs(2 * g))  4.25 us
    ppermute x3, waiting for transfers between devices, on_device(): lax.ppermute(chip[g - 1].astype(jnp.bfloat16), 'var', pairs(2 * g))  4.23 us
    ppermute x3, starting transfers between devices, on_device(): groups[g] = lax.ppermute(own, 'var', pairs(2 * g))  3.71 us
    ppermute x1, starting transfers between devices, on_device(): other = lax.ppermute(mine, 'var', pairs(8 * step))  2.65 us
    ppermute x1, waiting for transfers between devices, on_device(): other = lax.ppermute(mine, 'var', pairs(8 * step))  2.59 us
    pallas_call x1, Pallas kernels, on_device(): pl.pallas_call(lambda *refs: early_kernel(places(first), *refs), out_shap...  1.29 us
  transfers between devices with their start and end apart: 12, of which 8 were waited for; matrix products, arithmetic and copies ran while one was open for 0% of the time, Pallas kernels for 4%

profile of v4, /device:TPU:0, one launch (start us, length us, event | category | flops | bytes accessed | tf_op | source)
XLA Modules:
  0.0 35.3 jit_solution(11352214158381043736)
XLA Ops:
  0.7 8.4 %evolve.1 = (f8e4m3fn[16,512,1024]{2,1,0:T(32,128)(4,1)S(1)}, bf16[8,32,512]{2,1,0:T(8,128)(2,1)S(1)}, f32[8,32,512]{2,1,0:T(8,128)S(1)}, f32[2,32,512]{2,1,0:T(8,128)S(1)}) custom-call(bf16[8192,1024]{1,0:T(8,128)(2,1)} %refs_0_.1, bf16[32,8192]{1,0:T(8,128)(2,1)} %refs_1_.1, f32[1,1024]{1,0:T(1,128)} %bitcast.3, f32[1,1024]{1,0:T(1,128)} %bitcast.5, ...), custom_call_target="tpu_custom_call" | custom-call | tf_op jit(solution)/shard_map/evolve/pallas_call | solution.py:280
  9.1 0.6 %collective-permute-start = (bf16[8,32,512]{2,1,0:T(8,128)(2,1)S(1)}, bf16[8,32,512]{2,1,0:T(8,128)(2,1)S(1)}, u32[]{:S(2)}, u32[]{:S(2)}) collective-permute-start(bf16[8,32,512]{2,1,0:T(8,128)(2,1)S(1)} %get-tuple-element.10), channel_id=1, source_target_pairs={{0,1},{1,0},{2,3},{3,2},{4,5},{5,4},{6,7},{7,6},{8,9},{9,8},{10,11... | collective-permute-start | bytes 786440 | tf_op jit(solution)/shard_map/ppermute | solution.py:324
  9.7 1.2 %collective-permute-done = bf16[8,32,512]{2,1,0:T(8,128)(2,1)S(1)} collective-permute-done((bf16[8,32,512]{2,1,0:T(8,128)(2,1)S(1)}, bf16[8,32,512]{2,1,0:T(8,128)(2,1)S(1)}, u32[]{:S(2)}, u32[]{:S(2)}) %collective-permute-start) | collective-permute-done | bytes 262176 | tf_op jit(solution)/shard_map/ppermute | solution.py:324
  10.8 0.1 add_convert_fusion.4
  10.9 2.9 %collective-permute-start.1 = (bf16[2,32,512]{2,1,0:T(8,128)(2,1)S(1)}, bf16[2,32,512]{2,1,0:T(8,128)(2,1)S(1)}, u32[]{:S(2)}, u32[]{:S(2)}) collective-permute-start(bf16[2,32,512]{2,1,0:T(8,128)(2,1)S(1)} %get-tuple-element.14), channel_id=1, source_target_pairs={{0,2},{1,3},{2,0},{3,1},{4,6},{5,7},{6,4},{7,5},{8,10},{9,11},{10,... | collective-permute-start | bytes 196616 | tf_op jit(solution)/shard_map/ppermute | solution.py:330
  13.8 1.5 %collective-permute-start.3 = (bf16[2,32,512]{2,1,0:T(8,128)(2,1)S(1)}, bf16[2,32,512]{2,1,0:T(8,128)(2,1)S(1)}, u32[]{:S(2)}, u32[]{:S(2)}) collective-permute-start(bf16[2,32,512]{2,1,0:T(8,128)(2,1)S(1)} %get-tuple-element.15), channel_id=1, source_target_pairs={{0,6},{1,7},{2,4},{3,5},{4,2},{5,3},{6,0},{7,1},{8,14},{9,15},{10,... | collective-permute-start | bytes 196616 | tf_op jit(solution)/shard_map/ppermute | solution.py:330
  15.3 0.0 collective-permute-start.2
  15.4 1.6 %collective-permute-done.1 = bf16[2,32,512]{2,1,0:T(8,128)(2,1)S(1)} collective-permute-done((bf16[2,32,512]{2,1,0:T(8,128)(2,1)S(1)}, bf16[2,32,512]{2,1,0:T(8,128)(2,1)S(1)}, u32[]{:S(2)}, u32[]{:S(2)}) %collective-permute-start.1) | collective-permute-done | bytes 65568 | tf_op jit(solution)/shard_map/ppermute | solution.py:330
  17.0 2.5 %collective-permute-done.3 = bf16[2,32,512]{2,1,0:T(8,128)(2,1)S(1)} collective-permute-done((bf16[2,32,512]{2,1,0:T(8,128)(2,1)S(1)}, bf16[2,32,512]{2,1,0:T(8,128)(2,1)S(1)}, u32[]{:S(2)}, u32[]{:S(2)}) %collective-permute-start.3) | collective-permute-done | bytes 65568 | tf_op jit(solution)/shard_map/ppermute | solution.py:330
  19.5 0.1 collective-permute-done.2
  19.7 2.7 %collective-permute-start.4 = (bf16[2,32,512]{2,1,0:T(8,128)(2,1)S(1)}, bf16[2,32,512]{2,1,0:T(8,128)(2,1)S(1)}, u32[]{:S(2)}, u32[]{:S(2)}) collective-permute-start(bf16[2,32,512]{2,1,0:T(8,128)(2,1)S(1)} %add_convert_fusion.1), channel_id=1, source_target_pairs={{0,8},{1,9},{2,10},{3,11},{4,12},{5,13},{6,14},{7,15},{8,0},{9,1},... | collective-permute-start | bytes 196616 | tf_op jit(solution)/shard_map/ppermute | solution.py:339
  22.3 2.6 %collective-permute-done.4 = bf16[2,32,512]{2,1,0:T(8,128)(2,1)S(1)} collective-permute-done((bf16[2,32,512]{2,1,0:T(8,128)(2,1)S(1)}, bf16[2,32,512]{2,1,0:T(8,128)(2,1)S(1)}, u32[]{:S(2)}, u32[]{:S(2)}) %collective-permute-start.4) | collective-permute-done | bytes 65568 | tf_op jit(solution)/shard_map/ppermute | solution.py:339
  24.9 2.1 %collective-permute-start.7 = (bf16[2,32,512]{2,1,0:T(8,128)(2,1)S(1)}, bf16[2,32,512]{2,1,0:T(8,128)(2,1)S(1)}, u32[]{:S(2)}, u32[]{:S(2)}) collective-permute-start(bf16[2,32,512]{2,1,0:T(8,128)(2,1)S(1)} %add_convert_fusion.refs_1_.refs_3_), channel_id=1, source_target_pairs={{0,6},{1,7},{2,4},{3,5},{4,2},{5,3},{6,0},{7,1},{8,14},{9,15},{10,... | collective-permute-start | bytes 196616 | tf_op jit(solution)/shard_map/ppermute | solution.py:347
  27.0 1.6 %collective-permute-start.6 = (bf16[2,32,512]{2,1,0:T(8,128)(2,1)S(1)}, bf16[2,32,512]{2,1,0:T(8,128)(2,1)S(1)}, u32[]{:S(2)}, u32[]{:S(2)}) collective-permute-start(bf16[2,32,512]{2,1,0:T(8,128)(2,1)S(1)} %add_convert_fusion.refs_1_.refs_3_), channel_id=1, source_target_pairs={{0,4},{1,5},{2,6},{3,7},{4,0},{5,1},{6,2},{7,3},{8,12},{9,13},{10,... | collective-permute-start | bytes 196616 | tf_op jit(solution)/shard_map/ppermute | solution.py:347
  28.6 0.0 collective-permute-start.5
  28.6 1.5 %collective-permute-done.7.refs_4_ = bf16[2,32,512]{2,1,0:T(8,128)(2,1)S(1)} collective-permute-done((bf16[2,32,512]{2,1,0:T(8,128)(2,1)S(1)}, bf16[2,32,512]{2,1,0:T(8,128)(2,1)S(1)}, u32[]{:S(2)}, u32[]{:S(2)}) %collective-permute-start.7) | collective-permute-done | bytes 65568 | tf_op jit(solution)/shard_map/ppermute | solution.py:347
  30.2 0.0 collective-permute-start.9
  30.2 1.4 %collective-permute-done.6.refs_3_ = bf16[2,32,512]{2,1,0:T(8,128)(2,1)S(1)} collective-permute-done((bf16[2,32,512]{2,1,0:T(8,128)(2,1)S(1)}, bf16[2,32,512]{2,1,0:T(8,128)(2,1)S(1)}, u32[]{:S(2)}, u32[]{:S(2)}) %collective-permute-start.6) | collective-permute-done | bytes 65568 | tf_op jit(solution)/shard_map/ppermute | solution.py:347
  31.6 1.3 %collective-permute-done.5.refs_2_ = bf16[2,32,512]{2,1,0:T(8,128)(2,1)S(1)} collective-permute-done((bf16[2,32,512]{2,1,0:T(8,128)(2,1)S(1)}, bf16[2,32,512]{2,1,0:T(8,128)(2,1)S(1)}, u32[]{:S(2)}, u32[]{:S(2)}) %collective-permute-start.5) | collective-permute-done | bytes 65568 | tf_op jit(solution)/shard_map/ppermute | solution.py:347
  32.9 0.0 collective-permute-done.8.refs_5_
  32.9 0.0 collective-permute-done.9.refs_6_
  32.9 0.0 collective-permute-done.10.refs_7_
  32.9 1.3 %scan_early.1 = (f32[32,1024]{1,0:T(8,128)S(1)}, f32[32,128]{1,0:T(8,128)S(1)}) custom-call(f8e4m3fn[16,512,1024]{2,1,0:T(32,128)(4,1)S(1)} %get-tuple-element.8.refs_0_, bf16[2,32,512]{2,1,0:T(8,128)(2,1)S(1)} %add_convert_fusion.refs_1_.refs_3_, bf16[2,32,512]{2,1,0:T(8,128)(2,1)S(1)} %collective-permute-done.5.refs_2_, ...), custom_call_target="tpu_custom_call" | custom-call | tf_op jit(solution)/shard_map/scan_early/pallas_call | solution.py:362
  34.3 1.0 %scan_late.1 = (bf16[32,512]{1,0:T(8,128)(2,1)}, f32[32,1024]{1,0:T(8,128)}) custom-call(f8e4m3fn[16,512,1024]{2,1,0:T(32,128)(4,1)S(1)} %get-tuple-element.8.refs_0_, f32[1,1024]{1,0:T(1,128)S(1)} %bitcast.4, f32[1,1024]{1,0:T(1,128)S(1)} %bitcast.6, bf16[2,32,512]{2,1,0:T(8,128)(2,1)S(1)} %add_convert_fusion.refs_1_.refs_3_, ...), custom_call_target="tpu_custom_call" | custom-call | tf_op jit(solution)/shard_map/scan_late/pallas_call | solution.py:373
  (11 shorter events, 0.1 us)
Async XLA Ops:
  0.6 33.6 %copy-start.1 = (f32[1024]{0:T(1024)S(1)}, f32[1024]{0:T(1024)}, u32[]{:S(2)}) copy-start(f32[1024]{0:T(1024)} %param.9) | copy-start | bytes 12292
  0.6 33.6 %copy-start = (f32[1024]{0:T(1024)S(1)}, f32[1024]{0:T(1024)}, u32[]{:S(2)}) copy-start(f32[1024]{0:T(1024)} %param.8) | copy-start | bytes 12292
  9.1 1.7 %collective-permute-start = (bf16[8,32,512]{2,1,0:T(8,128)(2,1)S(1)}, bf16[8,32,512]{2,1,0:T(8,128)(2,1)S(1)}, u32[]{:S(2)}, u32[]{:S(2)}) collective-permute-start(bf16[8,32,512]{2,1,0:T(8,128)(2,1)S(1)} %get-tuple-element.10), channel_id=1, source_target_pairs={{0,1},{1,0},{2,3},{3,2},{4,5},{5,4},{6,7},{7,6},{8,9},{9,8},{10,11... | collective-permute-start | bytes 786440 | tf_op jit(solution)/shard_map/ppermute | solution.py:324
  10.9 6.1 %collective-permute-start.1 = (bf16[2,32,512]{2,1,0:T(8,128)(2,1)S(1)}, bf16[2,32,512]{2,1,0:T(8,128)(2,1)S(1)}, u32[]{:S(2)}, u32[]{:S(2)}) collective-permute-start(bf16[2,32,512]{2,1,0:T(8,128)(2,1)S(1)} %get-tuple-element.14), channel_id=1, source_target_pairs={{0,2},{1,3},{2,0},{3,1},{4,6},{5,7},{6,4},{7,5},{8,10},{9,11},{10,... | collective-permute-start | bytes 196616 | tf_op jit(solution)/shard_map/ppermute | solution.py:330
  13.8 5.7 %collective-permute-start.3 = (bf16[2,32,512]{2,1,0:T(8,128)(2,1)S(1)}, bf16[2,32,512]{2,1,0:T(8,128)(2,1)S(1)}, u32[]{:S(2)}, u32[]{:S(2)}) collective-permute-start(bf16[2,32,512]{2,1,0:T(8,128)(2,1)S(1)} %get-tuple-element.15), channel_id=1, source_target_pairs={{0,6},{1,7},{2,4},{3,5},{4,2},{5,3},{6,0},{7,1},{8,14},{9,15},{10,... | collective-permute-start | bytes 196616 | tf_op jit(solution)/shard_map/ppermute | solution.py:330
  15.3 4.3 %collective-permute-start.2 = (bf16[2,32,512]{2,1,0:T(8,128)(2,1)S(1)}, bf16[2,32,512]{2,1,0:T(8,128)(2,1)S(1)}, u32[]{:S(2)}, u32[]{:S(2)}) collective-permute-start(bf16[2,32,512]{2,1,0:T(8,128)(2,1)S(1)} %get-tuple-element.16), channel_id=1, source_target_pairs={{0,4},{1,5},{2,6},{3,7},{4,0},{5,1},{6,2},{7,3},{8,12},{9,13},{10,... | collective-permute-start | bytes 196616 | tf_op jit(solution)/shard_map/ppermute | solution.py:330
  19.7 5.2 %collective-permute-start.4 = (bf16[2,32,512]{2,1,0:T(8,128)(2,1)S(1)}, bf16[2,32,512]{2,1,0:T(8,128)(2,1)S(1)}, u32[]{:S(2)}, u32[]{:S(2)}) collective-permute-start(bf16[2,32,512]{2,1,0:T(8,128)(2,1)S(1)} %add_convert_fusion.1), channel_id=1, source_target_pairs={{0,8},{1,9},{2,10},{3,11},{4,12},{5,13},{6,14},{7,15},{8,0},{9,1},... | collective-permute-start | bytes 196616 | tf_op jit(solution)/shard_map/ppermute | solution.py:339
  24.9 5.2 %collective-permute-start.7 = (bf16[2,32,512]{2,1,0:T(8,128)(2,1)S(1)}, bf16[2,32,512]{2,1,0:T(8,128)(2,1)S(1)}, u32[]{:S(2)}, u32[]{:S(2)}) collective-permute-start(bf16[2,32,512]{2,1,0:T(8,128)(2,1)S(1)} %add_convert_fusion.refs_1_.refs_3_), channel_id=1, source_target_pairs={{0,6},{1,7},{2,4},{3,5},{4,2},{5,3},{6,0},{7,1},{8,14},{9,15},{10,... | collective-permute-start | bytes 196616 | tf_op jit(solution)/shard_map/ppermute | solution.py:347
  27.0 4.6 %collective-permute-start.6 = (bf16[2,32,512]{2,1,0:T(8,128)(2,1)S(1)}, bf16[2,32,512]{2,1,0:T(8,128)(2,1)S(1)}, u32[]{:S(2)}, u32[]{:S(2)}) collective-permute-start(bf16[2,32,512]{2,1,0:T(8,128)(2,1)S(1)} %add_convert_fusion.refs_1_.refs_3_), channel_id=1, source_target_pairs={{0,4},{1,5},{2,6},{3,7},{4,0},{5,1},{6,2},{7,3},{8,12},{9,13},{10,... | collective-permute-start | bytes 196616 | tf_op jit(solution)/shard_map/ppermute | solution.py:347
  28.6 4.3 %collective-permute-start.5 = (bf16[2,32,512]{2,1,0:T(8,128)(2,1)S(1)}, bf16[2,32,512]{2,1,0:T(8,128)(2,1)S(1)}, u32[]{:S(2)}, u32[]{:S(2)}) collective-permute-start(bf16[2,32,512]{2,1,0:T(8,128)(2,1)S(1)} %add_convert_fusion.refs_1_.refs_3_), channel_id=1, source_target_pairs={{0,2},{1,3},{2,0},{3,1},{4,6},{5,7},{6,4},{7,5},{8,10},{9,11},{10,... | collective-permute-start | bytes 196616 | tf_op jit(solution)/shard_map/ppermute | solution.py:347
  28.6 4.3 %collective-permute-start.8 = (bf16[2,32,512]{2,1,0:T(8,128)(2,1)S(1)}, bf16[2,32,512]{2,1,0:T(8,128)(2,1)S(1)}, u32[]{:S(2)}, u32[]{:S(2)}) collective-permute-start(bf16[2,32,512]{2,1,0:T(8,128)(2,1)S(1)} %add_convert_fusion.refs_1_.refs_3_), channel_id=1, source_target_pairs={{0,1},{1,0},{2,3},{3,2},{4,5},{5,4},{6,7},{7,6},{8,9},{9,8},{10,11... | collective-permute-start | bytes 196616 | tf_op jit(solution)/shard_map/ppermute | solution.py:348
  30.2 2.8 %collective-permute-start.9 = (bf16[2,32,512]{2,1,0:T(8,128)(2,1)S(1)}, bf16[2,32,512]{2,1,0:T(8,128)(2,1)S(1)}, u32[]{:S(2)}, u32[]{:S(2)}) collective-permute-start(bf16[2,32,512]{2,1,0:T(8,128)(2,1)S(1)} %collective-permute-done.7.refs_4_), channel_id=1, source_target_pairs={{0,1},{1,0},{2,3},{3,2},{4,5},{5,4},{6,7},{7,6},{8,9},{9,8},{10,11... | collective-permute-start | bytes 196616 | tf_op jit(solution)/shard_map/ppermute | solution.py:348
  31.6 1.3 %collective-permute-start.10 = (bf16[2,32,512]{2,1,0:T(8,128)(2,1)S(1)}, bf16[2,32,512]{2,1,0:T(8,128)(2,1)S(1)}, u32[]{:S(2)}, u32[]{:S(2)}) collective-permute-start(bf16[2,32,512]{2,1,0:T(8,128)(2,1)S(1)} %collective-permute-done.6.refs_3_), channel_id=1, source_target_pairs={{0,1},{1,0},{2,3},{3,2},{4,5},{5,4},{6,7},{7,6},{8,9},{9,8},{10,11... | collective-permute-start | bytes 196616 | tf_op jit(solution)/shard_map/ppermute | solution.py:348
  32.9 1.3 %collective-permute-start.11 = (bf16[2,32,512]{2,1,0:T(8,128)(2,1)S(1)}, bf16[2,32,512]{2,1,0:T(8,128)(2,1)S(1)}, u32[]{:S(2)}, u32[]{:S(2)}) collective-permute-start(bf16[2,32,512]{2,1,0:T(8,128)(2,1)S(1)} %collective-permute-done.5.refs_2_), channel_id=1, source_target_pairs={{0,1},{1,0},{2,3},{3,2},{4,5},{5,4},{6,7},{7,6},{8,9},{9,8},{10,11... | collective-permute-start | bytes 196616 | tf_op jit(solution)/shard_map/ppermute | solution.py:348

commit v5 on v4

--- a/solution.py
+++ b/solution.py
@@ -10,6 +10,7 @@
 SMALL = jnp.float8_e4m3fn
 LARGEST = 448.0
 FLIGHT = 3
+CROSS = 1
 SHIFT = 16.0
 EFFECT_SCALE = 1024.0
 
@@ -79,13 +80,13 @@
     half = blocks // 2
 
     def fetch(i):
-        start = pl.multiple_of((me ^ relative_of(i)) * share, share)
+        start = pl.multiple_of((me ^ relative_of(i, me)) * share, share)
         return pltpu.make_async_copy(
             genotypes_hbm.at[pl.ds(start, share), :], staged_ref.at[i], block_sem.at[i]
         )
 
     def fetch_noise(t):
-        start = pl.multiple_of((me ^ (t * (blocks // tails))) * share, share)
+        start = pl.multiple_of((me ^ relative_of(blocks - tails + t, me)) * share, share)
         return pltpu.make_async_copy(
             noise_hbm.at[:, pl.ds(start, share)], noise_ref.at[t], noise_sem.at[t]
         )
@@ -233,11 +234,14 @@
     column_ref[...] = jnp.broadcast_to(column, column_ref.shape)
 
 
-def late_kernel(order, scale_back, held_ref, means_ref, scales_ref, own_ref, *refs):
+def late_kernel(
+    order, scale_back, swapped, held_ref, means_ref, scales_ref, own_ref, other_ref, *refs
+):
     early_ref, early_column_ref = refs[:2]
     pieces = refs[2:-2]
     phen_ref, out_ref = refs[-2:]
-    phen_ref[...] = own_ref[0]
+    mine = swapped(lax.axis_index("var")) == 0
+    phen_ref[...] = jnp.where(mine, own_ref[0], other_ref[0])
     total, column = scan_pieces(order, held_ref, pieces)
     total = total + early_ref[...]
     column = column + early_column_ref[:, :1]
@@ -260,16 +264,23 @@
 
     half = blocks // 2
 
-    def relative_of(i):
+    def parity(chip):
+        total = 0
+        for bit in range(bits - 1):
+            if CROSS >> bit & 1:
+                total = total ^ (chip >> bit & 1)
+        return total
+
+    def relative_of(i, me):
         core = 1 - i // half
         group = (i % half // tails + 1) % 4
-        return core + 2 * group + 8 * (i % tails)
+        return (core ^ parity(me >> 1)) + 2 * group + 8 * (i % tails)
 
     def position(core, group, tail):
         return (1 - core) * half + (group + 3) % 4 * tails + tail
 
     def pairs(k):
-        return [(i, i ^ k) for i in range(blocks)]
+        return [(i, i ^ k ^ parity(k >> 1)) for i in range(blocks)]
 
     vmem = pl.BlockSpec(memory_space=pltpu.VMEM)
     hbm = pl.BlockSpec(memory_space=pltpu.HBM)
@@ -371,16 +382,18 @@
         name="scan_early",
     )(held, *arrays(first))
     phen_out, scores = pl.pallas_call(
-        lambda *refs: late_kernel(places(last), scale_back, *refs),
+        lambda *refs: late_kernel(
+            places(last), scale_back, lambda me: parity(me >> 1), *refs
+        ),
         out_shape=(
             jax.ShapeDtypeStruct((pheno, share), jnp.bfloat16),
             jax.ShapeDtypeStruct((pheno, variants), jnp.float32),
         ),
-        in_specs=[vmem] * (6 + len(last)),
+        in_specs=[vmem] * (7 + len(last)),
         out_specs=[vmem] * 2,
         compiler_params=params,
         name="scan_late",
-    )(held, means_row, scales_row, own, early, early_column, *arrays(last))
+    )(held, means_row, scales_row, own, others[0], early, early_column, *arrays(last))
     if alone:
         return phen_out, scores
 

time: 35.4 us -> 35 us (0.989)
    ppermute x3, waiting for transfers between devices: 4.25 us -> 2.39 us  [on_device(): groups[g] = lax.ppermute(own, 'var', pairs(2 * g))]
    ppermute x1, waiting for transfers between devices: 2.59 us -> 3.87 us  [on_device(): other = lax.ppermute(mine, 'var', pairs(8 * step))]
    ppermute x3, starting transfers between devices: 3.71 us -> 2.99 us  [on_device(): groups[g] = lax.ppermute(own, 'var', pairs(2 * g))]
    ppermute x4, starting transfers between devices: 0.01 us -> 0.64 us  [on_device(): others = {g: lax.ppermute(groups[g], 'var', pairs(1)) for g in range(4)}]
    ppermute x4, waiting for transfers between devices: 0.01 us -> 0.49 us  [on_device(): others = {g: lax.ppermute(groups[g], 'var', pairs(1)) for g in range(4)}]
  transfers between devices with their start and end apart: 12 -> 12, of which waited for: 8 -> 9; matrix products, arithmetic and copies ran while one was open for 0% -> 0% of each run, Pallas kernels for 4% -> 4%
where the time goes in v5:
time: 35 us; the launch traced here: 34.8 us
  waiting for transfers between devices  12.1 us (35%)
  starting transfers between devices  11.1 us (32%)
  Pallas kernels  10.8 us (31%)
  between operations  0.72 us (2%)
    pallas_call x1, Pallas kernels, on_device(): pl.pallas_call(lambda *refs: evolve_kernel(blocks, share, FLIGHT, relativ...  8.44 us
    ppermute x3, starting transfers between devices, on_device(): lax.ppermute(chip[g - 1].astype(jnp.bfloat16), 'var', pairs(2 * g))  4.23 us
    ppermute x3, waiting for transfers between devices, on_device(): lax.ppermute(chip[g - 1].astype(jnp.bfloat16), 'var', pairs(2 * g))  4.21 us
    ppermute x1, waiting for transfers between devices, on_device(): other = lax.ppermute(mine, 'var', pairs(8 * step))  3.87 us
    ppermute x3, starting transfers between devices, on_device(): groups[g] = lax.ppermute(own, 'var', pairs(2 * g))  2.99 us
    ppermute x1, starting transfers between devices, on_device(): other = lax.ppermute(mine, 'var', pairs(8 * step))  2.68 us
    ppermute x3, waiting for transfers between devices, on_device(): groups[g] = lax.ppermute(own, 'var', pairs(2 * g))  2.39 us
    pallas_call x1, Pallas kernels, on_device(): pl.pallas_call(lambda *refs: early_kernel(places(first), *refs), out_shap...  1.29 us
  transfers between devices with their start and end apart: 12, of which 9 were waited for; matrix products, arithmetic and copies ran while one was open for 0% of the time, Pallas kernels for 4%

profile of v5, /device:TPU:0, one launch (start us, length us, event | category | flops | bytes accessed | tf_op | source)
XLA Modules:
  0.0 34.8 jit_solution(13535995401093092583)
XLA Ops:
  0.7 8.4 %evolve.1 = (f8e4m3fn[16,512,1024]{2,1,0:T(32,128)(4,1)S(1)}, bf16[8,32,512]{2,1,0:T(8,128)(2,1)S(1)}, f32[8,32,512]{2,1,0:T(8,128)S(1)}, f32[2,32,512]{2,1,0:T(8,128)S(1)}) custom-call(bf16[8192,1024]{1,0:T(8,128)(2,1)} %refs_0_.1, bf16[32,8192]{1,0:T(8,128)(2,1)} %refs_1_.1, f32[1,1024]{1,0:T(1,128)} %bitcast.3, f32[1,1024]{1,0:T(1,128)} %bitcast.5, ...), custom_call_target="tpu_custom_call" | custom-call | tf_op jit(solution)/shard_map/evolve/pallas_call | solution.py:291
  9.1 0.6 %collective-permute-start = (bf16[8,32,512]{2,1,0:T(8,128)(2,1)S(1)}, bf16[8,32,512]{2,1,0:T(8,128)(2,1)S(1)}, u32[]{:S(2)}, u32[]{:S(2)}) collective-permute-start(bf16[8,32,512]{2,1,0:T(8,128)(2,1)S(1)} %get-tuple-element.10), channel_id=1, source_target_pairs={{0,1},{1,0},{2,3},{3,2},{4,5},{5,4},{6,7},{7,6},{8,9},{9,8},{10,11... | collective-permute-start | bytes 786440 | tf_op jit(solution)/shard_map/ppermute | solution.py:335
  9.7 1.2 %collective-permute-done = bf16[8,32,512]{2,1,0:T(8,128)(2,1)S(1)} collective-permute-done((bf16[8,32,512]{2,1,0:T(8,128)(2,1)S(1)}, bf16[8,32,512]{2,1,0:T(8,128)(2,1)S(1)}, u32[]{:S(2)}, u32[]{:S(2)}) %collective-permute-start) | collective-permute-done | bytes 262176 | tf_op jit(solution)/shard_map/ppermute | solution.py:335
  10.8 0.1 add_convert_fusion.4
  10.9 2.7 %collective-permute-start.1 = (bf16[2,32,512]{2,1,0:T(8,128)(2,1)S(1)}, bf16[2,32,512]{2,1,0:T(8,128)(2,1)S(1)}, u32[]{:S(2)}, u32[]{:S(2)}) collective-permute-start(bf16[2,32,512]{2,1,0:T(8,128)(2,1)S(1)} %get-tuple-element.14), channel_id=1, source_target_pairs={{0,3},{1,2},{2,1},{3,0},{4,7},{5,6},{6,5},{7,4},{8,11},{9,10},{10,... | collective-permute-start | bytes 196616 | tf_op jit(solution)/shard_map/ppermute | solution.py:341
  13.5 1.5 %collective-permute-start.3 = (bf16[2,32,512]{2,1,0:T(8,128)(2,1)S(1)}, bf16[2,32,512]{2,1,0:T(8,128)(2,1)S(1)}, u32[]{:S(2)}, u32[]{:S(2)}) collective-permute-start(bf16[2,32,512]{2,1,0:T(8,128)(2,1)S(1)} %get-tuple-element.15), channel_id=1, source_target_pairs={{0,7},{1,6},{2,5},{3,4},{4,3},{5,2},{6,1},{7,0},{8,15},{9,14},{10,... | collective-permute-start | bytes 196616 | tf_op jit(solution)/shard_map/ppermute | solution.py:341
  15.1 0.1 collective-permute-start.2
  15.1 2.0 %collective-permute-done.1 = bf16[2,32,512]{2,1,0:T(8,128)(2,1)S(1)} collective-permute-done((bf16[2,32,512]{2,1,0:T(8,128)(2,1)S(1)}, bf16[2,32,512]{2,1,0:T(8,128)(2,1)S(1)}, u32[]{:S(2)}, u32[]{:S(2)}) %collective-permute-start.1) | collective-permute-done | bytes 65568 | tf_op jit(solution)/shard_map/ppermute | solution.py:341
  17.1 1.1 %collective-permute-done.3 = bf16[2,32,512]{2,1,0:T(8,128)(2,1)S(1)} collective-permute-done((bf16[2,32,512]{2,1,0:T(8,128)(2,1)S(1)}, bf16[2,32,512]{2,1,0:T(8,128)(2,1)S(1)}, u32[]{:S(2)}, u32[]{:S(2)}) %collective-permute-start.3) | collective-permute-done | bytes 65568 | tf_op jit(solution)/shard_map/ppermute | solution.py:341
  18.3 1.1 %collective-permute-done.2 = bf16[2,32,512]{2,1,0:T(8,128)(2,1)S(1)} collective-permute-done((bf16[2,32,512]{2,1,0:T(8,128)(2,1)S(1)}, bf16[2,32,512]{2,1,0:T(8,128)(2,1)S(1)}, u32[]{:S(2)}, u32[]{:S(2)}) %collective-permute-start.2) | collective-permute-done | bytes 65568 | tf_op jit(solution)/shard_map/ppermute | solution.py:341
  19.4 2.7 %collective-permute-start.4 = (bf16[2,32,512]{2,1,0:T(8,128)(2,1)S(1)}, bf16[2,32,512]{2,1,0:T(8,128)(2,1)S(1)}, u32[]{:S(2)}, u32[]{:S(2)}) collective-permute-start(bf16[2,32,512]{2,1,0:T(8,128)(2,1)S(1)} %add_convert_fusion.1), channel_id=1, source_target_pairs={{0,8},{1,9},{2,10},{3,11},{4,12},{5,13},{6,14},{7,15},{8,0},{9,1},... | collective-permute-start | bytes 196616 | tf_op jit(solution)/shard_map/ppermute | solution.py:350
  22.1 3.9 %collective-permute-done.4 = bf16[2,32,512]{2,1,0:T(8,128)(2,1)S(1)} collective-permute-done((bf16[2,32,512]{2,1,0:T(8,128)(2,1)S(1)}, bf16[2,32,512]{2,1,0:T(8,128)(2,1)S(1)}, u32[]{:S(2)}, u32[]{:S(2)}) %collective-permute-start.4) | collective-permute-done | bytes 65568 | tf_op jit(solution)/shard_map/ppermute | solution.py:350
  26.0 0.1 collective-permute-start.8
  26.0 0.3 collective-permute-start.7
  26.3 2.6 %collective-permute-start.6 = (bf16[2,32,512]{2,1,0:T(8,128)(2,1)S(1)}, bf16[2,32,512]{2,1,0:T(8,128)(2,1)S(1)}, u32[]{:S(2)}, u32[]{:S(2)}) collective-permute-start(bf16[2,32,512]{2,1,0:T(8,128)(2,1)S(1)} %add_convert_fusion.refs_1_.refs_3_), channel_id=1, source_target_pairs={{0,3},{1,2},{2,1},{3,0},{4,7},{5,6},{6,5},{7,4},{8,11},{9,10},{10,... | collective-permute-start | bytes 196616 | tf_op jit(solution)/shard_map/ppermute | solution.py:358
  29.0 2.1 %collective-permute-done.8.refs_4_ = bf16[2,32,512]{2,1,0:T(8,128)(2,1)S(1)} collective-permute-done((bf16[2,32,512]{2,1,0:T(8,128)(2,1)S(1)}, bf16[2,32,512]{2,1,0:T(8,128)(2,1)S(1)}, u32[]{:S(2)}, u32[]{:S(2)}) %collective-permute-start.8) | collective-permute-done | bytes 65568 | tf_op jit(solution)/shard_map/ppermute | solution.py:358
  31.1 0.0 collective-permute-start.9
  31.1 0.5 %collective-permute-start.10 = (bf16[2,32,512]{2,1,0:T(8,128)(2,1)S(1)}, bf16[2,32,512]{2,1,0:T(8,128)(2,1)S(1)}, u32[]{:S(2)}, u32[]{:S(2)}) collective-permute-start(bf16[2,32,512]{2,1,0:T(8,128)(2,1)S(1)} %collective-permute-done.7.refs_3_), channel_id=1, source_target_pairs={{0,1},{1,0},{2,3},{3,2},{4,5},{5,4},{6,7},{7,6},{8,9},{9,8},{10,11... | collective-permute-start | bytes 196616 | tf_op jit(solution)/shard_map/ppermute | solution.py:359
  31.6 0.3 collective-permute-done.6.refs_2_
  31.9 0.1 collective-permute-start.11
  32.0 0.3 collective-permute-done.9.refs_6_
  32.3 0.2 collective-permute-done.10.refs_7_
  32.5 1.3 %scan_early.1 = (f32[32,1024]{1,0:T(8,128)S(1)}, f32[32,128]{1,0:T(8,128)S(1)}) custom-call(f8e4m3fn[16,512,1024]{2,1,0:T(32,128)(4,1)S(1)} %get-tuple-element.8.refs_0_, bf16[2,32,512]{2,1,0:T(8,128)(2,1)S(1)} %add_convert_fusion.refs_1_.refs_3_, bf16[2,32,512]{2,1,0:T(8,128)(2,1)S(1)} %collective-permute-done.6.refs_2_, ...), custom_call_target="tpu_custom_call" | custom-call | tf_op jit(solution)/shard_map/scan_early/pallas_call | solution.py:373
  33.8 1.0 %scan_late.1 = (bf16[32,512]{1,0:T(8,128)(2,1)}, f32[32,1024]{1,0:T(8,128)}) custom-call(f8e4m3fn[16,512,1024]{2,1,0:T(32,128)(4,1)S(1)} %get-tuple-element.8.refs_0_, f32[1,1024]{1,0:T(1,128)S(1)} %bitcast.4, f32[1,1024]{1,0:T(1,128)S(1)} %bitcast.6, bf16[2,32,512]{2,1,0:T(8,128)(2,1)S(1)} %add_convert_fusion.refs_1_.refs_3_, ...), custom_call_target="tpu_custom_call" | custom-call | tf_op jit(solution)/shard_map/scan_late/pallas_call | solution.py:384
  (11 shorter events, 0.1 us)
Async XLA Ops:
  0.6 33.2 %copy-start.1 = (f32[1024]{0:T(1024)S(1)}, f32[1024]{0:T(1024)}, u32[]{:S(2)}) copy-start(f32[1024]{0:T(1024)} %param.9) | copy-start | bytes 12292
  0.6 33.2 %copy-start = (f32[1024]{0:T(1024)S(1)}, f32[1024]{0:T(1024)}, u32[]{:S(2)}) copy-start(f32[1024]{0:T(1024)} %param.8) | copy-start | bytes 12292
  9.1 1.7 %collective-permute-start = (bf16[8,32,512]{2,1,0:T(8,128)(2,1)S(1)}, bf16[8,32,512]{2,1,0:T(8,128)(2,1)S(1)}, u32[]{:S(2)}, u32[]{:S(2)}) collective-permute-start(bf16[8,32,512]{2,1,0:T(8,128)(2,1)S(1)} %get-tuple-element.10), channel_id=1, source_target_pairs={{0,1},{1,0},{2,3},{3,2},{4,5},{5,4},{6,7},{7,6},{8,9},{9,8},{10,11... | collective-permute-start | bytes 786440 | tf_op jit(solution)/shard_map/ppermute | solution.py:335
  10.9 6.3 %collective-permute-start.1 = (bf16[2,32,512]{2,1,0:T(8,128)(2,1)S(1)}, bf16[2,32,512]{2,1,0:T(8,128)(2,1)S(1)}, u32[]{:S(2)}, u32[]{:S(2)}) collective-permute-start(bf16[2,32,512]{2,1,0:T(8,128)(2,1)S(1)} %get-tuple-element.14), channel_id=1, source_target_pairs={{0,3},{1,2},{2,1},{3,0},{4,7},{5,6},{6,5},{7,4},{8,11},{9,10},{10,... | collective-permute-start | bytes 196616 | tf_op jit(solution)/shard_map/ppermute | solution.py:341
  13.5 4.7 %collective-permute-start.3 = (bf16[2,32,512]{2,1,0:T(8,128)(2,1)S(1)}, bf16[2,32,512]{2,1,0:T(8,128)(2,1)S(1)}, u32[]{:S(2)}, u32[]{:S(2)}) collective-permute-start(bf16[2,32,512]{2,1,0:T(8,128)(2,1)S(1)} %get-tuple-element.15), channel_id=1, source_target_pairs={{0,7},{1,6},{2,5},{3,4},{4,3},{5,2},{6,1},{7,0},{8,15},{9,14},{10,... | collective-permute-start | bytes 196616 | tf_op jit(solution)/shard_map/ppermute | solution.py:341
  15.1 4.3 %collective-permute-start.2 = (bf16[2,32,512]{2,1,0:T(8,128)(2,1)S(1)}, bf16[2,32,512]{2,1,0:T(8,128)(2,1)S(1)}, u32[]{:S(2)}, u32[]{:S(2)}) collective-permute-start(bf16[2,32,512]{2,1,0:T(8,128)(2,1)S(1)} %get-tuple-element.16), channel_id=1, source_target_pairs={{0,4},{1,5},{2,6},{3,7},{4,0},{5,1},{6,2},{7,3},{8,12},{9,13},{10,... | collective-permute-start | bytes 196616 | tf_op jit(solution)/shard_map/ppermute | solution.py:341
  19.4 6.5 %collective-permute-start.4 = (bf16[2,32,512]{2,1,0:T(8,128)(2,1)S(1)}, bf16[2,32,512]{2,1,0:T(8,128)(2,1)S(1)}, u32[]{:S(2)}, u32[]{:S(2)}) collective-permute-start(bf16[2,32,512]{2,1,0:T(8,128)(2,1)S(1)} %add_convert_fusion.1), channel_id=1, source_target_pairs={{0,8},{1,9},{2,10},{3,11},{4,12},{5,13},{6,14},{7,15},{8,0},{9,1},... | collective-permute-start | bytes 196616 | tf_op jit(solution)/shard_map/ppermute | solution.py:350
  26.0 5.1 %collective-permute-start.8 = (bf16[2,32,512]{2,1,0:T(8,128)(2,1)S(1)}, bf16[2,32,512]{2,1,0:T(8,128)(2,1)S(1)}, u32[]{:S(2)}, u32[]{:S(2)}) collective-permute-start(bf16[2,32,512]{2,1,0:T(8,128)(2,1)S(1)} %add_convert_fusion.refs_1_.refs_3_), channel_id=1, source_target_pairs={{0,7},{1,6},{2,5},{3,4},{4,3},{5,2},{6,1},{7,0},{8,15},{9,14},{10,... | collective-permute-start | bytes 196616 | tf_op jit(solution)/shard_map/ppermute | solution.py:358
  26.0 5.0 %collective-permute-start.7 = (bf16[2,32,512]{2,1,0:T(8,128)(2,1)S(1)}, bf16[2,32,512]{2,1,0:T(8,128)(2,1)S(1)}, u32[]{:S(2)}, u32[]{:S(2)}) collective-permute-start(bf16[2,32,512]{2,1,0:T(8,128)(2,1)S(1)} %add_convert_fusion.refs_1_.refs_3_), channel_id=1, source_target_pairs={{0,4},{1,5},{2,6},{3,7},{4,0},{5,1},{6,2},{7,3},{8,12},{9,13},{10,... | collective-permute-start | bytes 196616 | tf_op jit(solution)/shard_map/ppermute | solution.py:358
  26.3 5.5 %collective-permute-start.6 = (bf16[2,32,512]{2,1,0:T(8,128)(2,1)S(1)}, bf16[2,32,512]{2,1,0:T(8,128)(2,1)S(1)}, u32[]{:S(2)}, u32[]{:S(2)}) collective-permute-start(bf16[2,32,512]{2,1,0:T(8,128)(2,1)S(1)} %add_convert_fusion.refs_1_.refs_3_), channel_id=1, source_target_pairs={{0,3},{1,2},{2,1},{3,0},{4,7},{5,6},{6,5},{7,4},{8,11},{9,10},{10,... | collective-permute-start | bytes 196616 | tf_op jit(solution)/shard_map/ppermute | solution.py:358
  29.0 3.0 %collective-permute-start.5 = (bf16[2,32,512]{2,1,0:T(8,128)(2,1)S(1)}, bf16[2,32,512]{2,1,0:T(8,128)(2,1)S(1)}, u32[]{:S(2)}, u32[]{:S(2)}) collective-permute-start(bf16[2,32,512]{2,1,0:T(8,128)(2,1)S(1)} %add_convert_fusion.refs_1_.refs_3_), channel_id=1, source_target_pairs={{0,1},{1,0},{2,3},{3,2},{4,5},{5,4},{6,7},{7,6},{8,9},{9,8},{10,11... | collective-permute-start | bytes 196616 | tf_op jit(solution)/shard_map/ppermute | solution.py:359
  31.1 1.3 %collective-permute-start.9 = (bf16[2,32,512]{2,1,0:T(8,128)(2,1)S(1)}, bf16[2,32,512]{2,1,0:T(8,128)(2,1)S(1)}, u32[]{:S(2)}, u32[]{:S(2)}) collective-permute-start(bf16[2,32,512]{2,1,0:T(8,128)(2,1)S(1)} %collective-permute-done.8.refs_4_), channel_id=1, source_target_pairs={{0,1},{1,0},{2,3},{3,2},{4,5},{5,4},{6,7},{7,6},{8,9},{9,8},{10,11... | collective-permute-start | bytes 196616 | tf_op jit(solution)/shard_map/ppermute | solution.py:359
  31.1 1.4 %collective-permute-start.10 = (bf16[2,32,512]{2,1,0:T(8,128)(2,1)S(1)}, bf16[2,32,512]{2,1,0:T(8,128)(2,1)S(1)}, u32[]{:S(2)}, u32[]{:S(2)}) collective-permute-start(bf16[2,32,512]{2,1,0:T(8,128)(2,1)S(1)} %collective-permute-done.7.refs_3_), channel_id=1, source_target_pairs={{0,1},{1,0},{2,3},{3,2},{4,5},{5,4},{6,7},{7,6},{8,9},{9,8},{10,11... | collective-permute-start | bytes 196616 | tf_op jit(solution)/shard_map/ppermute | solution.py:359
  31.9 1.9 %collective-permute-start.11 = (bf16[2,32,512]{2,1,0:T(8,128)(2,1)S(1)}, bf16[2,32,512]{2,1,0:T(8,128)(2,1)S(1)}, u32[]{:S(2)}, u32[]{:S(2)}) collective-permute-start(bf16[2,32,512]{2,1,0:T(8,128)(2,1)S(1)} %collective-permute-done.6.refs_2_), channel_id=1, source_target_pairs={{0,1},{1,0},{2,3},{3,2},{4,5},{5,4},{6,7},{7,6},{8,9},{9,8},{10,11... | collective-permute-start | bytes 196616 | tf_op jit(solution)/shard_map/ppermute | solution.py:359

commit v6 on v5

--- a/solution.py
+++ b/solution.py
@@ -179,31 +179,20 @@
     factor = heavy / scale
     shift = heavy * offset
 
-    def convert(i):
-        fetch(i).wait()
-        held_ref[i] = staged_ref[i].astype(SMALL)
-
-    def partial(i):
-        sums = lax.dot_general(
-            weights, held_ref[i], (((1,), (1,)), ((), ())), preferred_element_type=jnp.float32
-        )
-        return join(sums, 2) * factor - shift
-
-    convert(0)
-
-    def multiply_send(i, carry):
-        convert(i + 1)
-        send_ref[i] = partial(i).astype(send_ref.dtype)
-        return carry
-
-    def multiply_keep(i, carry):
-        convert(half + i + 1)
-        keep_ref[i] = partial(half + i).astype(keep_ref.dtype)
-        return carry
-
-    lax.fori_loop(0, half, multiply_send, 0, unroll=True)
-    lax.fori_loop(0, half - 1, multiply_keep, 0, unroll=True)
-    keep_ref[half - 1] = partial(blocks - 1).astype(keep_ref.dtype)
+    for start in range(0, blocks, 2):
+        for i in (start, start + 1):
+            fetch(i).wait()
+        for i in (start, start + 1):
+            block = staged_ref[i].astype(SMALL)
+            held_ref[i] = block
+            sums = lax.dot_general(
+                weights, block, (((1,), (1,)), ((), ())), preferred_element_type=jnp.float32
+            )
+            value = join(sums, 2) * factor - shift
+            if i < half:
+                send_ref[i] = value.astype(send_ref.dtype)
+            else:
+                keep_ref[i - half] = value.astype(keep_ref.dtype)
     for t in range(tails):
         fetch_noise(t).wait()
         tail_ref[t] = light * noise_ref[t].astype(jnp.float32)

time: 35 us -> 34 us (0.971)
  Pallas kernels: 10.8 us -> 9.74 us
    pallas_call x1, Pallas kernels: 8.44 us -> 7.44 us  [on_device(): pl.pallas_call(lambda *refs: evolve_kernel(blocks, share, FLIGHT, relativ...]
where the time goes in v6:
time: 34 us; the launch traced here: 33.8 us
  waiting for transfers between devices  12.1 us (36%)
  starting transfers between devices  11.1 us (33%)
  Pallas kernels  9.74 us (29%)
  between operations  0.72 us (2%)
    pallas_call x1, Pallas kernels, on_device(): pl.pallas_call(lambda *refs: evolve_kernel(blocks, share, FLIGHT, relativ...  7.44 us
    ppermute x3, starting transfers between devices, on_device(): lax.ppermute(chip[g - 1].astype(jnp.bfloat16), 'var', pairs(2 * g))  4.23 us
    ppermute x3, waiting for transfers between devices, on_device(): lax.ppermute(chip[g - 1].astype(jnp.bfloat16), 'var', pairs(2 * g))  4.21 us
    ppermute x1, waiting for transfers between devices, on_device(): other = lax.ppermute(mine, 'var', pairs(8 * step))  3.87 us
    ppermute x3, starting transfers between devices, on_device(): groups[g] = lax.ppermute(own, 'var', pairs(2 * g))  2.99 us
    ppermute x1, starting transfers between devices, on_device(): other = lax.ppermute(mine, 'var', pairs(8 * step))  2.68 us
    ppermute x3, waiting for transfers between devices, on_device(): groups[g] = lax.ppermute(own, 'var', pairs(2 * g))  2.39 us
    pallas_call x1, Pallas kernels, on_device(): pl.pallas_call(lambda *refs: early_kernel(places(first), *refs), out_shap...  1.29 us
  transfers between devices with their start and end apart: 12, of which 9 were waited for; matrix products, arithmetic and copies ran while one was open for 0% of the time, Pallas kernels for 4%

profile of v6, /device:TPU:0, one launch (start us, length us, event | category | flops | bytes accessed | tf_op | source)
XLA Modules:
  0.0 33.8 jit_solution(1682125690700337107)
XLA Ops:
  0.7 7.4 %evolve.1 = (f8e4m3fn[16,512,1024]{2,1,0:T(32,128)(4,1)S(1)}, bf16[8,32,512]{2,1,0:T(8,128)(2,1)S(1)}, f32[8,32,512]{2,1,0:T(8,128)S(1)}, f32[2,32,512]{2,1,0:T(8,128)S(1)}) custom-call(bf16[8192,1024]{1,0:T(8,128)(2,1)} %refs_0_.1, bf16[32,8192]{1,0:T(8,128)(2,1)} %refs_1_.1, f32[1,1024]{1,0:T(1,128)} %bitcast.3, f32[1,1024]{1,0:T(1,128)} %bitcast.5, ...), custom_call_target="tpu_custom_call" | custom-call | tf_op jit(solution)/shard_map/evolve/pallas_call | solution.py:280
  8.1 0.6 %collective-permute-start = (bf16[8,32,512]{2,1,0:T(8,128)(2,1)S(1)}, bf16[8,32,512]{2,1,0:T(8,128)(2,1)S(1)}, u32[]{:S(2)}, u32[]{:S(2)}) collective-permute-start(bf16[8,32,512]{2,1,0:T(8,128)(2,1)S(1)} %get-tuple-element.10), channel_id=1, source_target_pairs={{0,1},{1,0},{2,3},{3,2},{4,5},{5,4},{6,7},{7,6},{8,9},{9,8},{10,11... | collective-permute-start | bytes 786440 | tf_op jit(solution)/shard_map/ppermute | solution.py:324
  8.7 1.2 %collective-permute-done = bf16[8,32,512]{2,1,0:T(8,128)(2,1)S(1)} collective-permute-done((bf16[8,32,512]{2,1,0:T(8,128)(2,1)S(1)}, bf16[8,32,512]{2,1,0:T(8,128)(2,1)S(1)}, u32[]{:S(2)}, u32[]{:S(2)}) %collective-permute-start) | collective-permute-done | bytes 262176 | tf_op jit(solution)/shard_map/ppermute | solution.py:324
  9.8 0.1 add_convert_fusion.4
  9.9 2.7 %collective-permute-start.1 = (bf16[2,32,512]{2,1,0:T(8,128)(2,1)S(1)}, bf16[2,32,512]{2,1,0:T(8,128)(2,1)S(1)}, u32[]{:S(2)}, u32[]{:S(2)}) collective-permute-start(bf16[2,32,512]{2,1,0:T(8,128)(2,1)S(1)} %get-tuple-element.14), channel_id=1, source_target_pairs={{0,3},{1,2},{2,1},{3,0},{4,7},{5,6},{6,5},{7,4},{8,11},{9,10},{10,... | collective-permute-start | bytes 196616 | tf_op jit(solution)/shard_map/ppermute | solution.py:330
  12.5 1.5 %collective-permute-start.3 = (bf16[2,32,512]{2,1,0:T(8,128)(2,1)S(1)}, bf16[2,32,512]{2,1,0:T(8,128)(2,1)S(1)}, u32[]{:S(2)}, u32[]{:S(2)}) collective-permute-start(bf16[2,32,512]{2,1,0:T(8,128)(2,1)S(1)} %get-tuple-element.15), channel_id=1, source_target_pairs={{0,7},{1,6},{2,5},{3,4},{4,3},{5,2},{6,1},{7,0},{8,15},{9,14},{10,... | collective-permute-start | bytes 196616 | tf_op jit(solution)/shard_map/ppermute | solution.py:330
  14.1 0.1 collective-permute-start.2
  14.1 2.0 %collective-permute-done.1 = bf16[2,32,512]{2,1,0:T(8,128)(2,1)S(1)} collective-permute-done((bf16[2,32,512]{2,1,0:T(8,128)(2,1)S(1)}, bf16[2,32,512]{2,1,0:T(8,128)(2,1)S(1)}, u32[]{:S(2)}, u32[]{:S(2)}) %collective-permute-start.1) | collective-permute-done | bytes 65568 | tf_op jit(solution)/shard_map/ppermute | solution.py:330
  16.1 1.1 %collective-permute-done.3 = bf16[2,32,512]{2,1,0:T(8,128)(2,1)S(1)} collective-permute-done((bf16[2,32,512]{2,1,0:T(8,128)(2,1)S(1)}, bf16[2,32,512]{2,1,0:T(8,128)(2,1)S(1)}, u32[]{:S(2)}, u32[]{:S(2)}) %collective-permute-start.3) | collective-permute-done | bytes 65568 | tf_op jit(solution)/shard_map/ppermute | solution.py:330
  17.3 1.1 %collective-permute-done.2 = bf16[2,32,512]{2,1,0:T(8,128)(2,1)S(1)} collective-permute-done((bf16[2,32,512]{2,1,0:T(8,128)(2,1)S(1)}, bf16[2,32,512]{2,1,0:T(8,128)(2,1)S(1)}, u32[]{:S(2)}, u32[]{:S(2)}) %collective-permute-start.2) | collective-permute-done | bytes 65568 | tf_op jit(solution)/shard_map/ppermute | solution.py:330
  18.4 2.7 %collective-permute-start.4 = (bf16[2,32,512]{2,1,0:T(8,128)(2,1)S(1)}, bf16[2,32,512]{2,1,0:T(8,128)(2,1)S(1)}, u32[]{:S(2)}, u32[]{:S(2)}) collective-permute-start(bf16[2,32,512]{2,1,0:T(8,128)(2,1)S(1)} %add_convert_fusion.1), channel_id=1, source_target_pairs={{0,8},{1,9},{2,10},{3,11},{4,12},{5,13},{6,14},{7,15},{8,0},{9,1},... | collective-permute-start | bytes 196616 | tf_op jit(solution)/shard_map/ppermute | solution.py:339
  21.0 3.9 %collective-permute-done.4 = bf16[2,32,512]{2,1,0:T(8,128)(2,1)S(1)} collective-permute-done((bf16[2,32,512]{2,1,0:T(8,128)(2,1)S(1)}, bf16[2,32,512]{2,1,0:T(8,128)(2,1)S(1)}, u32[]{:S(2)}, u32[]{:S(2)}) %collective-permute-start.4) | collective-permute-done | bytes 65568 | tf_op jit(solution)/shard_map/ppermute | solution.py:339
  25.0 0.1 collective-permute-start.8
  25.0 0.3 collective-permute-start.7
  25.3 2.6 %collective-permute-start.6 = (bf16[2,32,512]{2,1,0:T(8,128)(2,1)S(1)}, bf16[2,32,512]{2,1,0:T(8,128)(2,1)S(1)}, u32[]{:S(2)}, u32[]{:S(2)}) collective-permute-start(bf16[2,32,512]{2,1,0:T(8,128)(2,1)S(1)} %add_convert_fusion.refs_1_.refs_3_), channel_id=1, source_target_pairs={{0,3},{1,2},{2,1},{3,0},{4,7},{5,6},{6,5},{7,4},{8,11},{9,10},{10,... | collective-permute-start | bytes 196616 | tf_op jit(solution)/shard_map/ppermute | solution.py:347
  27.9 2.1 %collective-permute-done.8.refs_4_ = bf16[2,32,512]{2,1,0:T(8,128)(2,1)S(1)} collective-permute-done((bf16[2,32,512]{2,1,0:T(8,128)(2,1)S(1)}, bf16[2,32,512]{2,1,0:T(8,128)(2,1)S(1)}, u32[]{:S(2)}, u32[]{:S(2)}) %collective-permute-start.8) | collective-permute-done | bytes 65568 | tf_op jit(solution)/shard_map/ppermute | solution.py:347
  30.1 0.5 %collective-permute-start.10 = (bf16[2,32,512]{2,1,0:T(8,128)(2,1)S(1)}, bf16[2,32,512]{2,1,0:T(8,128)(2,1)S(1)}, u32[]{:S(2)}, u32[]{:S(2)}) collective-permute-start(bf16[2,32,512]{2,1,0:T(8,128)(2,1)S(1)} %collective-permute-done.7.refs_3_), channel_id=1, source_target_pairs={{0,1},{1,0},{2,3},{3,2},{4,5},{5,4},{6,7},{7,6},{8,9},{9,8},{10,11... | collective-permute-start | bytes 196616 | tf_op jit(solution)/shard_map/ppermute | solution.py:348
  30.6 0.3 collective-permute-done.6.refs_2_
  30.9 0.1 collective-permute-start.11
  31.0 0.0 collective-permute-done.5.refs_5_.refs_4_
  31.0 0.3 collective-permute-done.9.refs_6_
  31.3 0.2 collective-permute-done.10.refs_7_
  31.5 1.3 %scan_early.1 = (f32[32,1024]{1,0:T(8,128)S(1)}, f32[32,128]{1,0:T(8,128)S(1)}) custom-call(f8e4m3fn[16,512,1024]{2,1,0:T(32,128)(4,1)S(1)} %get-tuple-element.8.refs_0_, bf16[2,32,512]{2,1,0:T(8,128)(2,1)S(1)} %add_convert_fusion.refs_1_.refs_3_, bf16[2,32,512]{2,1,0:T(8,128)(2,1)S(1)} %collective-permute-done.6.refs_2_, ...), custom_call_target="tpu_custom_call" | custom-call | tf_op jit(solution)/shard_map/scan_early/pallas_call | solution.py:362
  32.8 1.0 %scan_late.1 = (bf16[32,512]{1,0:T(8,128)(2,1)}, f32[32,1024]{1,0:T(8,128)}) custom-call(f8e4m3fn[16,512,1024]{2,1,0:T(32,128)(4,1)S(1)} %get-tuple-element.8.refs_0_, f32[1,1024]{1,0:T(1,128)S(1)} %bitcast.4, f32[1,1024]{1,0:T(1,128)S(1)} %bitcast.6, bf16[2,32,512]{2,1,0:T(8,128)(2,1)S(1)} %add_convert_fusion.refs_1_.refs_3_, ...), custom_call_target="tpu_custom_call" | custom-call | tf_op jit(solution)/shard_map/scan_late/pallas_call | solution.py:373
  (11 shorter events, 0.1 us)
Async XLA Ops:
  0.6 32.1 %copy-start.1 = (f32[1024]{0:T(1024)S(1)}, f32[1024]{0:T(1024)}, u32[]{:S(2)}) copy-start(f32[1024]{0:T(1024)} %param.9) | copy-start | bytes 12292
  0.6 32.1 %copy-start = (f32[1024]{0:T(1024)S(1)}, f32[1024]{0:T(1024)}, u32[]{:S(2)}) copy-start(f32[1024]{0:T(1024)} %param.8) | copy-start | bytes 12292
  8.1 1.7 %collective-permute-start = (bf16[8,32,512]{2,1,0:T(8,128)(2,1)S(1)}, bf16[8,32,512]{2,1,0:T(8,128)(2,1)S(1)}, u32[]{:S(2)}, u32[]{:S(2)}) collective-permute-start(bf16[8,32,512]{2,1,0:T(8,128)(2,1)S(1)} %get-tuple-element.10), channel_id=1, source_target_pairs={{0,1},{1,0},{2,3},{3,2},{4,5},{5,4},{6,7},{7,6},{8,9},{9,8},{10,11... | collective-permute-start | bytes 786440 | tf_op jit(solution)/shard_map/ppermute | solution.py:324
  9.9 6.3 %collective-permute-start.1 = (bf16[2,32,512]{2,1,0:T(8,128)(2,1)S(1)}, bf16[2,32,512]{2,1,0:T(8,128)(2,1)S(1)}, u32[]{:S(2)}, u32[]{:S(2)}) collective-permute-start(bf16[2,32,512]{2,1,0:T(8,128)(2,1)S(1)} %get-tuple-element.14), channel_id=1, source_target_pairs={{0,3},{1,2},{2,1},{3,0},{4,7},{5,6},{6,5},{7,4},{8,11},{9,10},{10,... | collective-permute-start | bytes 196616 | tf_op jit(solution)/shard_map/ppermute | solution.py:330
  12.5 4.7 %collective-permute-start.3 = (bf16[2,32,512]{2,1,0:T(8,128)(2,1)S(1)}, bf16[2,32,512]{2,1,0:T(8,128)(2,1)S(1)}, u32[]{:S(2)}, u32[]{:S(2)}) collective-permute-start(bf16[2,32,512]{2,1,0:T(8,128)(2,1)S(1)} %get-tuple-element.15), channel_id=1, source_target_pairs={{0,7},{1,6},{2,5},{3,4},{4,3},{5,2},{6,1},{7,0},{8,15},{9,14},{10,... | collective-permute-start | bytes 196616 | tf_op jit(solution)/shard_map/ppermute | solution.py:330
  14.1 4.3 %collective-permute-start.2 = (bf16[2,32,512]{2,1,0:T(8,128)(2,1)S(1)}, bf16[2,32,512]{2,1,0:T(8,128)(2,1)S(1)}, u32[]{:S(2)}, u32[]{:S(2)}) collective-permute-start(bf16[2,32,512]{2,1,0:T(8,128)(2,1)S(1)} %get-tuple-element.16), channel_id=1, source_target_pairs={{0,4},{1,5},{2,6},{3,7},{4,0},{5,1},{6,2},{7,3},{8,12},{9,13},{10,... | collective-permute-start | bytes 196616 | tf_op jit(solution)/shard_map/ppermute | solution.py:330
  18.4 6.5 %collective-permute-start.4 = (bf16[2,32,512]{2,1,0:T(8,128)(2,1)S(1)}, bf16[2,32,512]{2,1,0:T(8,128)(2,1)S(1)}, u32[]{:S(2)}, u32[]{:S(2)}) collective-permute-start(bf16[2,32,512]{2,1,0:T(8,128)(2,1)S(1)} %add_convert_fusion.1), channel_id=1, source_target_pairs={{0,8},{1,9},{2,10},{3,11},{4,12},{5,13},{6,14},{7,15},{8,0},{9,1},... | collective-permute-start | bytes 196616 | tf_op jit(solution)/shard_map/ppermute | solution.py:339
  25.0 5.1 %collective-permute-start.8 = (bf16[2,32,512]{2,1,0:T(8,128)(2,1)S(1)}, bf16[2,32,512]{2,1,0:T(8,128)(2,1)S(1)}, u32[]{:S(2)}, u32[]{:S(2)}) collective-permute-start(bf16[2,32,512]{2,1,0:T(8,128)(2,1)S(1)} %add_convert_fusion.refs_1_.refs_3_), channel_id=1, source_target_pairs={{0,7},{1,6},{2,5},{3,4},{4,3},{5,2},{6,1},{7,0},{8,15},{9,14},{10,... | collective-permute-start | bytes 196616 | tf_op jit(solution)/shard_map/ppermute | solution.py:347
  25.0 5.0 %collective-permute-start.7 = (bf16[2,32,512]{2,1,0:T(8,128)(2,1)S(1)}, bf16[2,32,512]{2,1,0:T(8,128)(2,1)S(1)}, u32[]{:S(2)}, u32[]{:S(2)}) collective-permute-start(bf16[2,32,512]{2,1,0:T(8,128)(2,1)S(1)} %add_convert_fusion.refs_1_.refs_3_), channel_id=1, source_target_pairs={{0,4},{1,5},{2,6},{3,7},{4,0},{5,1},{6,2},{7,3},{8,12},{9,13},{10,... | collective-permute-start | bytes 196616 | tf_op jit(solution)/shard_map/ppermute | solution.py:347
  25.3 5.5 %collective-permute-start.6 = (bf16[2,32,512]{2,1,0:T(8,128)(2,1)S(1)}, bf16[2,32,512]{2,1,0:T(8,128)(2,1)S(1)}, u32[]{:S(2)}, u32[]{:S(2)}) collective-permute-start(bf16[2,32,512]{2,1,0:T(8,128)(2,1)S(1)} %add_convert_fusion.refs_1_.refs_3_), channel_id=1, source_target_pairs={{0,3},{1,2},{2,1},{3,0},{4,7},{5,6},{6,5},{7,4},{8,11},{9,10},{10,... | collective-permute-start | bytes 196616 | tf_op jit(solution)/shard_map/ppermute | solution.py:347
  27.9 3.0 %collective-permute-start.5 = (bf16[2,32,512]{2,1,0:T(8,128)(2,1)S(1)}, bf16[2,32,512]{2,1,0:T(8,128)(2,1)S(1)}, u32[]{:S(2)}, u32[]{:S(2)}) collective-permute-start(bf16[2,32,512]{2,1,0:T(8,128)(2,1)S(1)} %add_convert_fusion.refs_1_.refs_3_), channel_id=1, source_target_pairs={{0,1},{1,0},{2,3},{3,2},{4,5},{5,4},{6,7},{7,6},{8,9},{9,8},{10,11... | collective-permute-start | bytes 196616 | tf_op jit(solution)/shard_map/ppermute | solution.py:348
  30.1 1.3 %collective-permute-start.9 = (bf16[2,32,512]{2,1,0:T(8,128)(2,1)S(1)}, bf16[2,32,512]{2,1,0:T(8,128)(2,1)S(1)}, u32[]{:S(2)}, u32[]{:S(2)}) collective-permute-start(bf16[2,32,512]{2,1,0:T(8,128)(2,1)S(1)} %collective-permute-done.8.refs_4_), channel_id=1, source_target_pairs={{0,1},{1,0},{2,3},{3,2},{4,5},{5,4},{6,7},{7,6},{8,9},{9,8},{10,11... | collective-permute-start | bytes 196616 | tf_op jit(solution)/shard_map/ppermute | solution.py:348
  30.1 1.4 %collective-permute-start.10 = (bf16[2,32,512]{2,1,0:T(8,128)(2,1)S(1)}, bf16[2,32,512]{2,1,0:T(8,128)(2,1)S(1)}, u32[]{:S(2)}, u32[]{:S(2)}) collective-permute-start(bf16[2,32,512]{2,1,0:T(8,128)(2,1)S(1)} %collective-permute-done.7.refs_3_), channel_id=1, source_target_pairs={{0,1},{1,0},{2,3},{3,2},{4,5},{5,4},{6,7},{7,6},{8,9},{9,8},{10,11... | collective-permute-start | bytes 196616 | tf_op jit(solution)/shard_map/ppermute | solution.py:348
  30.9 1.9 %collective-permute-start.11 = (bf16[2,32,512]{2,1,0:T(8,128)(2,1)S(1)}, bf16[2,32,512]{2,1,0:T(8,128)(2,1)S(1)}, u32[]{:S(2)}, u32[]{:S(2)}) collective-permute-start(bf16[2,32,512]{2,1,0:T(8,128)(2,1)S(1)} %collective-permute-done.6.refs_2_), channel_id=1, source_target_pairs={{0,1},{1,0},{2,3},{3,2},{4,5},{5,4},{6,7},{7,6},{8,9},{9,8},{10,11... | collective-permute-start | bytes 196616 | tf_op jit(solution)/shard_map/ppermute | solution.py:348

commit v7 on v6

--- a/solution.py
+++ b/solution.py
@@ -9,6 +9,7 @@
 MIB = 1 << 20
 SMALL = jnp.float8_e4m3fn
 LARGEST = 448.0
+EARLY = 2
 FLIGHT = 3
 CROSS = 1
 SHIFT = 16.0
@@ -103,7 +104,11 @@
             )
         )
     ]
-    for copy in small:
+    for copy in small[:2]:
+        copy.start()
+    for i in range(EARLY):
+        fetch(i).start()
+    for copy in small[2:]:
         copy.start()
     for t in range(tails):
         fetch_noise(t).start()
@@ -115,7 +120,7 @@
     value_ref[...] = jnp.zeros(value_ref.shape, jnp.float32)
     for copy in small[:2]:
         copy.wait()
-    for i in range(flight):
+    for i in range(EARLY, flight):
         fetch(i).start()
     local = causal_ref[...] - me * variants
     inside = (local >= 0) & (local < variants)

time: 34 us -> 33.6 us (0.988)
  Pallas kernels: 9.74 us -> 9.35 us
    pallas_call x1, Pallas kernels: 7.44 us -> 7.04 us  [on_device(): pl.pallas_call(lambda *refs: evolve_kernel(blocks, share, FLIGHT, relativ...]
where the time goes in v7:
time: 33.6 us; the launch traced here: 33.4 us
  waiting for transfers between devices  12.1 us (36%)
  starting transfers between devices  11.1 us (33%)
  Pallas kernels  9.35 us (28%)
  between operations  0.72 us (2%)
    pallas_call x1, Pallas kernels, on_device(): pl.pallas_call(lambda *refs: evolve_kernel(blocks, share, FLIGHT, relativ...  7.04 us
    ppermute x3, starting transfers between devices, on_device(): lax.ppermute(chip[g - 1].astype(jnp.bfloat16), 'var', pairs(2 * g))  4.23 us
    ppermute x3, waiting for transfers between devices, on_device(): lax.ppermute(chip[g - 1].astype(jnp.bfloat16), 'var', pairs(2 * g))  4.21 us
    ppermute x1, waiting for transfers between devices, on_device(): other = lax.ppermute(mine, 'var', pairs(8 * step))  3.87 us
    ppermute x3, starting transfers between devices, on_device(): groups[g] = lax.ppermute(own, 'var', pairs(2 * g))  2.99 us
    ppermute x1, starting transfers between devices, on_device(): other = lax.ppermute(mine, 'var', pairs(8 * step))  2.68 us
    ppermute x3, waiting for transfers between devices, on_device(): groups[g] = lax.ppermute(own, 'var', pairs(2 * g))  2.39 us
    pallas_call x1, Pallas kernels, on_device(): pl.pallas_call(lambda *refs: early_kernel(places(first), *refs), out_shap...  1.29 us
  transfers between devices with their start and end apart: 12, of which 9 were waited for; matrix products, arithmetic and copies ran while one was open for 0% of the time, Pallas kernels for 4%

profile of v7, /device:TPU:0, one launch (start us, length us, event | category | flops | bytes accessed | tf_op | source)
XLA Modules:
  0.0 33.4 jit_solution(2203253396364151988)
XLA Ops:
  0.7 7.0 %evolve.1 = (f8e4m3fn[16,512,1024]{2,1,0:T(32,128)(4,1)S(1)}, bf16[8,32,512]{2,1,0:T(8,128)(2,1)S(1)}, f32[8,32,512]{2,1,0:T(8,128)S(1)}, f32[2,32,512]{2,1,0:T(8,128)S(1)}) custom-call(bf16[8192,1024]{1,0:T(8,128)(2,1)} %refs_0_.1, bf16[32,8192]{1,0:T(8,128)(2,1)} %refs_1_.1, f32[1,1024]{1,0:T(1,128)} %bitcast.3, f32[1,1024]{1,0:T(1,128)} %bitcast.5, ...), custom_call_target="tpu_custom_call" | custom-call | tf_op jit(solution)/shard_map/evolve/pallas_call | solution.py:285
  7.7 0.6 %collective-permute-start = (bf16[8,32,512]{2,1,0:T(8,128)(2,1)S(1)}, bf16[8,32,512]{2,1,0:T(8,128)(2,1)S(1)}, u32[]{:S(2)}, u32[]{:S(2)}) collective-permute-start(bf16[8,32,512]{2,1,0:T(8,128)(2,1)S(1)} %get-tuple-element.10), channel_id=1, source_target_pairs={{0,1},{1,0},{2,3},{3,2},{4,5},{5,4},{6,7},{7,6},{8,9},{9,8},{10,11... | collective-permute-start | bytes 786440 | tf_op jit(solution)/shard_map/ppermute | solution.py:329
  8.3 1.2 %collective-permute-done = bf16[8,32,512]{2,1,0:T(8,128)(2,1)S(1)} collective-permute-done((bf16[8,32,512]{2,1,0:T(8,128)(2,1)S(1)}, bf16[8,32,512]{2,1,0:T(8,128)(2,1)S(1)}, u32[]{:S(2)}, u32[]{:S(2)}) %collective-permute-start) | collective-permute-done | bytes 262176 | tf_op jit(solution)/shard_map/ppermute | solution.py:329
  9.4 0.1 add_convert_fusion.4
  9.5 2.7 %collective-permute-start.1 = (bf16[2,32,512]{2,1,0:T(8,128)(2,1)S(1)}, bf16[2,32,512]{2,1,0:T(8,128)(2,1)S(1)}, u32[]{:S(2)}, u32[]{:S(2)}) collective-permute-start(bf16[2,32,512]{2,1,0:T(8,128)(2,1)S(1)} %get-tuple-element.14), channel_id=1, source_target_pairs={{0,3},{1,2},{2,1},{3,0},{4,7},{5,6},{6,5},{7,4},{8,11},{9,10},{10,... | collective-permute-start | bytes 196616 | tf_op jit(solution)/shard_map/ppermute | solution.py:335
  12.1 1.5 %collective-permute-start.3 = (bf16[2,32,512]{2,1,0:T(8,128)(2,1)S(1)}, bf16[2,32,512]{2,1,0:T(8,128)(2,1)S(1)}, u32[]{:S(2)}, u32[]{:S(2)}) collective-permute-start(bf16[2,32,512]{2,1,0:T(8,128)(2,1)S(1)} %get-tuple-element.15), channel_id=1, source_target_pairs={{0,7},{1,6},{2,5},{3,4},{4,3},{5,2},{6,1},{7,0},{8,15},{9,14},{10,... | collective-permute-start | bytes 196616 | tf_op jit(solution)/shard_map/ppermute | solution.py:335
  13.7 0.1 collective-permute-start.2
  13.7 2.0 %collective-permute-done.1 = bf16[2,32,512]{2,1,0:T(8,128)(2,1)S(1)} collective-permute-done((bf16[2,32,512]{2,1,0:T(8,128)(2,1)S(1)}, bf16[2,32,512]{2,1,0:T(8,128)(2,1)S(1)}, u32[]{:S(2)}, u32[]{:S(2)}) %collective-permute-start.1) | collective-permute-done | bytes 65568 | tf_op jit(solution)/shard_map/ppermute | solution.py:335
  15.7 1.1 %collective-permute-done.3 = bf16[2,32,512]{2,1,0:T(8,128)(2,1)S(1)} collective-permute-done((bf16[2,32,512]{2,1,0:T(8,128)(2,1)S(1)}, bf16[2,32,512]{2,1,0:T(8,128)(2,1)S(1)}, u32[]{:S(2)}, u32[]{:S(2)}) %collective-permute-start.3) | collective-permute-done | bytes 65568 | tf_op jit(solution)/shard_map/ppermute | solution.py:335
  16.9 1.1 %collective-permute-done.2 = bf16[2,32,512]{2,1,0:T(8,128)(2,1)S(1)} collective-permute-done((bf16[2,32,512]{2,1,0:T(8,128)(2,1)S(1)}, bf16[2,32,512]{2,1,0:T(8,128)(2,1)S(1)}, u32[]{:S(2)}, u32[]{:S(2)}) %collective-permute-start.2) | collective-permute-done | bytes 65568 | tf_op jit(solution)/shard_map/ppermute | solution.py:335
  18.0 2.7 %collective-permute-start.4 = (bf16[2,32,512]{2,1,0:T(8,128)(2,1)S(1)}, bf16[2,32,512]{2,1,0:T(8,128)(2,1)S(1)}, u32[]{:S(2)}, u32[]{:S(2)}) collective-permute-start(bf16[2,32,512]{2,1,0:T(8,128)(2,1)S(1)} %add_convert_fusion.1), channel_id=1, source_target_pairs={{0,8},{1,9},{2,10},{3,11},{4,12},{5,13},{6,14},{7,15},{8,0},{9,1},... | collective-permute-start | bytes 196616 | tf_op jit(solution)/shard_map/ppermute | solution.py:344
  20.6 3.9 %collective-permute-done.4 = bf16[2,32,512]{2,1,0:T(8,128)(2,1)S(1)} collective-permute-done((bf16[2,32,512]{2,1,0:T(8,128)(2,1)S(1)}, bf16[2,32,512]{2,1,0:T(8,128)(2,1)S(1)}, u32[]{:S(2)}, u32[]{:S(2)}) %collective-permute-start.4) | collective-permute-done | bytes 65568 | tf_op jit(solution)/shard_map/ppermute | solution.py:344
  24.6 0.1 collective-permute-start.8
  24.6 0.3 collective-permute-start.7
  24.9 2.6 %collective-permute-start.6 = (bf16[2,32,512]{2,1,0:T(8,128)(2,1)S(1)}, bf16[2,32,512]{2,1,0:T(8,128)(2,1)S(1)}, u32[]{:S(2)}, u32[]{:S(2)}) collective-permute-start(bf16[2,32,512]{2,1,0:T(8,128)(2,1)S(1)} %add_convert_fusion.refs_1_.refs_3_), channel_id=1, source_target_pairs={{0,3},{1,2},{2,1},{3,0},{4,7},{5,6},{6,5},{7,4},{8,11},{9,10},{10,... | collective-permute-start | bytes 196616 | tf_op jit(solution)/shard_map/ppermute | solution.py:352
  27.5 0.0 collective-permute-start.5
  27.6 2.1 %collective-permute-done.8.refs_4_ = bf16[2,32,512]{2,1,0:T(8,128)(2,1)S(1)} collective-permute-done((bf16[2,32,512]{2,1,0:T(8,128)(2,1)S(1)}, bf16[2,32,512]{2,1,0:T(8,128)(2,1)S(1)}, u32[]{:S(2)}, u32[]{:S(2)}) %collective-permute-start.8) | collective-permute-done | bytes 65568 | tf_op jit(solution)/shard_map/ppermute | solution.py:352
  29.7 0.5 %collective-permute-start.10 = (bf16[2,32,512]{2,1,0:T(8,128)(2,1)S(1)}, bf16[2,32,512]{2,1,0:T(8,128)(2,1)S(1)}, u32[]{:S(2)}, u32[]{:S(2)}) collective-permute-start(bf16[2,32,512]{2,1,0:T(8,128)(2,1)S(1)} %collective-permute-done.7.refs_3_), channel_id=1, source_target_pairs={{0,1},{1,0},{2,3},{3,2},{4,5},{5,4},{6,7},{7,6},{8,9},{9,8},{10,11... | collective-permute-start | bytes 196616 | tf_op jit(solution)/shard_map/ppermute | solution.py:353
  30.2 0.3 collective-permute-done.6.refs_2_
  30.5 0.1 collective-permute-start.11
  30.6 0.3 collective-permute-done.9.refs_6_
  30.9 0.2 collective-permute-done.10.refs_7_
  31.1 1.3 %scan_early.1 = (f32[32,1024]{1,0:T(8,128)S(1)}, f32[32,128]{1,0:T(8,128)S(1)}) custom-call(f8e4m3fn[16,512,1024]{2,1,0:T(32,128)(4,1)S(1)} %get-tuple-element.8.refs_0_, bf16[2,32,512]{2,1,0:T(8,128)(2,1)S(1)} %add_convert_fusion.refs_1_.refs_3_, bf16[2,32,512]{2,1,0:T(8,128)(2,1)S(1)} %collective-permute-done.6.refs_2_, ...), custom_call_target="tpu_custom_call" | custom-call | tf_op jit(solution)/shard_map/scan_early/pallas_call | solution.py:367
  32.4 1.0 %scan_late.1 = (bf16[32,512]{1,0:T(8,128)(2,1)}, f32[32,1024]{1,0:T(8,128)}) custom-call(f8e4m3fn[16,512,1024]{2,1,0:T(32,128)(4,1)S(1)} %get-tuple-element.8.refs_0_, f32[1,1024]{1,0:T(1,128)S(1)} %bitcast.4, f32[1,1024]{1,0:T(1,128)S(1)} %bitcast.6, bf16[2,32,512]{2,1,0:T(8,128)(2,1)S(1)} %add_convert_fusion.refs_1_.refs_3_, ...), custom_call_target="tpu_custom_call" | custom-call | tf_op jit(solution)/shard_map/scan_late/pallas_call | solution.py:378
  (11 shorter events, 0.1 us)
Async XLA Ops:
  0.6 31.7 %copy-start.1 = (f32[1024]{0:T(1024)S(1)}, f32[1024]{0:T(1024)}, u32[]{:S(2)}) copy-start(f32[1024]{0:T(1024)} %param.9) | copy-start | bytes 12292
  0.6 31.7 %copy-start = (f32[1024]{0:T(1024)S(1)}, f32[1024]{0:T(1024)}, u32[]{:S(2)}) copy-start(f32[1024]{0:T(1024)} %param.8) | copy-start | bytes 12292
  7.7 1.7 %collective-permute-start = (bf16[8,32,512]{2,1,0:T(8,128)(2,1)S(1)}, bf16[8,32,512]{2,1,0:T(8,128)(2,1)S(1)}, u32[]{:S(2)}, u32[]{:S(2)}) collective-permute-start(bf16[8,32,512]{2,1,0:T(8,128)(2,1)S(1)} %get-tuple-element.10), channel_id=1, source_target_pairs={{0,1},{1,0},{2,3},{3,2},{4,5},{5,4},{6,7},{7,6},{8,9},{9,8},{10,11... | collective-permute-start | bytes 786440 | tf_op jit(solution)/shard_map/ppermute | solution.py:329
  9.5 6.3 %collective-permute-start.1 = (bf16[2,32,512]{2,1,0:T(8,128)(2,1)S(1)}, bf16[2,32,512]{2,1,0:T(8,128)(2,1)S(1)}, u32[]{:S(2)}, u32[]{:S(2)}) collective-permute-start(bf16[2,32,512]{2,1,0:T(8,128)(2,1)S(1)} %get-tuple-element.14), channel_id=1, source_target_pairs={{0,3},{1,2},{2,1},{3,0},{4,7},{5,6},{6,5},{7,4},{8,11},{9,10},{10,... | collective-permute-start | bytes 196616 | tf_op jit(solution)/shard_map/ppermute | solution.py:335
  12.1 4.7 %collective-permute-start.3 = (bf16[2,32,512]{2,1,0:T(8,128)(2,1)S(1)}, bf16[2,32,512]{2,1,0:T(8,128)(2,1)S(1)}, u32[]{:S(2)}, u32[]{:S(2)}) collective-permute-start(bf16[2,32,512]{2,1,0:T(8,128)(2,1)S(1)} %get-tuple-element.15), channel_id=1, source_target_pairs={{0,7},{1,6},{2,5},{3,4},{4,3},{5,2},{6,1},{7,0},{8,15},{9,14},{10,... | collective-permute-start | bytes 196616 | tf_op jit(solution)/shard_map/ppermute | solution.py:335
  13.7 4.3 %collective-permute-start.2 = (bf16[2,32,512]{2,1,0:T(8,128)(2,1)S(1)}, bf16[2,32,512]{2,1,0:T(8,128)(2,1)S(1)}, u32[]{:S(2)}, u32[]{:S(2)}) collective-permute-start(bf16[2,32,512]{2,1,0:T(8,128)(2,1)S(1)} %get-tuple-element.16), channel_id=1, source_target_pairs={{0,4},{1,5},{2,6},{3,7},{4,0},{5,1},{6,2},{7,3},{8,12},{9,13},{10,... | collective-permute-start | bytes 196616 | tf_op jit(solution)/shard_map/ppermute | solution.py:335
  18.0 6.5 %collective-permute-start.4 = (bf16[2,32,512]{2,1,0:T(8,128)(2,1)S(1)}, bf16[2,32,512]{2,1,0:T(8,128)(2,1)S(1)}, u32[]{:S(2)}, u32[]{:S(2)}) collective-permute-start(bf16[2,32,512]{2,1,0:T(8,128)(2,1)S(1)} %add_convert_fusion.1), channel_id=1, source_target_pairs={{0,8},{1,9},{2,10},{3,11},{4,12},{5,13},{6,14},{7,15},{8,0},{9,1},... | collective-permute-start | bytes 196616 | tf_op jit(solution)/shard_map/ppermute | solution.py:344
  24.6 5.1 %collective-permute-start.8 = (bf16[2,32,512]{2,1,0:T(8,128)(2,1)S(1)}, bf16[2,32,512]{2,1,0:T(8,128)(2,1)S(1)}, u32[]{:S(2)}, u32[]{:S(2)}) collective-permute-start(bf16[2,32,512]{2,1,0:T(8,128)(2,1)S(1)} %add_convert_fusion.refs_1_.refs_3_), channel_id=1, source_target_pairs={{0,7},{1,6},{2,5},{3,4},{4,3},{5,2},{6,1},{7,0},{8,15},{9,14},{10,... | collective-permute-start | bytes 196616 | tf_op jit(solution)/shard_map/ppermute | solution.py:352
  24.6 5.0 %collective-permute-start.7 = (bf16[2,32,512]{2,1,0:T(8,128)(2,1)S(1)}, bf16[2,32,512]{2,1,0:T(8,128)(2,1)S(1)}, u32[]{:S(2)}, u32[]{:S(2)}) collective-permute-start(bf16[2,32,512]{2,1,0:T(8,128)(2,1)S(1)} %add_convert_fusion.refs_1_.refs_3_), channel_id=1, source_target_pairs={{0,4},{1,5},{2,6},{3,7},{4,0},{5,1},{6,2},{7,3},{8,12},{9,13},{10,... | collective-permute-start | bytes 196616 | tf_op jit(solution)/shard_map/ppermute | solution.py:352
  24.9 5.5 %collective-permute-start.6 = (bf16[2,32,512]{2,1,0:T(8,128)(2,1)S(1)}, bf16[2,32,512]{2,1,0:T(8,128)(2,1)S(1)}, u32[]{:S(2)}, u32[]{:S(2)}) collective-permute-start(bf16[2,32,512]{2,1,0:T(8,128)(2,1)S(1)} %add_convert_fusion.refs_1_.refs_3_), channel_id=1, source_target_pairs={{0,3},{1,2},{2,1},{3,0},{4,7},{5,6},{6,5},{7,4},{8,11},{9,10},{10,... | collective-permute-start | bytes 196616 | tf_op jit(solution)/shard_map/ppermute | solution.py:352
  27.5 3.0 %collective-permute-start.5 = (bf16[2,32,512]{2,1,0:T(8,128)(2,1)S(1)}, bf16[2,32,512]{2,1,0:T(8,128)(2,1)S(1)}, u32[]{:S(2)}, u32[]{:S(2)}) collective-permute-start(bf16[2,32,512]{2,1,0:T(8,128)(2,1)S(1)} %add_convert_fusion.refs_1_.refs_3_), channel_id=1, source_target_pairs={{0,1},{1,0},{2,3},{3,2},{4,5},{5,4},{6,7},{7,6},{8,9},{9,8},{10,11... | collective-permute-start | bytes 196616 | tf_op jit(solution)/shard_map/ppermute | solution.py:353
  29.7 1.3 %collective-permute-start.9 = (bf16[2,32,512]{2,1,0:T(8,128)(2,1)S(1)}, bf16[2,32,512]{2,1,0:T(8,128)(2,1)S(1)}, u32[]{:S(2)}, u32[]{:S(2)}) collective-permute-start(bf16[2,32,512]{2,1,0:T(8,128)(2,1)S(1)} %collective-permute-done.8.refs_4_), channel_id=1, source_target_pairs={{0,1},{1,0},{2,3},{3,2},{4,5},{5,4},{6,7},{7,6},{8,9},{9,8},{10,11... | collective-permute-start | bytes 196616 | tf_op jit(solution)/shard_map/ppermute | solution.py:353
  29.7 1.4 %collective-permute-start.10 = (bf16[2,32,512]{2,1,0:T(8,128)(2,1)S(1)}, bf16[2,32,512]{2,1,0:T(8,128)(2,1)S(1)}, u32[]{:S(2)}, u32[]{:S(2)}) collective-permute-start(bf16[2,32,512]{2,1,0:T(8,128)(2,1)S(1)} %collective-permute-done.7.refs_3_), channel_id=1, source_target_pairs={{0,1},{1,0},{2,3},{3,2},{4,5},{5,4},{6,7},{7,6},{8,9},{9,8},{10,11... | collective-permute-start | bytes 196616 | tf_op jit(solution)/shard_map/ppermute | solution.py:353
  30.5 1.9 %collective-permute-start.11 = (bf16[2,32,512]{2,1,0:T(8,128)(2,1)S(1)}, bf16[2,32,512]{2,1,0:T(8,128)(2,1)S(1)}, u32[]{:S(2)}, u32[]{:S(2)}) collective-permute-start(bf16[2,32,512]{2,1,0:T(8,128)(2,1)S(1)} %collective-permute-done.6.refs_2_), channel_id=1, source_target_pairs={{0,1},{1,0},{2,3},{3,2},{4,5},{5,4},{6,7},{7,6},{8,9},{9,8},{10,11... | collective-permute-start | bytes 196616 | tf_op jit(solution)/shard_map/ppermute | solution.py:353

commit v8 on v7

--- a/solution.py
+++ b/solution.py
@@ -351,8 +351,8 @@
     for g in (1, 2, 3):
         groups[g] = lax.ppermute(own, "var", pairs(2 * g))
     others = {g: lax.ppermute(groups[g], "var", pairs(1)) for g in range(4)}
-    first = [(0, g, groups[g]) for g in range(4)] + [(1, g, others[g]) for g in (0, 3, 2)]
-    last = [(1, 1, others[1])]
+    first = [(0, g, groups[g]) for g in (0, 2, 3)] + [(1, g, others[g]) for g in (0, 3)]
+    last = [(0, 1, groups[1]), (1, 1, others[1]), (1, 2, others[2])]
 
     def places(chosen):
         return [position(core, g, t) for core, g, _ in chosen for t in range(tails)]

time: 33.6 us -> 33.1 us (0.985)
  waiting for transfers between devices: 12.1 us -> 11.3 us
    ppermute x3, waiting for transfers between devices: 2.39 us -> 1.77 us  [on_device(): groups[g] = lax.ppermute(own, 'var', pairs(2 * g))]
  transfers between devices with their start and end apart: 12 -> 12, of which waited for: 9 -> 9; matrix products, arithmetic and copies ran while one was open for 0% -> 0% of each run, Pallas kernels for 4% -> 3%
where the time goes in v8:
time: 33.1 us; the launch traced here: 32.9 us
  starting transfers between devices  11.4 us (34%)
  waiting for transfers between devices  11.3 us (34%)
  Pallas kernels  9.34 us (28%)
  between operations  0.72 us (2%)
    pallas_call x1, Pallas kernels, on_device(): pl.pallas_call(lambda *refs: evolve_kernel(blocks, share, FLIGHT, relativ...  7.04 us
    ppermute x3, starting transfers between devices, on_device(): lax.ppermute(chip[g - 1].astype(jnp.bfloat16), 'var', pairs(2 * g))  4.23 us
    ppermute x3, waiting for transfers between devices, on_device(): lax.ppermute(chip[g - 1].astype(jnp.bfloat16), 'var', pairs(2 * g))  4.21 us
    ppermute x1, waiting for transfers between devices, on_device(): other = lax.ppermute(mine, 'var', pairs(8 * step))  3.87 us
    ppermute x3, starting transfers between devices, on_device(): groups[g] = lax.ppermute(own, 'var', pairs(2 * g))  3.27 us
    ppermute x1, starting transfers between devices, on_device(): other = lax.ppermute(mine, 'var', pairs(8 * step))  2.68 us
    ppermute x3, waiting for transfers between devices, on_device(): groups[g] = lax.ppermute(own, 'var', pairs(2 * g))  1.77 us
    pallas_call x1, Pallas kernels, on_device(): pl.pallas_call(lambda *refs: late_kernel(places(last), scale_back, lambda...  1.32 us
  transfers between devices with their start and end apart: 12, of which 9 were waited for; matrix products, arithmetic and copies ran while one was open for 0% of the time, Pallas kernels for 3%

profile of v8, /device:TPU:0, one launch (start us, length us, event | category | flops | bytes accessed | tf_op | source)
XLA Modules:
  0.0 32.9 jit_solution(14289832601708622210)
XLA Ops:
  0.7 7.0 %evolve.1 = (f8e4m3fn[16,512,1024]{2,1,0:T(32,128)(4,1)S(1)}, bf16[8,32,512]{2,1,0:T(8,128)(2,1)S(1)}, f32[8,32,512]{2,1,0:T(8,128)S(1)}, f32[2,32,512]{2,1,0:T(8,128)S(1)}) custom-call(bf16[8192,1024]{1,0:T(8,128)(2,1)} %refs_0_.1, bf16[32,8192]{1,0:T(8,128)(2,1)} %refs_1_.1, f32[1,1024]{1,0:T(1,128)} %bitcast.3, f32[1,1024]{1,0:T(1,128)} %bitcast.5, ...), custom_call_target="tpu_custom_call" | custom-call | tf_op jit(solution)/shard_map/evolve/pallas_call | solution.py:285
  7.7 0.6 %collective-permute-start = (bf16[8,32,512]{2,1,0:T(8,128)(2,1)S(1)}, bf16[8,32,512]{2,1,0:T(8,128)(2,1)S(1)}, u32[]{:S(2)}, u32[]{:S(2)}) collective-permute-start(bf16[8,32,512]{2,1,0:T(8,128)(2,1)S(1)} %get-tuple-element.10), channel_id=1, source_target_pairs={{0,1},{1,0},{2,3},{3,2},{4,5},{5,4},{6,7},{7,6},{8,9},{9,8},{10,11... | collective-permute-start | bytes 786440 | tf_op jit(solution)/shard_map/ppermute | solution.py:329
  8.3 1.2 %collective-permute-done = bf16[8,32,512]{2,1,0:T(8,128)(2,1)S(1)} collective-permute-done((bf16[8,32,512]{2,1,0:T(8,128)(2,1)S(1)}, bf16[8,32,512]{2,1,0:T(8,128)(2,1)S(1)}, u32[]{:S(2)}, u32[]{:S(2)}) %collective-permute-start) | collective-permute-done | bytes 262176 | tf_op jit(solution)/shard_map/ppermute | solution.py:329
  9.4 0.1 add_convert_fusion.4
  9.5 2.7 %collective-permute-start.1 = (bf16[2,32,512]{2,1,0:T(8,128)(2,1)S(1)}, bf16[2,32,512]{2,1,0:T(8,128)(2,1)S(1)}, u32[]{:S(2)}, u32[]{:S(2)}) collective-permute-start(bf16[2,32,512]{2,1,0:T(8,128)(2,1)S(1)} %get-tuple-element.14), channel_id=1, source_target_pairs={{0,3},{1,2},{2,1},{3,0},{4,7},{5,6},{6,5},{7,4},{8,11},{9,10},{10,... | collective-permute-start | bytes 196616 | tf_op jit(solution)/shard_map/ppermute | solution.py:335
  12.1 1.5 %collective-permute-start.3 = (bf16[2,32,512]{2,1,0:T(8,128)(2,1)S(1)}, bf16[2,32,512]{2,1,0:T(8,128)(2,1)S(1)}, u32[]{:S(2)}, u32[]{:S(2)}) collective-permute-start(bf16[2,32,512]{2,1,0:T(8,128)(2,1)S(1)} %get-tuple-element.15), channel_id=1, source_target_pairs={{0,7},{1,6},{2,5},{3,4},{4,3},{5,2},{6,1},{7,0},{8,15},{9,14},{10,... | collective-permute-start | bytes 196616 | tf_op jit(solution)/shard_map/ppermute | solution.py:335
  13.7 0.1 collective-permute-start.2
  13.7 2.0 %collective-permute-done.1 = bf16[2,32,512]{2,1,0:T(8,128)(2,1)S(1)} collective-permute-done((bf16[2,32,512]{2,1,0:T(8,128)(2,1)S(1)}, bf16[2,32,512]{2,1,0:T(8,128)(2,1)S(1)}, u32[]{:S(2)}, u32[]{:S(2)}) %collective-permute-start.1) | collective-permute-done | bytes 65568 | tf_op jit(solution)/shard_map/ppermute | solution.py:335
  15.7 1.1 %collective-permute-done.3 = bf16[2,32,512]{2,1,0:T(8,128)(2,1)S(1)} collective-permute-done((bf16[2,32,512]{2,1,0:T(8,128)(2,1)S(1)}, bf16[2,32,512]{2,1,0:T(8,128)(2,1)S(1)}, u32[]{:S(2)}, u32[]{:S(2)}) %collective-permute-start.3) | collective-permute-done | bytes 65568 | tf_op jit(solution)/shard_map/ppermute | solution.py:335
  16.9 1.1 %collective-permute-done.2 = bf16[2,32,512]{2,1,0:T(8,128)(2,1)S(1)} collective-permute-done((bf16[2,32,512]{2,1,0:T(8,128)(2,1)S(1)}, bf16[2,32,512]{2,1,0:T(8,128)(2,1)S(1)}, u32[]{:S(2)}, u32[]{:S(2)}) %collective-permute-start.2) | collective-permute-done | bytes 65568 | tf_op jit(solution)/shard_map/ppermute | solution.py:335
  18.0 2.7 %collective-permute-start.4 = (bf16[2,32,512]{2,1,0:T(8,128)(2,1)S(1)}, bf16[2,32,512]{2,1,0:T(8,128)(2,1)S(1)}, u32[]{:S(2)}, u32[]{:S(2)}) collective-permute-start(bf16[2,32,512]{2,1,0:T(8,128)(2,1)S(1)} %add_convert_fusion.1), channel_id=1, source_target_pairs={{0,8},{1,9},{2,10},{3,11},{4,12},{5,13},{6,14},{7,15},{8,0},{9,1},... | collective-permute-start | bytes 196616 | tf_op jit(solution)/shard_map/ppermute | solution.py:344
  20.6 3.9 %collective-permute-done.4 = bf16[2,32,512]{2,1,0:T(8,128)(2,1)S(1)} collective-permute-done((bf16[2,32,512]{2,1,0:T(8,128)(2,1)S(1)}, bf16[2,32,512]{2,1,0:T(8,128)(2,1)S(1)}, u32[]{:S(2)}, u32[]{:S(2)}) %collective-permute-start.4) | collective-permute-done | bytes 65568 | tf_op jit(solution)/shard_map/ppermute | solution.py:344
  24.6 0.1 collective-permute-start.7
  24.6 1.4 %collective-permute-start.9 = (bf16[2,32,512]{2,1,0:T(8,128)(2,1)S(1)}, bf16[2,32,512]{2,1,0:T(8,128)(2,1)S(1)}, u32[]{:S(2)}, u32[]{:S(2)}) collective-permute-start(bf16[2,32,512]{2,1,0:T(8,128)(2,1)S(1)} %add_convert_fusion.refs_1_.refs_3_), channel_id=1, source_target_pairs={{0,3},{1,2},{2,1},{3,0},{4,7},{5,6},{6,5},{7,4},{8,11},{9,10},{10,... | collective-permute-start | bytes 196616 | tf_op jit(solution)/shard_map/ppermute | solution.py:352
  26.0 1.8 %collective-permute-start.6 = (bf16[2,32,512]{2,1,0:T(8,128)(2,1)S(1)}, bf16[2,32,512]{2,1,0:T(8,128)(2,1)S(1)}, u32[]{:S(2)}, u32[]{:S(2)}) collective-permute-start(bf16[2,32,512]{2,1,0:T(8,128)(2,1)S(1)} %add_convert_fusion.refs_1_.refs_3_), channel_id=1, source_target_pairs={{0,4},{1,5},{2,6},{3,7},{4,0},{5,1},{6,2},{7,3},{8,12},{9,13},{10,... | collective-permute-start | bytes 196616 | tf_op jit(solution)/shard_map/ppermute | solution.py:352
  27.8 0.0 collective-permute-start.5
  27.8 1.5 %collective-permute-done.7.refs_3_ = bf16[2,32,512]{2,1,0:T(8,128)(2,1)S(1)} collective-permute-done((bf16[2,32,512]{2,1,0:T(8,128)(2,1)S(1)}, bf16[2,32,512]{2,1,0:T(8,128)(2,1)S(1)}, u32[]{:S(2)}, u32[]{:S(2)}) %collective-permute-start.7) | collective-permute-done | bytes 65568 | tf_op jit(solution)/shard_map/ppermute | solution.py:352
  29.3 0.2 collective-permute-done.9.refs_7_
  29.6 0.7 %collective-permute-start.10 = (bf16[2,32,512]{2,1,0:T(8,128)(2,1)S(1)}, bf16[2,32,512]{2,1,0:T(8,128)(2,1)S(1)}, u32[]{:S(2)}, u32[]{:S(2)}) collective-permute-start(bf16[2,32,512]{2,1,0:T(8,128)(2,1)S(1)} %collective-permute-done.9.refs_7_), channel_id=1, source_target_pairs={{0,1},{1,0},{2,3},{3,2},{4,5},{5,4},{6,7},{7,6},{8,9},{9,8},{10,11... | collective-permute-start | bytes 196616 | tf_op jit(solution)/shard_map/ppermute | solution.py:353
  30.2 0.1 collective-permute-done.6.refs_2_
  30.3 0.0 collective-permute-start.11
  30.3 0.3 collective-permute-done.8.refs_5_
  30.6 1.0 %scan_early.1 = (f32[32,1024]{1,0:T(8,128)S(1)}, f32[32,128]{1,0:T(8,128)S(1)}) custom-call(f8e4m3fn[16,512,1024]{2,1,0:T(32,128)(4,1)S(1)} %get-tuple-element.8.refs_0_, bf16[2,32,512]{2,1,0:T(8,128)(2,1)S(1)} %add_convert_fusion.refs_1_.refs_3_, bf16[2,32,512]{2,1,0:T(8,128)(2,1)S(1)} %collective-permute-done.6.refs_2_, ...), custom_call_target="tpu_custom_call" | custom-call | tf_op jit(solution)/shard_map/scan_early/pallas_call | solution.py:367
  31.6 1.3 %scan_late.1 = (bf16[32,512]{1,0:T(8,128)(2,1)}, f32[32,1024]{1,0:T(8,128)}) custom-call(f8e4m3fn[16,512,1024]{2,1,0:T(32,128)(4,1)S(1)} %get-tuple-element.8.refs_0_, f32[1,1024]{1,0:T(1,128)S(1)} %bitcast.4, f32[1,1024]{1,0:T(1,128)S(1)} %bitcast.6, bf16[2,32,512]{2,1,0:T(8,128)(2,1)S(1)} %add_convert_fusion.refs_1_.refs_3_, ...), custom_call_target="tpu_custom_call" | custom-call | tf_op jit(solution)/shard_map/scan_late/pallas_call | solution.py:378
  (11 shorter events, 0.1 us)
Async XLA Ops:
  0.6 30.9 %copy-start.1 = (f32[1024]{0:T(1024)S(1)}, f32[1024]{0:T(1024)}, u32[]{:S(2)}) copy-start(f32[1024]{0:T(1024)} %param.9) | copy-start | bytes 12292
  0.6 30.9 %copy-start = (f32[1024]{0:T(1024)S(1)}, f32[1024]{0:T(1024)}, u32[]{:S(2)}) copy-start(f32[1024]{0:T(1024)} %param.8) | copy-start | bytes 12292
  7.7 1.7 %collective-permute-start = (bf16[8,32,512]{2,1,0:T(8,128)(2,1)S(1)}, bf16[8,32,512]{2,1,0:T(8,128)(2,1)S(1)}, u32[]{:S(2)}, u32[]{:S(2)}) collective-permute-start(bf16[8,32,512]{2,1,0:T(8,128)(2,1)S(1)} %get-tuple-element.10), channel_id=1, source_target_pairs={{0,1},{1,0},{2,3},{3,2},{4,5},{5,4},{6,7},{7,6},{8,9},{9,8},{10,11... | collective-permute-start | bytes 786440 | tf_op jit(solution)/shard_map/ppermute | solution.py:329
  9.5 6.3 %collective-permute-start.1 = (bf16[2,32,512]{2,1,0:T(8,128)(2,1)S(1)}, bf16[2,32,512]{2,1,0:T(8,128)(2,1)S(1)}, u32[]{:S(2)}, u32[]{:S(2)}) collective-permute-start(bf16[2,32,512]{2,1,0:T(8,128)(2,1)S(1)} %get-tuple-element.14), channel_id=1, source_target_pairs={{0,3},{1,2},{2,1},{3,0},{4,7},{5,6},{6,5},{7,4},{8,11},{9,10},{10,... | collective-permute-start | bytes 196616 | tf_op jit(solution)/shard_map/ppermute | solution.py:335
  12.1 4.7 %collective-permute-start.3 = (bf16[2,32,512]{2,1,0:T(8,128)(2,1)S(1)}, bf16[2,32,512]{2,1,0:T(8,128)(2,1)S(1)}, u32[]{:S(2)}, u32[]{:S(2)}) collective-permute-start(bf16[2,32,512]{2,1,0:T(8,128)(2,1)S(1)} %get-tuple-element.15), channel_id=1, source_target_pairs={{0,7},{1,6},{2,5},{3,4},{4,3},{5,2},{6,1},{7,0},{8,15},{9,14},{10,... | collective-permute-start | bytes 196616 | tf_op jit(solution)/shard_map/ppermute | solution.py:335
  13.7 4.3 %collective-permute-start.2 = (bf16[2,32,512]{2,1,0:T(8,128)(2,1)S(1)}, bf16[2,32,512]{2,1,0:T(8,128)(2,1)S(1)}, u32[]{:S(2)}, u32[]{:S(2)}) collective-permute-start(bf16[2,32,512]{2,1,0:T(8,128)(2,1)S(1)} %get-tuple-element.16), channel_id=1, source_target_pairs={{0,4},{1,5},{2,6},{3,7},{4,0},{5,1},{6,2},{7,3},{8,12},{9,13},{10,... | collective-permute-start | bytes 196616 | tf_op jit(solution)/shard_map/ppermute | solution.py:335
  18.0 6.5 %collective-permute-start.4 = (bf16[2,32,512]{2,1,0:T(8,128)(2,1)S(1)}, bf16[2,32,512]{2,1,0:T(8,128)(2,1)S(1)}, u32[]{:S(2)}, u32[]{:S(2)}) collective-permute-start(bf16[2,32,512]{2,1,0:T(8,128)(2,1)S(1)} %add_convert_fusion.1), channel_id=1, source_target_pairs={{0,8},{1,9},{2,10},{3,11},{4,12},{5,13},{6,14},{7,15},{8,0},{9,1},... | collective-permute-start | bytes 196616 | tf_op jit(solution)/shard_map/ppermute | solution.py:344
  24.6 4.8 %collective-permute-start.7 = (bf16[2,32,512]{2,1,0:T(8,128)(2,1)S(1)}, bf16[2,32,512]{2,1,0:T(8,128)(2,1)S(1)}, u32[]{:S(2)}, u32[]{:S(2)}) collective-permute-start(bf16[2,32,512]{2,1,0:T(8,128)(2,1)S(1)} %add_convert_fusion.refs_1_.refs_3_), channel_id=1, source_target_pairs={{0,7},{1,6},{2,5},{3,4},{4,3},{5,2},{6,1},{7,0},{8,15},{9,14},{10,... | collective-permute-start | bytes 196616 | tf_op jit(solution)/shard_map/ppermute | solution.py:352
  24.6 4.9 %collective-permute-start.9 = (bf16[2,32,512]{2,1,0:T(8,128)(2,1)S(1)}, bf16[2,32,512]{2,1,0:T(8,128)(2,1)S(1)}, u32[]{:S(2)}, u32[]{:S(2)}) collective-permute-start(bf16[2,32,512]{2,1,0:T(8,128)(2,1)S(1)} %add_convert_fusion.refs_1_.refs_3_), channel_id=1, source_target_pairs={{0,3},{1,2},{2,1},{3,0},{4,7},{5,6},{6,5},{7,4},{8,11},{9,10},{10,... | collective-permute-start | bytes 196616 | tf_op jit(solution)/shard_map/ppermute | solution.py:352
  26.0 4.3 %collective-permute-start.6 = (bf16[2,32,512]{2,1,0:T(8,128)(2,1)S(1)}, bf16[2,32,512]{2,1,0:T(8,128)(2,1)S(1)}, u32[]{:S(2)}, u32[]{:S(2)}) collective-permute-start(bf16[2,32,512]{2,1,0:T(8,128)(2,1)S(1)} %add_convert_fusion.refs_1_.refs_3_), channel_id=1, source_target_pairs={{0,4},{1,5},{2,6},{3,7},{4,0},{5,1},{6,2},{7,3},{8,12},{9,13},{10,... | collective-permute-start | bytes 196616 | tf_op jit(solution)/shard_map/ppermute | solution.py:352
  27.8 2.5 %collective-permute-start.5 = (bf16[2,32,512]{2,1,0:T(8,128)(2,1)S(1)}, bf16[2,32,512]{2,1,0:T(8,128)(2,1)S(1)}, u32[]{:S(2)}, u32[]{:S(2)}) collective-permute-start(bf16[2,32,512]{2,1,0:T(8,128)(2,1)S(1)} %add_convert_fusion.refs_1_.refs_3_), channel_id=1, source_target_pairs={{0,1},{1,0},{2,3},{3,2},{4,5},{5,4},{6,7},{7,6},{8,9},{9,8},{10,11... | collective-permute-start | bytes 196616 | tf_op jit(solution)/shard_map/ppermute | solution.py:353
  29.3 1.3 %collective-permute-start.8 = (bf16[2,32,512]{2,1,0:T(8,128)(2,1)S(1)}, bf16[2,32,512]{2,1,0:T(8,128)(2,1)S(1)}, u32[]{:S(2)}, u32[]{:S(2)}) collective-permute-start(bf16[2,32,512]{2,1,0:T(8,128)(2,1)S(1)} %collective-permute-done.7.refs_3_), channel_id=1, source_target_pairs={{0,1},{1,0},{2,3},{3,2},{4,5},{5,4},{6,7},{7,6},{8,9},{9,8},{10,11... | collective-permute-start | bytes 196616 | tf_op jit(solution)/shard_map/ppermute | solution.py:353
  29.6 2.0 %collective-permute-start.10 = (bf16[2,32,512]{2,1,0:T(8,128)(2,1)S(1)}, bf16[2,32,512]{2,1,0:T(8,128)(2,1)S(1)}, u32[]{:S(2)}, u32[]{:S(2)}) collective-permute-start(bf16[2,32,512]{2,1,0:T(8,128)(2,1)S(1)} %collective-permute-done.9.refs_7_), channel_id=1, source_target_pairs={{0,1},{1,0},{2,3},{3,2},{4,5},{5,4},{6,7},{7,6},{8,9},{9,8},{10,11... | collective-permute-start | bytes 196616 | tf_op jit(solution)/shard_map/ppermute | solution.py:353
  30.3 1.3 %collective-permute-start.11 = (bf16[2,32,512]{2,1,0:T(8,128)(2,1)S(1)}, bf16[2,32,512]{2,1,0:T(8,128)(2,1)S(1)}, u32[]{:S(2)}, u32[]{:S(2)}) collective-permute-start(bf16[2,32,512]{2,1,0:T(8,128)(2,1)S(1)} %collective-permute-done.6.refs_2_), channel_id=1, source_target_pairs={{0,1},{1,0},{2,3},{3,2},{4,5},{5,4},{6,7},{7,6},{8,9},{9,8},{10,11... | collective-permute-start | bytes 196616 | tf_op jit(solution)/shard_map/ppermute | solution.py:353
